TPU v7x, 32 devices: a whole 2x2x4 slice. The times are simulated.
32 devices in a mesh: ctx: 8 (over z, y), head: 4 (over x, core).
Axes of the slice: x: 2, y: 2, z: 4, core: 2. Of those that a mesh axis runs over, the one named last changes fastest.
Arguments:
- query: bfloat16 [1024, 8192], P('ctx', 'head'), may hold values from -240 to 240
- keys: bfloat16 [1024, 8192], P('ctx', 'head'), may hold values from -4 to 4
- values: bfloat16 [1024, 8192], P('ctx', 'head'), may hold values from -6 to 6
- memory_keys: bfloat16 [768, 8192], P('ctx', 'head'), may hold values from -6 to 6
- memory_values: bfloat16 [768, 8192], P('ctx', 'head'), may hold values from -6 to 6
- routes: int32 [96, 1], replicated, may hold values from 0 to 7; in each aligned block of 12 rows (0 to 11, 12 to 23, ...) at most 2 rows name the same one
- documents: int32 [1024], replicated, may hold values from 0 to 15, never falling along the last dimension, each value on 1 to 257 neighbouring positions
- cotangent: bfloat16 [1024, 8192], P('ctx', 'head'), may hold values from -40 to 40
Outputs:
- attended: bfloat16 [1024, 8192], P('ctx', 'head')
- query_grad: bfloat16 [1024, 8192], P('ctx', 'head')
- key_grad: bfloat16 [1024, 8192], P('ctx', 'head')
- value_grad: bfloat16 [1024, 8192], P('ctx', 'head')
Inputs may be any that keep to these rules, and one draw needn't show every extreme that they name: `routes`: in the 12 aligned rows of one segment block's store, no segment block is named more than 2 times. `documents`: document numbers never fall; a document covers 1 to 257 positions.
All inputs are finite; a program needn't handle non-finite values.
Results may differ from a plain program's by a relative error of at most 0.01.
Values may be sent and summed in bfloat16 or wider, within the bound.
No kernel may reach another device: no remote copies, remote signals or barrier semaphores. Data moves between devices by JAX's collectives and lax.ppermute only.
A program may use at most 64 MiB of HBM per device.

v0:
```python
import math

import jax
import jax.numpy as jnp
from jax import lax
from jax.sharding import PartitionSpec as P

HDIM = 128
BLK = 8
CAP = 2
REACH = 3


NEGATIVE = -1e30


def shifted(value, axis, steps):
    count = lax.axis_size(axis)
    initial, last = (max(0, -steps), min(count, count - steps))
    return lax.ppermute(value, axis, [(source, source + steps) for source in range(initial, last)])


def absorb(state, query_heads, block_keys, block_values, mask, scaling):
    running_max, running_sum, running_acc = state
    scores = (
        jnp.einsum("qhd,khd->hqk", query_heads, block_keys, preferred_element_type=jnp.float32)
        * scaling
    )
    visible = mask[None, :, :]
    block_max = jnp.max(jnp.where(visible, scores, NEGATIVE), axis=-1)
    new_max = jnp.maximum(running_max, block_max)
    weights = jnp.where(visible, jnp.exp(scores - new_max[..., None]), 0.0)
    shrink = jnp.exp(running_max - new_max)
    new_sum = running_sum * shrink + jnp.sum(weights, axis=-1)
    new_acc = running_acc * shrink[..., None] + jnp.einsum(
        "hqk,khd->hqd",
        weights.astype(jnp.bfloat16),
        block_values,
        preferred_element_type=jnp.float32,
    )
    return (new_max, new_sum, new_acc)


def block_grads(
    query_heads, upstream, log_total, delta, block_keys, block_values, mask, scaling, with_keys
):
    scores = (
        jnp.einsum("qhd,khd->hqk", query_heads, block_keys, preferred_element_type=jnp.float32)
        * scaling
    )
    probs = jnp.where(mask[None, :, :], jnp.exp(scores - log_total[..., None]), 0.0)
    pressure = jnp.einsum(
        "qhd,khd->hqk", upstream, block_values, preferred_element_type=jnp.float32
    )
    score_grad = (probs * (pressure - delta[..., None])).astype(jnp.bfloat16)
    query_part = (
        jnp.einsum("hqk,khd->qhd", score_grad, block_keys, preferred_element_type=jnp.float32)
        * scaling
    )
    if not with_keys:
        return query_part
    key_part = (
        jnp.einsum("hqk,qhd->khd", score_grad, query_heads, preferred_element_type=jnp.float32)
        * scaling
    )
    value_part = jnp.einsum(
        "hqk,qhd->khd", probs.astype(jnp.bfloat16), upstream, preferred_element_type=jnp.float32
    )
    return (query_part, key_part, value_part)


def on_device(query, keys, values, memory_keys, memory_values, routes, documents, cotangent):
    row_count, width = query.shape
    heads = width // HDIM
    scaling = 1.0 / math.sqrt(HDIM)
    cycle_size = lax.axis_size("ctx")
    position = lax.axis_index("ctx")
    query_heads = query.reshape(row_count, heads, HDIM)
    upstream = cotangent.reshape(row_count, heads, HDIM)
    query_docs = lax.dynamic_slice_in_dim(documents, position * row_count, row_count)
    query_pos = position * row_count + jnp.arange(row_count, dtype=jnp.int32)
    own_mask = (query_pos[None, :] <= query_pos[:, None]) & (
        query_docs[None, :] == query_docs[:, None]
    )
    per_device = memory_keys.shape[0] // BLK
    route_table = routes[:, 0].reshape(cycle_size, per_device)
    my_routes = lax.dynamic_slice_in_dim(route_table, position, 1, 0)[0]
    ordering = jnp.arange(per_device, dtype=jnp.int32)
    ranking = jnp.sum(
        (my_routes[None, :] == my_routes[:, None]) & (ordering[None, :] < ordering[:, None]), axis=1
    )
    owners = jnp.arange(cycle_size, dtype=jnp.int32)
    slot_ids = jnp.arange(CAP, dtype=jnp.int32)
    selector = (
        (my_routes[None, None, :] == owners[:, None, None])
        & (ranking[None, None, :] == slot_ids[None, :, None])
    ).astype(jnp.bfloat16)

    def pack(array):
        flat = array.reshape(per_device, BLK * width)
        placed = jnp.einsum("dcb,bx->dcx", selector, flat, preferred_element_type=jnp.float32)
        return placed.astype(jnp.bfloat16).reshape(cycle_size, CAP * BLK, width)

    arrived_keys, arrived_values = (
        lax.all_to_all(pack(memory_keys), "ctx", split_axis=0, concat_axis=0, tiled=True),
        lax.all_to_all(pack(memory_values), "ctx", split_axis=0, concat_axis=0, tiled=True),
    )
    memory_count = cycle_size * CAP * BLK
    arrivals = jnp.sum((route_table == position).astype(jnp.int32), axis=1)
    slot_live = slot_ids[None, :] < arrivals[:, None]
    memory_live = jnp.broadcast_to(slot_live[:, :, None], (cycle_size, CAP, BLK)).reshape(
        memory_count
    )
    memory_mask = jnp.broadcast_to(memory_live[None, :], (row_count, memory_count))
    memory_key_heads = arrived_keys.reshape(memory_count, heads, HDIM)
    memory_value_heads = arrived_values.reshape(memory_count, heads, HDIM)
    state = (
        jnp.full((heads, row_count), NEGATIVE, jnp.float32),
        jnp.zeros((heads, row_count), jnp.float32),
        jnp.zeros((heads, row_count, HDIM), jnp.float32),
    )
    state = absorb(state, query_heads, memory_key_heads, memory_value_heads, memory_mask, scaling)
    own_keys = keys.reshape(row_count, heads, HDIM)
    own_values = values.reshape(row_count, heads, HDIM)
    state = absorb(state, query_heads, own_keys, own_values, own_mask, scaling)

    def keep(carried):
        return carried

    seen = []
    moving_keys, moving_values = (keys, values)
    for step in range(1, REACH):
        moving_keys, moving_values = shifted((moving_keys, moving_values), "ctx", 1)
        source = (position - step) % cycle_size
        key_docs = lax.dynamic_slice_in_dim(documents, source * row_count, row_count)
        block_mask = (key_docs[None, :] == query_docs[:, None]) & (source < position)
        block_keys = moving_keys.reshape(row_count, heads, HDIM)
        block_values = moving_values.reshape(row_count, heads, HDIM)

        def take_block(carried):
            return absorb(carried, query_heads, block_keys, block_values, block_mask, scaling)

        state = lax.cond(jnp.any(block_mask), take_block, keep, state)
        seen.append((block_keys, block_values, block_mask))
    running_max, running_sum, running_acc = state
    output = running_acc / running_sum[..., None]
    attended = jnp.transpose(output, (1, 0, 2)).reshape(row_count, width).astype(jnp.bfloat16)
    log_total = running_max + jnp.log(running_sum)
    delta = jnp.einsum("hqd,qhd->hq", output, upstream.astype(jnp.float32))
    query_total = block_grads(
        query_heads,
        upstream,
        log_total,
        delta,
        memory_key_heads,
        memory_value_heads,
        memory_mask,
        scaling,
        False,
    )
    own_query, own_key, own_value = block_grads(
        query_heads, upstream, log_total, delta, own_keys, own_values, own_mask, scaling, True
    )
    query_total = query_total + own_query
    own_key = own_key.reshape(row_count, width)
    own_value = own_value.reshape(row_count, width)
    pieces = []
    for step in range(1, REACH):
        block_keys, block_values, block_mask = seen[step - 1]

        def make_terms(carried):
            query_part, key_part, value_part = block_grads(
                query_heads,
                upstream,
                log_total,
                delta,
                block_keys,
                block_values,
                block_mask,
                scaling,
                True,
            )
            return (
                query_part,
                key_part.reshape(row_count, width),
                value_part.reshape(row_count, width),
            )

        def no_terms(carried):
            return (jnp.zeros_like(query_total), jnp.zeros_like(own_key), jnp.zeros_like(own_value))

        query_part, key_part, value_part = lax.cond(jnp.any(block_mask), make_terms, no_terms, 0)
        query_total = query_total + query_part
        pieces.append((key_part, value_part))
    key_moving = jnp.zeros_like(own_key)
    value_moving = jnp.zeros_like(own_value)
    for step in range(REACH - 1, 0, -1):
        key_moving = key_moving + pieces[step - 1][0]
        value_moving = value_moving + pieces[step - 1][1]
        key_moving, value_moving = (
            shifted(key_moving.astype(jnp.bfloat16), "ctx", -1).astype(key_moving.dtype),
            shifted(value_moving.astype(jnp.bfloat16), "ctx", -1).astype(value_moving.dtype),
        )
    key_total = key_moving + own_key
    value_total = value_moving + own_value
    query_flat = query_total.reshape(row_count, width)
    local_squares = (
        jnp.sum(query_flat * query_flat)
        + jnp.sum(key_total * key_total)
        + jnp.sum(value_total * value_total)
    )
    all_squares = lax.psum(local_squares, ("ctx", "head"))
    entries = 3.0 * cycle_size * row_count * width * lax.axis_size("head")
    spread = jnp.sqrt(all_squares / entries + 1e-06)
    return (
        attended,
        (query_flat / spread).astype(jnp.bfloat16),
        (key_total / spread).astype(jnp.bfloat16),
        (value_total / spread).astype(jnp.bfloat16),
    )


def solution(mesh):
    placed = (
        P("ctx", "head"),
        P("ctx", "head"),
        P("ctx", "head"),
        P("ctx", "head"),
        P("ctx", "head"),
        P(),
        P(),
        P("ctx", "head"),
    )
    return jax.shard_map(
        on_device,
        mesh=mesh,
        in_specs=placed,
        out_specs=(P("ctx", "head"), P("ctx", "head"), P("ctx", "head"), P("ctx", "head")),
        check_vma=False,
    )
```

profile of v0, /device:TPU:0, one launch (start us, length us, event | category | flops | bytes accessed | tf_op | source)
XLA Modules:
  0.0 216.7 jit_solution(11295030608780293349)
XLA Ops:
  0.6 0.5 broadcast.209
  1.3 0.7 reduce.7
  2.2 1.3 reshape.261
  3.9 0.5 copy.106
  4.4 1.2 reshape.246
  5.6 7.4 %all-to-all-start = ((bf16[8,16,2048]{2,1,0:T(8,128)(2,1)}), bf16[8,16,2048]{2,1,0:T(8,128)(2,1)S(1)}, u32[]{:S(2)}, u32[]{:S(2)}) async-start(bf16[8,16,2048]{2,1,0:T(8,128)(2,1)} %reshape.246), calls=%async_computation | async-start | bytes 1048576 | tf_op jit(solution)/shard_map/all_to_all | solution.py:105
  13.3 4.8 %collective-permute-start = (bf16[128,2048]{0,1:T(8,128)(2,1)S(1)}, bf16[128,2048]{0,1:T(8,128)(2,1)}, u32[]{:S(2)}, u32[]{:S(2)}) collective-permute-start(bf16[128,2048]{0,1:T(8,128)(2,1)S(1)} %copy.181), channel_id=1, source_target_pairs={{0,4},{4,8},{8,12},{12,16},{16,20},{20,24},{24,28},{1,5},{5,9},{9,... | collective-permute-start | bytes 1572872 | tf_op jit(solution)/shard_map/ppermute | solution.py:20
  18.2 1.0 copy.118
  19.2 3.4 %collective-permute-start.1 = (bf16[128,2048]{0,1:T(8,128)(2,1)}, bf16[128,2048]{0,1:T(8,128)(2,1)}, u32[]{:S(2)}, u32[]{:S(2)}) collective-permute-start(bf16[128,2048]{0,1:T(8,128)(2,1)} %copy.118), channel_id=1, source_target_pairs={{0,4},{4,8},{8,12},{12,16},{16,20},{20,24},{24,28},{1,5},{5,9},{9,... | collective-permute-start | bytes 1572872 | tf_op jit(solution)/shard_map/ppermute | solution.py:20
  22.6 0.3 reshape.262
  22.9 0.3 convolution_convert_fusion
  23.2 0.5 copy.113
  23.7 1.2 reshape.251
  24.9 2.6 %all-to-all-done = bf16[8,16,2048]{2,1,0:T(8,128)(2,1)S(1)} async-done(((bf16[8,16,2048]{2,1,0:T(8,128)(2,1)}), bf16[8,16,2048]{2,1,0:T(8,128)(2,1)S(1)}, u32[]{:S(2)}, u32[]{:S(2)}) %all-to-all-start) | async-done | bytes 524320 | tf_op jit(solution)/shard_map/all_to_all | solution.py:105
  27.5 4.1 %all-to-all-start.1 = ((bf16[8,16,2048]{2,1,0:T(8,128)(2,1)}), bf16[8,16,2048]{2,1,0:T(8,128)(2,1)}, u32[]{:S(2)}, u32[]{:S(2)}) async-start(bf16[8,16,2048]{2,1,0:T(8,128)(2,1)} %reshape.251), calls=%async_computation.1 | async-start | bytes 1048576 | tf_op jit(solution)/shard_map/all_to_all | solution.py:106
  31.8 0.9 fusion.84
  33.2 0.7 fusion.83
  35.5 0.6 select_reduce_fusion.2
  36.1 4.6 %collective-permute-start.2 = (bf16[128,2048]{0,1:T(8,128)(2,1)}, bf16[128,2048]{0,1:T(8,128)(2,1)}, u32[]{:S(2)}, u32[]{:S(2)}) collective-permute-start(bf16[128,2048]{0,1:T(8,128)(2,1)} %collective-permute-done), channel_id=1, source_target_pairs={{0,4},{4,8},{8,12},{12,16},{16,20},{20,24},{24,28},{1,5},{5,9},{9,... | collective-permute-start | bytes 1572872 | tf_op jit(solution)/shard_map/ppermute | solution.py:20
  40.7 6.1 %collective-permute-done.1 = bf16[128,2048]{0,1:T(8,128)(2,1)} collective-permute-done((bf16[128,2048]{0,1:T(8,128)(2,1)}, bf16[128,2048]{0,1:T(8,128)(2,1)}, u32[]{:S(2)}, u32[]{:S(2)}) %collective-permute-start.1) | collective-permute-done | bytes 524320 | tf_op jit(solution)/shard_map/ppermute | solution.py:20
  46.8 6.9 %collective-permute-start.3 = (bf16[128,2048]{0,1:T(8,128)(2,1)}, bf16[128,2048]{0,1:T(8,128)(2,1)}, u32[]{:S(2)}, u32[]{:S(2)}) collective-permute-start(bf16[128,2048]{0,1:T(8,128)(2,1)} %collective-permute-done.1), channel_id=1, source_target_pairs={{0,4},{4,8},{8,12},{12,16},{16,20},{20,24},{24,28},{1,5},{5,9},{9,... | collective-permute-start | bytes 1572872 | tf_op jit(solution)/shard_map/ppermute | solution.py:20
  53.7 0.9 copy.184
  54.6 1.5 copy.131
  56.1 1.3 copy.185
  57.4 0.4 select_reduce_fusion.3
  58.1 0.7 fusion.45
  58.8 0.9 fusion.38
  59.8 0.5 convolution_add_fusion.2
  60.4 9.8 %collective-permute-done.3 = bf16[128,2048]{0,1:T(8,128)(2,1)} collective-permute-done((bf16[128,2048]{0,1:T(8,128)(2,1)}, bf16[128,2048]{0,1:T(8,128)(2,1)}, u32[]{:S(2)}, u32[]{:S(2)}) %collective-permute-start.3) | collective-permute-done | bytes 524320 | tf_op jit(solution)/shard_map/ppermute | solution.py:20
  70.2 1.5 convert_bitcast_fusion
  71.7 1.6 copy.175
  73.4 0.9 copy-done.14
  74.3 1.7 fusion.40
  76.0 2.9 %fusion.36 = f32[128,16,128]{2,0,1:T(8,128)} fusion(bf16[128,16,128]{0,2,1:T(8,128)(2,1)} %copy-done.5, bf16[128,16,128]{0,2,1:T(8,128)(2,1)S(1)} %bitcast.127, f32[16,128,128]{2,1,0:T(8,128)S(1)} %copy-done.1, f32[16,128]{1,0:T(8,128)S(1)} %multiply_reduce_fusion, f32[16,128]{1,0:T(8,128)S(1)} %log_add_fusion, ...), kind=kOutput, calls=%fused_computation.60 | convolution fusion | flops 135790592 | bytes 3686528 | tf_op jit(solution)/shard_map/hqk,khd->qhd/dot_general | solution.py:57
  78.9 2.7 %conditional.7 = (f32[128,16,128]{2,0,1:T(8,128)}, bf16[128,2048]{0,1:T(8,128)(2,1)}, bf16[128,2048]{0,1:T(8,128)(2,1)}) conditional(s32[]{:T(128)} %convert_element_type.104, () %tuple.52, (pred[128,128]{1,0:T(8,128)(4,1)S(1)}, bf16[128,16,128]{0,2,1:T(8,128)(2,1)S(1)}, bf16[128,16,128]{0,2,1:T(8,128)(2,1)}, f32[16,128]{1,0:T(8,128)S(1)}, ...), branch_computations={%region_18.19_spmd, %region_19.20_spmd} | conditional | flops 338165760 | bytes 13664308 | solution.py:192
  78.9 1.1 broadcast.188
  80.0 0.8 broadcast.189
  80.8 0.8 broadcast.189.clone
  81.6 1.3 collective-permute-start.6
  82.9 1.4 collective-permute-start.4
  84.4 0.6 fusion.47
  84.9 1.5 fusion.32
  86.5 1.6 copy.143
  88.0 3.3 %conditional.6 = (f32[128,16,128]{2,0,1:T(8,128)}, f32[128,2048]{0,1:T(8,128)}, f32[128,2048]{0,1:T(8,128)}) conditional(s32[]{:T(128)} %convert_element_type.105, () %tuple.50, (pred[128,128]{1,0:T(8,128)(4,1)S(1)}, bf16[128,16,128]{0,2,1:T(8,128)(2,1)S(1)}, bf16[128,16,128]{0,2,1:T(8,128)(2,1)}, f32[16,128]{1,0:T(8,128)S(1)}, ...), branch_computations={%region_16.17_spmd, %region_17.18_spmd} | conditional | flops 337903616 | bytes 26247304 | solution.py:192
  88.1 1.1 broadcast.185
  89.2 1.1 broadcast.186
  90.2 1.1 broadcast.186.clone
  91.3 24.8 %collective-permute-done.4 = bf16[128,2048]{0,1:T(8,128)(2,1)} collective-permute-done((bf16[128,2048]{0,1:T(8,128)(2,1)}, bf16[128,2048]{0,1:T(8,128)(2,1)}, u32[]{:S(2)}, u32[]{:S(2)}) %collective-permute-start.4) | collective-permute-done | bytes 524320 | tf_op jit(solution)/shard_map/ppermute | solution.py:20
  116.1 1.5 add_convert_fusion.1
  117.6 1.3 collective-permute-start.5
  118.9 2.4 %add_convert_fusion = bf16[128,2048]{0,1:T(8,128)(2,1)} fusion(f32[128,2048]{0,1:T(8,128)} %get-tuple-element.137, bf16[128,2048]{0,1:T(8,128)(2,1)} %collective-permute-done.6), kind=kLoop, calls=%fused_computation.79 | loop fusion | flops 786432 | bytes 2097152 | tf_op jit(solution)/shard_map/convert_element_type | solution.py:202
  121.3 1.3 collective-permute-start.7
  122.6 2.7 %multiply_reduce_fusion.3 = (f32[]{:T(128)}, f32[128,16,128]{2,0,1:T(8,128)S(1)}) fusion(f32[128,16,128]{2,0,1:T(8,128)} %get-tuple-element.133, f32[128,16,128]{2,0,1:T(8,128)} %get-tuple-element.132, f32[128,16,128]{2,0,1:T(8,128)S(1)} %copy-done.11, bf16[16,128,128]{2,1,0:T(8,128)(2,1)S(1)} %copy-done.18, bf16[128,16,128]{0,2,1:T(8,128)(2,1)S(1)} %bitcast.134), kind=kOutput, calls=%fused_computation.82 | convolution fusion | flops 68681728 | bytes 5242884 | tf_op jit(solution)/shard_map/hqk,khd->qhd/dot_general | solution.py:57
  125.3 10.4 %collective-permute-done.5 = bf16[128,2048]{0,1:T(8,128)(2,1)S(1)} collective-permute-done((bf16[128,2048]{0,1:T(8,128)(2,1)S(1)}, bf16[128,2048]{0,1:T(8,128)(2,1)S(1)}, u32[]{:S(2)}, u32[]{:S(2)}) %collective-permute-start.5) | collective-permute-done | bytes 524320 | tf_op jit(solution)/shard_map/ppermute | solution.py:20
  135.7 0.8 multiply_reduce_fusion.2
  137.7 6.5 %collective-permute-done.7 = bf16[128,2048]{0,1:T(8,128)(2,1)} collective-permute-done((bf16[128,2048]{0,1:T(8,128)(2,1)}, bf16[128,2048]{0,1:T(8,128)(2,1)}, u32[]{:S(2)}, u32[]{:S(2)}) %collective-permute-start.7) | collective-permute-done | bytes 524320 | tf_op jit(solution)/shard_map/ppermute | solution.py:20
  144.3 2.0 multiply_reduce_fusion.1
  147.0 2.0 copy.200
  148.9 58.6 %psum.7 = f32[]{:T(128)} all-reduce(f32[]{:T(128)S(6)} %add.115), channel_id=1, replica_groups=mesh['ctx'=8,'head'=4] {'ctx','head'}, use_global_device_ids=true, to_apply=%region_23.24 | all-reduce | flops 1 | bytes 8 | tf_op jit(solution)/shard_map/psum | solution.py:212
  208.3 2.1 divide_convert_fusion
  210.4 2.1 copy.147
  212.6 1.0 copy.146
  213.6 1.7 divide_convert_fusion.2
  215.7 1.0 copy.145
  (63 shorter events, 2.9 us)
Async XLA Ops:
  0.6 0.7 copy-start.23
  5.6 7.4 %copy-start.19 = (bf16[128,2048]{1,0:T(8,128)(2,1)S(1)}, bf16[128,2048]{1,0:T(8,128)(2,1)}, u32[]{:S(2)}) copy-start(bf16[128,2048]{1,0:T(8,128)(2,1)} %param.17) | copy-start | bytes 1572868
  5.6 21.9 %all-to-all-start = ((bf16[8,16,2048]{2,1,0:T(8,128)(2,1)}), bf16[8,16,2048]{2,1,0:T(8,128)(2,1)S(1)}, u32[]{:S(2)}, u32[]{:S(2)}) async-start(bf16[8,16,2048]{2,1,0:T(8,128)(2,1)} %reshape.246), calls=%async_computation | async-start | bytes 1048576 | tf_op jit(solution)/shard_map/all_to_all | solution.py:105
  13.0 5.2 %copy-start.12 = (bf16[128,2048]{1,0:T(8,128)(2,1)S(1)}, bf16[128,2048]{1,0:T(8,128)(2,1)}, u32[]{:S(2)}) copy-start(bf16[128,2048]{1,0:T(8,128)(2,1)} %param.18) | copy-start | bytes 1572868
  13.3 22.2 %copy-start.9 = (bf16[128,2048]{0,1:T(8,128)(2,1)}, bf16[128,2048]{0,1:T(8,128)(2,1)S(1)}, u32[]{:S(2)}) copy-start(bf16[128,2048]{0,1:T(8,128)(2,1)S(1)} %copy.181) | copy-start | bytes 1572868
  13.3 9.2 %copy-start.22 = (bf16[96,2048]{1,0:T(8,128)(2,1)S(1)}, bf16[96,2048]{1,0:T(8,128)(2,1)}, u32[]{:S(2)}) copy-start(bf16[96,2048]{1,0:T(8,128)(2,1)} %param.20) | copy-start | bytes 1179652
  13.3 22.7 %collective-permute-start = (bf16[128,2048]{0,1:T(8,128)(2,1)S(1)}, bf16[128,2048]{0,1:T(8,128)(2,1)}, u32[]{:S(2)}, u32[]{:S(2)}) collective-permute-start(bf16[128,2048]{0,1:T(8,128)(2,1)S(1)} %copy.181), channel_id=1, source_target_pairs={{0,4},{4,8},{8,12},{12,16},{16,20},{20,24},{24,28},{1,5},{5,9},{9,... | collective-permute-start | bytes 1572872 | tf_op jit(solution)/shard_map/ppermute | solution.py:20
  19.2 27.7 %collective-permute-start.1 = (bf16[128,2048]{0,1:T(8,128)(2,1)}, bf16[128,2048]{0,1:T(8,128)(2,1)}, u32[]{:S(2)}, u32[]{:S(2)}) collective-permute-start(bf16[128,2048]{0,1:T(8,128)(2,1)} %copy.118), channel_id=1, source_target_pairs={{0,4},{4,8},{8,12},{12,16},{16,20},{20,24},{24,28},{1,5},{5,9},{9,... | collective-permute-start | bytes 1572872 | tf_op jit(solution)/shard_map/ppermute | solution.py:20
  24.9 7.8 %copy-start.20 = (bf16[128,2048]{1,0:T(8,128)(2,1)S(1)}, bf16[128,2048]{1,0:T(8,128)(2,1)}, u32[]{:S(2)}) copy-start(bf16[128,2048]{1,0:T(8,128)(2,1)} %param.16) | copy-start | bytes 1572868
  27.5 28.6 %all-to-all-start.1 = ((bf16[8,16,2048]{2,1,0:T(8,128)(2,1)}), bf16[8,16,2048]{2,1,0:T(8,128)(2,1)}, u32[]{:S(2)}, u32[]{:S(2)}) async-start(bf16[8,16,2048]{2,1,0:T(8,128)(2,1)} %reshape.251), calls=%async_computation.1 | async-start | bytes 1048576 | tf_op jit(solution)/shard_map/all_to_all | solution.py:106
  32.7 2.5 %copy-start.21 = (bf16[128,2048]{1,0:T(8,128)(2,1)S(1)}, bf16[128,2048]{1,0:T(8,128)(2,1)}, u32[]{:S(2)}) copy-start(bf16[128,2048]{1,0:T(8,128)(2,1)} %param.23) | copy-start | bytes 1572868
  36.1 24.3 %collective-permute-start.2 = (bf16[128,2048]{0,1:T(8,128)(2,1)}, bf16[128,2048]{0,1:T(8,128)(2,1)}, u32[]{:S(2)}, u32[]{:S(2)}) collective-permute-start(bf16[128,2048]{0,1:T(8,128)(2,1)} %collective-permute-done), channel_id=1, source_target_pairs={{0,4},{4,8},{8,12},{12,16},{16,20},{20,24},{24,28},{1,5},{5,9},{9,... | collective-permute-start | bytes 1572872 | tf_op jit(solution)/shard_map/ppermute | solution.py:20
  46.8 23.4 %collective-permute-start.3 = (bf16[128,2048]{0,1:T(8,128)(2,1)}, bf16[128,2048]{0,1:T(8,128)(2,1)}, u32[]{:S(2)}, u32[]{:S(2)}) collective-permute-start(bf16[128,2048]{0,1:T(8,128)(2,1)} %collective-permute-done.1), channel_id=1, source_target_pairs={{0,4},{4,8},{8,12},{12,16},{16,20},{20,24},{24,28},{1,5},{5,9},{9,... | collective-permute-start | bytes 1572872 | tf_op jit(solution)/shard_map/ppermute | solution.py:20
  56.0 1.4 copy-start.5
  57.4 1.4 copy-start.8
  57.8 1.0 copy-start
  58.8 1.0 copy-start.13
  73.3 1.0 copy-start.14
  74.3 1.7 copy-start.1
  81.6 37.2 %collective-permute-start.6 = (bf16[128,2048]{0,1:T(8,128)(2,1)}, bf16[128,2048]{0,1:T(8,128)(2,1)}, u32[]{:S(2)}, u32[]{:S(2)}) collective-permute-start(bf16[128,2048]{0,1:T(8,128)(2,1)} %get-tuple-element.136), channel_id=1, source_target_pairs={{4,0},{8,4},{12,8},{16,12},{20,16},{24,20},{28,24},{5,1},{9,5},{13... | collective-permute-start | bytes 1572872 | tf_op jit(solution)/shard_map/ppermute | solution.py:20
  82.9 2.0 copy-start.17
  82.9 33.2 %collective-permute-start.4 = (bf16[128,2048]{0,1:T(8,128)(2,1)}, bf16[128,2048]{0,1:T(8,128)(2,1)}, u32[]{:S(2)}, u32[]{:S(2)}) collective-permute-start(bf16[128,2048]{0,1:T(8,128)(2,1)} %get-tuple-element.134), channel_id=1, source_target_pairs={{4,0},{8,4},{12,8},{16,12},{20,16},{24,20},{28,24},{5,1},{9,5},{13... | collective-permute-start | bytes 1572872 | tf_op jit(solution)/shard_map/ppermute | solution.py:20
  117.6 18.1 %collective-permute-start.5 = (bf16[128,2048]{0,1:T(8,128)(2,1)S(1)}, bf16[128,2048]{0,1:T(8,128)(2,1)S(1)}, u32[]{:S(2)}, u32[]{:S(2)}) collective-permute-start(bf16[128,2048]{0,1:T(8,128)(2,1)S(1)} %add_convert_fusion.1), channel_id=1, source_target_pairs={{4,0},{8,4},{12,8},{16,12},{20,16},{24,20},{28,24},{5,1},{9,5},{13... | collective-permute-start | bytes 1572872 | tf_op jit(solution)/shard_map/ppermute | solution.py:20
  118.9 3.7 %copy-start.10 = (bf16[128,2048]{0,1:T(8,128)(2,1)S(1)}, bf16[128,2048]{0,1:T(8,128)(2,1)}, u32[]{:S(2)}) copy-start(bf16[128,2048]{0,1:T(8,128)(2,1)} %copy-done.9) | copy-start | bytes 1572868
  118.9 3.7 %copy-start.11 = (f32[128,16,128]{2,0,1:T(8,128)S(1)}, f32[128,16,128]{2,0,1:T(8,128)}, u32[]{:S(2)}) copy-start(f32[128,16,128]{2,0,1:T(8,128)} %fusion.36) | copy-start | bytes 3145732
  118.9 3.7 %copy-start.18 = (bf16[16,128,128]{2,1,0:T(8,128)(2,1)S(1)}, bf16[16,128,128]{2,1,0:T(8,128)(2,1)}, u32[]{:S(2)}) copy-start(bf16[16,128,128]{2,1,0:T(8,128)(2,1)} %fusion.40) | copy-start | bytes 1572868
  121.3 23.0 %collective-permute-start.7 = (bf16[128,2048]{0,1:T(8,128)(2,1)}, bf16[128,2048]{0,1:T(8,128)(2,1)}, u32[]{:S(2)}, u32[]{:S(2)}) collective-permute-start(bf16[128,2048]{0,1:T(8,128)(2,1)} %add_convert_fusion), channel_id=1, source_target_pairs={{4,0},{8,4},{12,8},{16,12},{20,16},{24,20},{28,24},{5,1},{9,5},{13... | collective-permute-start | bytes 1572872 | tf_op jit(solution)/shard_map/ppermute | solution.py:20
  135.7 0.9 copy-start.15
  210.4 2.1 copy-start.16
where the time goes:
time: 218 us; the launch traced here: 217 us
  waiting for transfers between devices  60.3 us (28%)
  blocking collectives  58.6 us (27%)
  starting transfers between devices  36.5 us (17%)
  local copies, waits for them, and re-layouts  28.1 us (13%)
  other arithmetic  15.9 us (7%)
  matrix products  12.3 us (6%)
  between operations  4.93 us (2%)
    psum x1, blocking collectives, on_device(): all_squares = lax.psum(local_squares, ('ctx', 'head'))  58.6 us
    ppermute x8, waiting for transfers between devices, shifted(): lax.ppermute(value, axis, [(source, source + steps) for source in range(i...  57.7 us
    ppermute x8, starting transfers between devices, shifted(): lax.ppermute(value, axis, [(source, source + steps) for source in range(i...  25 us
    unnamed x48, local copies, waits for them, and re-layouts  11.2 us
    all_to_all x1, starting transfers between devices, on_device(): lax.all_to_all(pack(memory_keys), 'ctx', split_axis=0, concat_axis=0, til...  7.41 us
    another operation x6, local copies, waits for them, and re-layouts  5.98 us
    dot_general x2, matrix products, block_grads(): jnp.einsum('hqk,khd->qhd', score_grad, block_keys, preferred_element_type...  5.62 us
  transfers between devices with their start and end apart: 10, of which 6 were waited for; matrix products, arithmetic and copies ran while one was open for 13% of the time, Pallas kernels for 0%

commit v1 on v0

v1 whole, which is shorter than its diff:
```python
import math

import jax
import jax.numpy as jnp
from jax import lax
from jax.experimental import pallas as pl
from jax.experimental.pallas import tpu as pltpu
from jax.sharding import PartitionSpec as P

HDIM = 128
BLK = 8
CAP = 2
NEGATIVE = -1e30
LOG2E = 1.4426950408889634
F32 = jnp.float32
BF16 = jnp.bfloat16


def dot_nt(a, b):
    return lax.dot_general(a, b, (((1,), (1,)), ((), ())), preferred_element_type=F32)


def dot_nn(a, b):
    return lax.dot_general(a, b, (((1,), (0,)), ((), ())), preferred_element_type=F32)


def shifted(value, steps):
    count = lax.axis_size("ctx")
    pairs = [(i, i + steps) for i in range(count) if 0 <= i + steps < count]
    return lax.ppermute(value, "ctx", pairs)


def swapped(value):
    count = lax.axis_size("ctx")
    return lax.ppermute(value, "ctx", [(i, i ^ 1) for i in range(count)])


def cost(flops, size, exps=0):
    return pl.CostEstimate(flops=int(flops), bytes_accessed=int(size), transcendentals=int(exps))


def pack_memory(my_routes, memory_keys, memory_values, count):
    blocks = memory_keys.shape[0] // BLK
    width = memory_keys.shape[1]
    half = width // 2

    def body(routes_ref, mk_ref, mv_ref, out_ref, used):
        out_ref[...] = jnp.zeros_like(out_ref)
        for owner in range(count):
            used[owner] = 0

        def place(block, carry):
            owner = routes_ref[block]
            slot = used[owner]
            used[owner] = slot + 1
            partner = owner + 1 - 2 * (owner % 2)
            near = pl.multiple_of((owner % 2) * half, half)
            far = pl.multiple_of(half - (owner % 2) * half, half)
            out_ref[owner, 0, slot, :, :half] = mk_ref[block, :, pl.ds(near, half)]
            out_ref[owner, 0, slot, :, half:] = mv_ref[block, :, pl.ds(near, half)]
            out_ref[partner, 1, slot, :, :half] = mk_ref[block, :, pl.ds(far, half)]
            out_ref[partner, 1, slot, :, half:] = mv_ref[block, :, pl.ds(far, half)]
            return carry

        lax.fori_loop(0, blocks, place, 0)

    return pl.pallas_call(
        body,
        out_shape=jax.ShapeDtypeStruct((count, 2, CAP, BLK, width), BF16),
        in_specs=[
            pl.BlockSpec(memory_space=pltpu.SMEM),
            pl.BlockSpec(memory_space=pltpu.VMEM),
            pl.BlockSpec(memory_space=pltpu.VMEM),
        ],
        out_specs=pl.BlockSpec(memory_space=pltpu.VMEM),
        scratch_shapes=[pltpu.SMEM((count,), jnp.int32)],
        cost_estimate=cost(0, 4 * memory_keys.size * 2),
        name="pack_memory",
    )(
        my_routes,
        memory_keys.reshape(blocks, BLK, width),
        memory_values.reshape(blocks, BLK, width),
    )


def visible_bias(key_doc, key_pos, query_doc, query_pos):
    return jnp.where((key_doc == query_doc) & (key_pos <= query_pos), 0.0, NEGATIVE)


class Plan:
    def __init__(self, rows, half, memory_rows):
        self.rows, self.half, self.memory_rows = rows, half, memory_rows
        self.heads = half // HDIM
        self.group = 2 if self.heads % 2 == 0 else 1
        self.steps = self.heads // self.group
        self.cols = self.group * HDIM
        self.scale = 1.0 / math.sqrt(HDIM)

    def first(self):
        return pl.BlockSpec((self.rows, self.cols), lambda i: (0, i))

    def second(self):
        return pl.BlockSpec((self.rows, self.cols), lambda i: (0, self.steps + i))

    def memory(self, part):
        slots = self.memory_rows // (CAP * BLK)
        return pl.BlockSpec(
            (slots, 2, CAP * BLK, self.cols), lambda i: (0, 0, 0, part * self.steps + i)
        )

    def whole(self, shape):
        return pl.BlockSpec(shape, lambda i: (0,) * len(shape))

    def stacked(self):
        return pl.BlockSpec((2, self.rows, self.cols), lambda i: (0, 0, i))


def joined(refs, lanes):
    return jnp.concatenate([ref[:, lanes] for ref in refs], axis=0)


def scores_of(plan, query, key_refs, memory_ref, bias, memory_bias_ref, lanes, rows):
    scaling = plan.scale * LOG2E
    keys = joined(key_refs, lanes)
    current = dot_nt(query, keys) * scaling + bias
    parts, memory_keys = [], []
    for part in range(2):
        mem = memory_ref[:, part, :, lanes].reshape(plan.memory_rows, HDIM)
        score = dot_nt(query[part * rows : (part + 1) * rows], mem)
        parts.append(score * scaling + memory_bias_ref[part : part + 1, :])
        memory_keys.append(mem)
    return keys, memory_keys, current, jnp.concatenate(parts, axis=0)


def forward(plan, own_qd, far_qd, kv, memory, key_row, query_col, memory_bias):
    rows = plan.rows

    def body(
        qo, qf, do_o, do_f, k0, k1, k2, k3, v0, v1, v2, v3, mk, mv, krow, qcol, mbias,
        att_own, att_far, stat_col, stat_row,
    ):
        bias = visible_bias(krow[0:1, :], krow[1:2, :], qcol[:, 0:1], qcol[:, 1:2])
        lane = lax.broadcasted_iota(jnp.int32, (2 * rows, HDIM), 1)
        stats = jnp.zeros((2 * rows, HDIM), F32)
        for g in range(plan.group):
            lanes = slice(g * HDIM, (g + 1) * HDIM)
            query = joined((qo, qf), lanes)
            _, _, current, mem = scores_of(
                plan, query, (k0, k1, k2, k3), mk, bias, mbias, lanes, rows
            )
            top = jnp.maximum(
                jnp.max(current, axis=1, keepdims=True), jnp.max(mem, axis=1, keepdims=True)
            )
            weight = jnp.exp2(current - top)
            mem_weight = jnp.exp2(mem - top)
            total = jnp.sum(weight, axis=1, keepdims=True) + jnp.sum(
                mem_weight, axis=1, keepdims=True
            )
            values = joined((v0, v1, v2, v3), lanes)
            mixed = dot_nn(weight.astype(BF16), values)
            mem16 = mem_weight.astype(BF16)
            mixed_mem = [
                dot_nn(
                    mem16[part * rows : (part + 1) * rows],
                    mv[:, part, :, lanes].reshape(plan.memory_rows, HDIM),
                )
                for part in range(2)
            ]
            output = (mixed + jnp.concatenate(mixed_mem, axis=0)) / total
            upstream = joined((do_o, do_f), lanes).astype(F32)
            delta = jnp.sum(upstream * output, axis=1, keepdims=True)
            level = top + jnp.log2(total)
            stats = jnp.where(lane == g, level, stats)
            stats = jnp.where(lane == plan.group + g, delta, stats)
            att_own[:, lanes] = output[:rows].astype(BF16)
            att_far[:, lanes] = output[rows:].astype(BF16)
        stat_col[0] = stats
        stat_row[0] = stats.T[0:8, :]

    flops = 2 * 2 * (2 * rows) * (4 * rows + plan.memory_rows) * plan.half
    return pl.pallas_call(
        body,
        grid=(plan.steps,),
        out_shape=(
            jax.ShapeDtypeStruct((rows, plan.half), BF16),
            jax.ShapeDtypeStruct((rows, plan.half), BF16),
            jax.ShapeDtypeStruct((plan.steps, 2 * rows, HDIM), F32),
            jax.ShapeDtypeStruct((plan.steps, 8, 2 * rows), F32),
        ),
        in_specs=[plan.first()] * 2
        + [plan.second()] * 2
        + [plan.first()] * 4
        + [plan.second()] * 4
        + [plan.memory(0), plan.memory(1)]
        + [plan.whole(key_row.shape), plan.whole(query_col.shape), plan.whole(memory_bias.shape)],
        out_specs=(
            plan.first(),
            plan.first(),
            pl.BlockSpec((1, 2 * rows, HDIM), lambda i: (i, 0, 0)),
            pl.BlockSpec((1, 8, 2 * rows), lambda i: (i, 0, 0)),
        ),
        cost_estimate=cost(flops, 12 * rows * plan.half * 2, 2 * rows * 5 * rows * plan.heads),
        name="attend",
    )(own_qd, far_qd, own_qd, far_qd, *kv, *kv, memory, memory, key_row, query_col, memory_bias)


def query_gradient(plan, own_qd, far_qd, kv, memory, key_row, query_col, memory_bias, stats, att):
    rows = plan.rows

    def body(
        qo, qf, do_o, do_f, k0, k1, k2, k3, v0, v1, v2, v3, mk, mv, krow, qcol, mbias,
        stat_col, att_far, dq_own, send, squares,
    ):
        bias = visible_bias(krow[0:1, :], krow[1:2, :], qcol[:, 0:1], qcol[:, 1:2])
        acc = jnp.zeros((8, HDIM), F32)
        for g in range(plan.group):
            lanes = slice(g * HDIM, (g + 1) * HDIM)
            query = joined((qo, qf), lanes)
            upstream = joined((do_o, do_f), lanes)
            level = stat_col[0, :, g : g + 1]
            delta = stat_col[0, :, plan.group + g : plan.group + g + 1]
            keys, mem_keys, current, mem = scores_of(
                plan, query, (k0, k1, k2, k3), mk, bias, mbias, lanes, rows
            )
            values = joined((v0, v1, v2, v3), lanes)
            press = dot_nt(upstream, values) - delta
            grad = (jnp.exp2(current - level) * press).astype(BF16)
            result = dot_nn(grad, keys)
            extra = []
            for part in range(2):
                span = slice(part * rows, (part + 1) * rows)
                mem_values = mv[:, part, :, lanes].reshape(plan.memory_rows, HDIM)
                mem_press = dot_nt(upstream[span], mem_values) - delta[span]
                mem_grad = (jnp.exp2(mem[span] - level[span]) * mem_press).astype(BF16)
                extra.append(dot_nn(mem_grad, mem_keys[part]))
            result = (result + jnp.concatenate(extra, axis=0)) * plan.scale
            dq_own[:, lanes] = result[:rows]
            send[0, :, lanes] = result[rows:].astype(BF16)
            acc = acc + jnp.sum((result * result).reshape(-1, 8, HDIM), axis=0)
        send[1] = att_far[...]

        @pl.when(pl.program_id(0) == 0)
        def _():
            squares[...] = jnp.zeros_like(squares)

        squares[...] += acc

    flops = 3 * 2 * (2 * rows) * (4 * rows + plan.memory_rows) * plan.half
    return pl.pallas_call(
        body,
        grid=(plan.steps,),
        out_shape=(
            jax.ShapeDtypeStruct((rows, plan.half), F32),
            jax.ShapeDtypeStruct((2, rows, plan.half), BF16),
            jax.ShapeDtypeStruct((8, HDIM), F32),
        ),
        in_specs=[plan.first()] * 2
        + [plan.second()] * 2
        + [plan.first()] * 4
        + [plan.second()] * 4
        + [plan.memory(0), plan.memory(1)]
        + [plan.whole(key_row.shape), plan.whole(query_col.shape), plan.whole(memory_bias.shape)]
        + [pl.BlockSpec((1, 2 * rows, HDIM), lambda i: (i, 0, 0)), plan.first()],
        out_specs=(plan.first(), plan.stacked(), plan.whole((8, HDIM))),
        cost_estimate=cost(flops, 14 * rows * plan.half * 2, 2 * rows * 5 * rows * plan.heads),
        name="query_gradient",
    )(
        own_qd, far_qd, own_qd, far_qd, *kv, *kv, memory, memory, key_row, query_col, memory_bias,
        stats, att,
    )


def key_terms(plan, key, value, query, upstream, bias, level, delta):
    score = dot_nt(key, query) * (plan.scale * LOG2E) + bias
    prob = jnp.exp2(score - level)
    grad = (prob * (dot_nt(value, upstream) - delta)).astype(BF16)
    return dot_nn(grad, query) * plan.scale, dot_nn(prob.astype(BF16), upstream)


def key_gradient_near(plan, own_qd, far_qd, own_kv, far_kv, query_row, key_col, stats):
    rows = plan.rows

    def body(qo, qf, do_o, do_f, k0, k1, v0, v1, qrow, kcol, stat, dk, dv):
        bias = visible_bias(kcol[:, 0:1], kcol[:, 1:2], qrow[0:1, :], qrow[1:2, :])
        for g in range(plan.group):
            lanes = slice(g * HDIM, (g + 1) * HDIM)
            key_part, value_part = key_terms(
                plan,
                joined((k0, k1), lanes),
                joined((v0, v1), lanes),
                joined((qo, qf), lanes),
                joined((do_o, do_f), lanes),
                bias,
                stat[0, g : g + 1, :],
                stat[0, plan.group + g : plan.group + g + 1, :],
            )
            dk[:, lanes] = key_part
            dv[:, lanes] = value_part

    both = pl.BlockSpec((2 * rows, plan.cols), lambda i: (0, i))
    return pl.pallas_call(
        body,
        grid=(plan.steps,),
        out_shape=(jax.ShapeDtypeStruct((2 * rows, plan.half), F32),) * 2,
        in_specs=[plan.first()] * 2
        + [plan.second()] * 2
        + [plan.first()] * 2
        + [plan.second()] * 2
        + [plan.whole(query_row.shape), plan.whole(key_col.shape)]
        + [pl.BlockSpec((1, 8, 2 * rows), lambda i: (i, 0, 0))],
        out_specs=(both, both),
        cost_estimate=cost(
            4 * 2 * (2 * rows) ** 2 * plan.half, 16 * rows * plan.half * 2, 4 * rows * rows * plan.heads
        ),
        name="key_gradient_near",
    )(own_qd, far_qd, own_qd, far_qd, own_kv, far_kv, own_kv, far_kv, query_row, key_col, stats)


def key_gradient_next(
    plan, own_qd, far_qd, own_kv, far_kv, query_row, key_col, stats, near_dk, near_dv, dq_squares, devices
):
    rows = plan.rows

    def body(
        qo, qf, do_o, do_f, k0, k1, v0, v1, qrow, kcol, stat, dk_in, dv_in, dq_sq,
        dk_own, dv_own, send, share, squares,
    ):
        bias = visible_bias(kcol[:, 0:1], kcol[:, 1:2], qrow[0:1, :], qrow[1:2, :])
        acc = jnp.zeros((8, HDIM), F32)
        for g in range(plan.group):
            lanes = slice(g * HDIM, (g + 1) * HDIM)
            key_part, value_part = key_terms(
                plan,
                joined((k0, k1), lanes),
                joined((v0, v1), lanes),
                joined((qo, qf), lanes),
                joined((do_o, do_f), lanes),
                bias,
                stat[0, g : g + 1, :],
                stat[0, plan.group + g : plan.group + g + 1, :],
            )
            key_part = key_part + dk_in[:, lanes]
            value_part = value_part + dv_in[:, lanes]
            dk_own[:, lanes] = key_part[:rows]
            dv_own[:, lanes] = value_part[:rows]
            send[0, :, lanes] = key_part[rows:].astype(BF16)
            send[1, :, lanes] = value_part[rows:].astype(BF16)
            both = key_part * key_part + value_part * value_part
            acc = acc + jnp.sum(both.reshape(-1, 8, HDIM), axis=0)

        @pl.when(pl.program_id(0) == 0)
        def _():
            squares[...] = dq_sq[...]

        squares[...] += acc

        @pl.when(pl.program_id(0) == plan.steps - 1)
        def _():
            row = jnp.sum(squares[...], axis=0, keepdims=True)
            share[...] = jnp.broadcast_to(row, share.shape)

    both = pl.BlockSpec((2 * rows, plan.cols), lambda i: (0, i))
    return pl.pallas_call(
        body,
        grid=(plan.steps,),
        out_shape=(
            jax.ShapeDtypeStruct((rows, plan.half), F32),
            jax.ShapeDtypeStruct((rows, plan.half), F32),
            jax.ShapeDtypeStruct((2, rows, plan.half), BF16),
            jax.ShapeDtypeStruct((devices, HDIM), F32),
        ),
        in_specs=[plan.first()] * 2
        + [plan.second()] * 2
        + [plan.first()] * 2
        + [plan.second()] * 2
        + [plan.whole(query_row.shape), plan.whole(key_col.shape)]
        + [pl.BlockSpec((1, 8, 2 * rows), lambda i: (i, 0, 0)), both, both]
        + [plan.whole((8, HDIM))],
        out_specs=(plan.first(), plan.first(), plan.stacked(), plan.whole((devices, HDIM))),
        scratch_shapes=[pltpu.VMEM((8, HDIM), F32)],
        cost_estimate=cost(
            4 * 2 * (2 * rows) ** 2 * plan.half, 24 * rows * plan.half * 2, 4 * rows * rows * plan.heads
        ),
        name="key_gradient_next",
    )(
        own_qd, far_qd, own_qd, far_qd, own_kv, far_kv, own_kv, far_kv, query_row, key_col, stats,
        near_dk, near_dv, dq_squares,
    )


def scaled(plan, side, shares, entries, dq_own, dq_far, dk_own, dv_own, kv_far):
    rows, half = plan.rows, plan.half

    def body(side_ref, share, dq, dq_other, dk, dv, other, dq_out, dk_out, dv_out):
        squares = jnp.sum(jnp.sum(share[...], axis=0, keepdims=True), axis=1, keepdims=True)
        inverse = 1.0 / jnp.sqrt(squares / entries + 1e-06)
        near = pl.multiple_of(side_ref[0] * half, half)
        away = pl.multiple_of(half - side_ref[0] * half, half)
        for out, mine, theirs in (
            (dq_out, dq[...], dq_other[0]),
            (dk_out, dk[...], other[0]),
            (dv_out, dv[...], other[1]),
        ):
            out[:, pl.ds(near, half)] = (mine * inverse).astype(BF16)
            out[:, pl.ds(away, half)] = (theirs.astype(F32) * inverse).astype(BF16)

    vmem = pl.BlockSpec(memory_space=pltpu.VMEM)
    return pl.pallas_call(
        body,
        out_shape=(jax.ShapeDtypeStruct((rows, 2 * half), BF16),) * 3,
        in_specs=[pl.BlockSpec(memory_space=pltpu.SMEM)] + [vmem] * 6,
        out_specs=(vmem,) * 3,
        cost_estimate=cost(6 * rows * half, 20 * rows * half),
        name="scaled",
    )(side, shares, dq_own, dq_far, dk_own, dv_own, kv_far)


def on_device(query, keys, values, memory_keys, memory_values, routes, documents, cotangent):
    rows, width = query.shape
    half = width // 2
    count = lax.axis_size("ctx")
    devices = count * lax.axis_size("head")
    position = lax.axis_index("ctx").astype(jnp.int32)
    side = position % 2
    partner = position + 1 - 2 * side
    per_device = memory_keys.shape[0] // BLK
    memory_rows = count * CAP * BLK
    plan = Plan(rows, half, memory_rows)

    def halves(left, right, which):
        start = which * half
        return jnp.concatenate(
            [
                lax.dynamic_slice(left, (0, start), (rows, half)),
                lax.dynamic_slice(right, (0, start), (rows, half)),
            ],
            axis=1,
        )

    own_kv = halves(keys, values, side)
    own_qd = halves(query, cotangent, side)
    far_kv = swapped(halves(keys, values, 1 - side))
    far_qd = swapped(halves(query, cotangent, 1 - side))
    route_table = routes[:, 0].reshape(count, per_device)
    my_routes = lax.dynamic_slice_in_dim(routes[:, 0], position * per_device, per_device)
    packed = pack_memory(my_routes, memory_keys, memory_values, count)
    arrived = lax.all_to_all(
        packed.reshape(count, 2 * CAP * BLK, width), "ctx", split_axis=0, concat_axis=0, tiled=True
    ).reshape(count, 2, CAP * BLK, width)
    prev_own_kv = shifted(own_kv, 2)
    prev_far_kv = shifted(far_kv, 2)
    next_own_qd = shifted(own_qd, -2)
    next_far_qd = shifted(far_qd, -2)

    def labels(block):
        docs = lax.dynamic_slice_in_dim(documents, block * rows, rows)
        docs = jnp.where((block >= 0) & (block < count), docs, -1)
        return jnp.stack([docs, block * rows + jnp.arange(rows, dtype=jnp.int32)])

    near_row = jnp.concatenate([labels(position), labels(partner)], axis=1)
    prev_row = jnp.concatenate([labels(position - 2), labels(partner - 2)], axis=1)
    next_row = jnp.concatenate([labels(position + 2), labels(partner + 2)], axis=1)
    key_row = jnp.concatenate([near_row, prev_row], axis=1)
    near_col = near_row.T
    readers = jnp.stack([position, partner])
    arrivals = jnp.sum((route_table[None] == readers[:, None, None]).astype(jnp.int32), axis=2)
    live = jnp.arange(CAP, dtype=jnp.int32)[None, None, :] < arrivals[:, :, None]
    memory_bias = jnp.broadcast_to(
        jnp.where(live, 0.0, NEGATIVE)[..., None], (2, count, CAP, BLK)
    ).reshape(2, memory_rows)

    kv = (own_kv, far_kv, prev_own_kv, prev_far_kv)
    att_own, att_far, stat_col, stat_row = forward(
        plan, own_qd, far_qd, kv, arrived, key_row, near_col, memory_bias
    )
    next_stats = shifted(stat_row, -2)
    dq_own, first_send, dq_squares = query_gradient(
        plan, own_qd, far_qd, kv, arrived, key_row, near_col, memory_bias, stat_col, att_far
    )
    first_back = swapped(first_send)
    near_dk, near_dv = key_gradient_near(
        plan, own_qd, far_qd, own_kv, far_kv, near_row, near_col, stat_row
    )
    dk_own, dv_own, second_send, share = key_gradient_next(
        plan, next_own_qd, next_far_qd, own_kv, far_kv, next_row, near_col, next_stats,
        near_dk, near_dv, dq_squares, devices,
    )
    second_back = swapped(second_send)
    shares = lax.all_to_all(share, ("ctx", "head"), split_axis=0, concat_axis=0, tiled=True)
    entries = 3.0 * count * rows * width * lax.axis_size("head")
    query_grad, key_grad, value_grad = scaled(
        plan, side[None], shares, entries, dq_own, first_back, dk_own, dv_own, second_back
    )
    att_back = first_back[1]
    attended = jnp.where(
        side == 0,
        jnp.concatenate([att_own, att_back], axis=1),
        jnp.concatenate([att_back, att_own], axis=1),
    )
    return attended, query_grad, key_grad, value_grad


def solution(mesh):
    spread = P("ctx", "head")
    return jax.shard_map(
        on_device,
        mesh=mesh,
        in_specs=(spread,) * 5 + (P(), P(), spread),
        out_specs=(spread,) * 4,
        check_vma=False,
    )
```

time: 218 us -> 111 us (0.51)
  blocking collectives: 58.6 us -> 0 us
  Pallas kernels: 0 us -> 30 us
  waiting for transfers between devices: 60.3 us -> 34.7 us
  local copies, waits for them, and re-layouts: 28.1 us -> 7.12 us
  matrix products: 12.3 us -> 0 us
  other arithmetic: 15.9 us -> 5.01 us
  between operations: 4.93 us -> 0.89 us
  starting transfers between devices: 36.5 us -> 32.9 us
    psum x1 -> x0, blocking collectives: 58.6 us -> none  [on_device(): all_squares = lax.psum(local_squares, ('ctx', 'head'))]
    pallas_call x0 -> x6, Pallas kernels: none -> 30 us  [the longest x1 6.93 us: query_gradient(): pl.pallas_call(body, grid=(plan.steps,), out_shape=(jax.ShapeDtypeStruct(...]
    ppermute x8 -> x9, waiting for transfers between devices: 57.7 us -> 29.5 us  [the longest x4 22.4 us: swapped(): return lax.ppermute(value, 'ctx', [(i, i ^ 1) for i in range(count)])]
    dot_general x11 -> x0, matrix products: 12.3 us -> none  [the longest x2 5.62 us: block_grads(): jnp.einsum('hqk,khd->qhd', score_grad, block_keys, preferred_element_type...]
    convert_element_type x5 -> x0, other arithmetic: 7.84 us -> none  [the longest x1 2.4 us: on_device(): value_moving.astype(jnp.bfloat16)]
    ppermute x8 -> x9, starting transfers between devices: 25 us -> 18 us  [the longest x5 13.4 us: shifted(): return lax.ppermute(value, 'ctx', pairs)]
    unnamed x48 -> x37, local copies, waits for them, and re-layouts: 11.2 us -> 4.66 us
    another operation x8 -> x0, local copies, waits for them, and re-layouts: 6.17 us -> none
  transfers between devices with their start and end apart: 10 -> 11, of which waited for: 6 -> 3; matrix products, arithmetic and copies ran while one was open for 13% -> 7% of each run, Pallas kernels for 0% -> 22%
where the time goes in v1:
time: 111 us
  waiting for transfers between devices  34.7 us (31%)
  starting transfers between devices  32.9 us (30%)
  Pallas kernels  30 us (27%)
  local copies, waits for them, and re-layouts  7.12 us (6%)
  other arithmetic  5.01 us (5%)
    ppermute x4, waiting for transfers between devices, swapped(): return lax.ppermute(value, 'ctx', [(i, i ^ 1) for i in range(count)])  22.4 us
    ppermute x5, starting transfers between devices, shifted(): return lax.ppermute(value, 'ctx', pairs)  13.4 us
    all_to_all x1, starting transfers between devices, on_device(): lax.all_to_all(packed.reshape(count, 2 * CAP * BLK, width), 'ctx', split_...  7.41 us
    all_to_all x1, starting transfers between devices, on_device(): lax.all_to_all(share, ('ctx', 'head'), split_axis=0, concat_axis=0, tiled...  7.4 us
    ppermute x5, waiting for transfers between devices, shifted(): return lax.ppermute(value, 'ctx', pairs)  7.12 us
    pallas_call x1, Pallas kernels, query_gradient(): pl.pallas_call(body, grid=(plan.steps,), out_shape=(jax.ShapeDtypeStruct(...  6.93 us
    pallas_call x1, Pallas kernels, forward(): pl.pallas_call(body, grid=(plan.steps,), out_shape=(jax.ShapeDtypeStruct(...  6.79 us
    pallas_call x1, Pallas kernels, key_gradient_next(): pl.pallas_call(body, grid=(plan.steps,), out_shape=(jax.ShapeDtypeStruct(...  5.58 us
  transfers between devices with their start and end apart: 11, of which 3 were waited for; matrix products, arithmetic and copies ran while one was open for 7% of the time, Pallas kernels for 22%

profile of v1, /device:TPU:0, one launch (start us, length us, event | category | flops | bytes accessed | tf_op | source)
XLA Modules:
  0.0 110.6 jit_solution(6474595468828399799)
XLA Ops:
  0.6 0.0 copy-start.17
  0.6 0.6 copy-done.17
  1.3 0.6 fusion.7.routes_ref
  1.9 2.4 %pack_memory.1 = bf16[8,2,2,8,2048]{4,3,2,1,0:T(8,128)(2,1)} custom-call(s32[12]{0:T(128)} %fusion.7.routes_ref, bf16[12,8,2048]{2,1,0:T(8,128)(2,1)} %bitcast.38, bf16[12,8,2048]{2,1,0:T(8,128)(2,1)} %bitcast.39), custom_call_target="tpu_custom_call" | custom-call | bytes 1572864 | tf_op jit(solution)/shard_map/pack_memory/pallas_call | solution.py:67
  4.3 7.4 %all-to-all-start = ((bf16[8,32,2048]{2,1,0:T(8,128)(2,1)}), bf16[8,32,2048]{2,1,0:T(8,128)(2,1)S(1)}, u32[]{:S(2)}, u32[]{:S(2)}) async-start(bf16[8,32,2048]{2,1,0:T(8,128)(2,1)} %bitcast.33), calls=%async_computation | async-start | bytes 2097152 | tf_op jit(solution)/shard_map/all_to_all | solution.py:447
  11.7 0.0 copy-done.6
  11.7 0.1 constant_dynamic-slice_fusion.5
  11.8 0.0 copy-start.3
  11.8 1.3 %collective-permute-start.5 = (bf16[128,2048]{1,0:T(8,128)(2,1)S(1)}, bf16[128,2048]{1,0:T(8,128)(2,1)}, u32[]{:S(2)}, u32[]{:S(2)}) collective-permute-start(bf16[128,2048]{1,0:T(8,128)(2,1)S(1)} %pad_maximum_fusion.qo.do_o), channel_id=1, source_target_pairs={{8,0},{12,4},{16,8},{20,12},{24,16},{28,20},{9,1},{13,5},{17,9},{2... | collective-permute-start | bytes 1572872 | tf_op jit(solution)/shard_map/ppermute | solution.py:30
  13.1 0.0 copy-start.8
  13.1 0.0 copy-start.9
  13.2 0.8 pad_maximum_fusion.1
  14.0 0.0 copy-done.3
  14.0 2.0 %collective-permute-start = (bf16[128,2048]{1,0:T(8,128)(2,1)}, bf16[128,2048]{1,0:T(8,128)(2,1)S(1)}, u32[]{:S(2)}, u32[]{:S(2)}) collective-permute-start(bf16[128,2048]{1,0:T(8,128)(2,1)} %pad_maximum_fusion.1), channel_id=1, source_target_pairs={{0,4},{4,0},{8,12},{12,8},{16,20},{20,16},{24,28},{28,24},{1,5},{5... | collective-permute-start | bytes 1572872 | tf_op jit(solution)/shard_map/ppermute | solution.py:35
  16.0 0.0 copy-done.8
  16.0 0.1 constant_dynamic-slice_fusion.1
  16.1 0.8 pad_maximum_fusion.3
  16.9 0.5 collective-permute-start.1
  17.5 0.0 copy-start
  17.5 5.3 %collective-permute-start.2 = (bf16[128,2048]{1,0:T(8,128)(2,1)S(1)}, bf16[128,2048]{1,0:T(8,128)(2,1)}, u32[]{:S(2)}, u32[]{:S(2)}) collective-permute-start(bf16[128,2048]{1,0:T(8,128)(2,1)S(1)} %pad_maximum_fusion.2.k0.v0), channel_id=1, source_target_pairs={{0,8},{4,12},{8,16},{12,20},{16,24},{20,28},{1,9},{5,13},{9,17},{1... | collective-permute-start | bytes 1572872 | tf_op jit(solution)/shard_map/ppermute | solution.py:30
  22.9 0.6 broadcast.61
  23.4 0.7 reduce.3
  24.1 0.1 eq.21
  24.2 0.1 pad_add_fusion
  24.3 0.2 convert_reduce_fusion
  24.5 0.1 fusion
  24.6 0.1 broadcast_in_dim.32
  24.7 0.7 reshape.79.mbias
  25.4 22.4 %collective-permute-done.1.k1.v1 = bf16[128,2048]{1,0:T(8,128)(2,1)S(1)} collective-permute-done((bf16[128,2048]{1,0:T(8,128)(2,1)}, bf16[128,2048]{1,0:T(8,128)(2,1)S(1)}, u32[]{:S(2)}, u32[]{:S(2)}) %collective-permute-start.1) | collective-permute-done | bytes 524320 | tf_op jit(solution)/shard_map/ppermute | solution.py:35
  47.7 4.2 %collective-permute-start.3 = (bf16[128,2048]{1,0:T(8,128)(2,1)S(1)}, bf16[128,2048]{1,0:T(8,128)(2,1)}, u32[]{:S(2)}, u32[]{:S(2)}) collective-permute-start(bf16[128,2048]{1,0:T(8,128)(2,1)S(1)} %collective-permute-done.1.k1.v1), channel_id=1, source_target_pairs={{0,8},{4,12},{8,16},{12,20},{16,24},{20,28},{1,9},{5,13},{9,17},{1... | collective-permute-start | bytes 1572872 | tf_op jit(solution)/shard_map/ppermute | solution.py:30
  51.9 0.1 fusion.5
  52.0 0.8 copy.21
  52.8 0.6 add_add_fusion.krow
  53.4 0.0 collective-permute-done.qf.do_f
  53.4 1.3 %collective-permute-start.6 = (bf16[128,2048]{1,0:T(8,128)(2,1)S(1)}, bf16[128,2048]{1,0:T(8,128)(2,1)}, u32[]{:S(2)}, u32[]{:S(2)}) collective-permute-start(bf16[128,2048]{1,0:T(8,128)(2,1)S(1)} %collective-permute-done.qf.do_f), channel_id=1, source_target_pairs={{8,0},{12,4},{16,8},{20,12},{24,16},{28,20},{9,1},{13,5},{17,9},{2... | collective-permute-start | bytes 1572872 | tf_op jit(solution)/shard_map/ppermute | solution.py:30
  54.7 0.0 collective-permute-done.2.k2.v2
  54.7 7.1 %collective-permute-done.3.k3.v3 = bf16[128,2048]{1,0:T(8,128)(2,1)} collective-permute-done((bf16[128,2048]{1,0:T(8,128)(2,1)S(1)}, bf16[128,2048]{1,0:T(8,128)(2,1)}, u32[]{:S(2)}, u32[]{:S(2)}) %collective-permute-start.3) | collective-permute-done | bytes 524320 | tf_op jit(solution)/shard_map/ppermute | solution.py:30
  61.9 0.0 all-to-all-done
  61.9 0.0 copy-done.4
  61.9 1.0 copy-done.2
  62.8 6.8 %attend.1 = (bf16[128,1024]{1,0:T(8,128)(2,1)}, bf16[128,1024]{1,0:T(8,128)(2,1)}, f32[4,256,128]{2,1,0:T(8,128)}, f32[4,8,256]{2,1,0:T(8,128)}) custom-call(bf16[128,2048]{1,0:T(8,128)(2,1)} %copy-done.3, bf16[128,2048]{1,0:T(8,128)(2,1)} %copy-done.4, bf16[128,2048]{1,0:T(8,128)(2,1)} %copy-done.3, bf16[128,2048]{1,0:T(8,128)(2,1)} %copy-done.4, ...), custom_call_target="tpu_custom_call" | custom-call | flops 671088640 | bytes 3145728 | tf_op jit(solution)/shard_map/attend/pallas_call | solution.py:181
  69.6 6.9 %query_gradient.1 = (f32[128,1024]{1,0:T(8,128)}, bf16[2,128,1024]{2,1,0:T(8,128)(2,1)}, f32[8,128]{1,0:T(8,128)}) custom-call(bf16[128,2048]{1,0:T(8,128)(2,1)} %copy-done.3, bf16[128,2048]{1,0:T(8,128)(2,1)} %copy-done.4, bf16[128,2048]{1,0:T(8,128)(2,1)} %copy-done.3, bf16[128,2048]{1,0:T(8,128)(2,1)} %copy-done.4, bf16[128,2048]{1,0:T(8,128)(2,1)} %copy-done, ...), custom_call_target="tpu_custom_call" | custom-call | flops 1006632960 | bytes 3670016 | tf_op jit(solution)/shard_map/query_gradient/pallas_call | solution.py:249
  76.6 0.4 collective-permute-start.4
  76.9 0.6 add_add_fusion.2.qrow
  77.5 0.0 copy-done.13
  77.5 1.3 %collective-permute-start.7 = (f32[4,8,256]{2,1,0:T(8,128)S(1)}, f32[4,8,256]{2,1,0:T(8,128)S(1)}, u32[]{:S(2)}, u32[]{:S(2)}) collective-permute-start(f32[4,8,256]{2,1,0:T(8,128)S(1)} %copy-done.13), channel_id=1, source_target_pairs={{8,0},{12,4},{16,8},{20,12},{24,16},{28,20},{9,1},{13,5},{17,9},{2... | collective-permute-start | bytes 98312 | tf_op jit(solution)/shard_map/ppermute | solution.py:30
  78.8 5.3 %key_gradient_near.1 = (f32[256,1024]{1,0:T(8,128)}, f32[256,1024]{1,0:T(8,128)}) custom-call(bf16[128,2048]{1,0:T(8,128)(2,1)} %copy-done.3, bf16[128,2048]{1,0:T(8,128)(2,1)} %copy-done.4, bf16[128,2048]{1,0:T(8,128)(2,1)} %copy-done.3, bf16[128,2048]{1,0:T(8,128)(2,1)} %copy-done.4, bf16[128,2048]{1,0:T(8,128)(2,1)} %copy-done, ...), custom_call_target="tpu_custom_call" | custom-call | flops 536870912 | bytes 4194304 | tf_op jit(solution)/shard_map/key_gradient_near/pallas_call | solution.py:301
  84.1 0.0 collective-permute-done.5.qo.do_o
  84.2 0.0 collective-permute-done.6.qf.do_f
  84.2 0.0 collective-permute-done.7.stat
  84.2 0.0 copy-start.14
  84.2 0.6 copy-done.14
  84.8 5.6 %key_gradient_next.1 = (f32[128,1024]{1,0:T(8,128)}, f32[128,1024]{1,0:T(8,128)}, bf16[2,128,1024]{2,1,0:T(8,128)(2,1)}, f32[32,128]{1,0:T(8,128)}) custom-call(bf16[128,2048]{1,0:T(8,128)(2,1)} %collective-permute-done.5.qo.do_o, bf16[128,2048]{1,0:T(8,128)(2,1)} %collective-permute-done.6.qf.do_f, bf16[128,2048]{1,0:T(8,128)(2,1)} %collective-permute-done.5.qo.do_o, ...), custom_call_target="tpu_custom_call" | custom-call | flops 536870912 | bytes 6291456 | tf_op jit(solution)/shard_map/key_gradient_next/pallas_call | solution.py:363
  90.4 1.8 %collective-permute-start.8 = (bf16[2,128,1024]{2,1,0:T(8,128)(2,1)}, bf16[2,128,1024]{2,1,0:T(8,128)(2,1)S(1)}, u32[]{:S(2)}, u32[]{:S(2)}) collective-permute-start(bf16[2,128,1024]{2,1,0:T(8,128)(2,1)} %get-tuple-element.32), channel_id=1, source_target_pairs={{0,4},{4,0},{8,12},{12,8},{16,20},{20,16},{24,28},{28,24},{1,5},{5... | collective-permute-start | bytes 1572872 | tf_op jit(solution)/shard_map/ppermute | solution.py:35
  92.2 7.4 %all-to-all-start.1 = ((f32[32,1,128]{2,1,0:T(1,128)}), f32[32,1,128]{2,1,0:T(1,128)S(1)}, u32[]{:S(2)}, u32[]{:S(2)}) async-start(f32[32,1,128]{2,1,0:T(1,128)} %bitcast.41), calls=%async_computation.1 | async-start | bytes 32768 | tf_op jit(solution)/shard_map/all_to_all | solution.py:489
  99.6 0.0 collective-permute-done.4.dq_other
  99.6 0.0 copy-start.5
  99.6 1.0 copy-done.11
  100.6 0.9 maximum_select_fusion
  101.5 5.2 %all-to-all-done.1 = f32[32,1,128]{2,1,0:T(1,128)S(1)} async-done(((f32[32,1,128]{2,1,0:T(1,128)}), f32[32,1,128]{2,1,0:T(1,128)S(1)}, u32[]{:S(2)}, u32[]{:S(2)}) %all-to-all-start.1) | async-done | bytes 16416 | tf_op jit(solution)/shard_map/all_to_all | solution.py:489
  106.7 0.0 collective-permute-done.8.other
  106.7 0.6 copy-done.12
  107.3 0.2 copy-done.10
  107.6 3.0 %scaled.1 = (bf16[128,2048]{1,0:T(8,128)(2,1)}, bf16[128,2048]{1,0:T(8,128)(2,1)}, bf16[128,2048]{1,0:T(8,128)(2,1)}) custom-call(s32[1]{0:T(128)} %bitcast.13.side_ref, f32[32,128]{1,0:T(8,128)} %bitcast.40, f32[128,1024]{1,0:T(8,128)} %get-tuple-element.29.dq, bf16[2,128,1024]{2,1,0:T(8,128)(2,1)} %copy-done.5, f32[128,1024]{1,0:T(8,128)} %get-tuple-element.30.dk, ...), custom_call_target="tpu_custom_call" | custom-call | flops 786432 | bytes 2621440 | tf_op jit(solution)/shard_map/scaled/pallas_call | solution.py:408
  (25 shorter events, 0.1 us)
Async XLA Ops:
  0.6 0.7 copy-start.17
  4.2 7.4 %copy-start.6 = (bf16[128,2048]{1,0:T(8,128)(2,1)S(1)}, bf16[128,2048]{1,0:T(8,128)(2,1)}, u32[]{:S(2)}) copy-start(bf16[128,2048]{1,0:T(8,128)(2,1)} %param.15) | copy-start | bytes 1572868
  4.3 7.4 %copy-start.7 = (bf16[128,2048]{1,0:T(8,128)(2,1)S(1)}, bf16[128,2048]{1,0:T(8,128)(2,1)}, u32[]{:S(2)}) copy-start(bf16[128,2048]{1,0:T(8,128)(2,1)} %param.8) | copy-start | bytes 1572868
  4.3 57.6 %all-to-all-start = ((bf16[8,32,2048]{2,1,0:T(8,128)(2,1)}), bf16[8,32,2048]{2,1,0:T(8,128)(2,1)S(1)}, u32[]{:S(2)}, u32[]{:S(2)}) async-start(bf16[8,32,2048]{2,1,0:T(8,128)(2,1)} %bitcast.33), calls=%async_computation | async-start | bytes 2097152 | tf_op jit(solution)/shard_map/all_to_all | solution.py:447
  11.8 2.2 %copy-start.3 = (bf16[128,2048]{1,0:T(8,128)(2,1)}, bf16[128,2048]{1,0:T(8,128)(2,1)S(1)}, u32[]{:S(2)}) copy-start(bf16[128,2048]{1,0:T(8,128)(2,1)S(1)} %pad_maximum_fusion.qo.do_o) | copy-start | bytes 1572868
  11.8 72.3 %collective-permute-start.5 = (bf16[128,2048]{1,0:T(8,128)(2,1)S(1)}, bf16[128,2048]{1,0:T(8,128)(2,1)}, u32[]{:S(2)}, u32[]{:S(2)}) collective-permute-start(bf16[128,2048]{1,0:T(8,128)(2,1)S(1)} %pad_maximum_fusion.qo.do_o), channel_id=1, source_target_pairs={{8,0},{12,4},{16,8},{20,12},{24,16},{28,20},{9,1},{13,5},{17,9},{2... | collective-permute-start | bytes 1572872 | tf_op jit(solution)/shard_map/ppermute | solution.py:30
  13.1 2.9 %copy-start.8 = (bf16[128,2048]{1,0:T(8,128)(2,1)S(1)}, bf16[128,2048]{1,0:T(8,128)(2,1)}, u32[]{:S(2)}) copy-start(bf16[128,2048]{1,0:T(8,128)(2,1)} %param.10) | copy-start | bytes 1572868
  13.1 2.9 %copy-start.9 = (bf16[128,2048]{1,0:T(8,128)(2,1)S(1)}, bf16[128,2048]{1,0:T(8,128)(2,1)}, u32[]{:S(2)}) copy-start(bf16[128,2048]{1,0:T(8,128)(2,1)} %param.9) | copy-start | bytes 1572868
  14.0 39.4 %collective-permute-start = (bf16[128,2048]{1,0:T(8,128)(2,1)}, bf16[128,2048]{1,0:T(8,128)(2,1)S(1)}, u32[]{:S(2)}, u32[]{:S(2)}) collective-permute-start(bf16[128,2048]{1,0:T(8,128)(2,1)} %pad_maximum_fusion.1), channel_id=1, source_target_pairs={{0,4},{4,0},{8,12},{12,8},{16,20},{20,16},{24,28},{28,24},{1,5},{5... | collective-permute-start | bytes 1572872 | tf_op jit(solution)/shard_map/ppermute | solution.py:35
  16.9 30.8 %collective-permute-start.1 = (bf16[128,2048]{1,0:T(8,128)(2,1)}, bf16[128,2048]{1,0:T(8,128)(2,1)S(1)}, u32[]{:S(2)}, u32[]{:S(2)}) collective-permute-start(bf16[128,2048]{1,0:T(8,128)(2,1)} %pad_maximum_fusion.3), channel_id=1, source_target_pairs={{0,4},{4,0},{8,12},{12,8},{16,20},{20,16},{24,28},{28,24},{1,5},{5... | collective-permute-start | bytes 1572872 | tf_op jit(solution)/shard_map/ppermute | solution.py:35
  17.5 44.4 %copy-start = (bf16[128,2048]{1,0:T(8,128)(2,1)}, bf16[128,2048]{1,0:T(8,128)(2,1)S(1)}, u32[]{:S(2)}) copy-start(bf16[128,2048]{1,0:T(8,128)(2,1)S(1)} %pad_maximum_fusion.2.k0.v0) | copy-start | bytes 1572868
  17.5 37.2 %collective-permute-start.2 = (bf16[128,2048]{1,0:T(8,128)(2,1)S(1)}, bf16[128,2048]{1,0:T(8,128)(2,1)}, u32[]{:S(2)}, u32[]{:S(2)}) collective-permute-start(bf16[128,2048]{1,0:T(8,128)(2,1)S(1)} %pad_maximum_fusion.2.k0.v0), channel_id=1, source_target_pairs={{0,8},{4,12},{8,16},{12,20},{16,24},{20,28},{1,9},{5,13},{9,17},{1... | collective-permute-start | bytes 1572872 | tf_op jit(solution)/shard_map/ppermute | solution.py:30
  25.4 26.5 %copy-start.16 = (s32[1024]{0:T(1024)S(1)}, s32[1024]{0:T(1024)}, u32[]{:S(2)}) copy-start(s32[1024]{0:T(1024)} %param.14) | copy-start | bytes 12292
  47.7 14.1 %copy-start.1 = (bf16[128,2048]{1,0:T(8,128)(2,1)}, bf16[128,2048]{1,0:T(8,128)(2,1)S(1)}, u32[]{:S(2)}) copy-start(bf16[128,2048]{1,0:T(8,128)(2,1)S(1)} %collective-permute-done.1.k1.v1) | copy-start | bytes 1572868
  47.7 14.1 %collective-permute-start.3 = (bf16[128,2048]{1,0:T(8,128)(2,1)S(1)}, bf16[128,2048]{1,0:T(8,128)(2,1)}, u32[]{:S(2)}, u32[]{:S(2)}) collective-permute-start(bf16[128,2048]{1,0:T(8,128)(2,1)S(1)} %collective-permute-done.1.k1.v1), channel_id=1, source_target_pairs={{0,8},{4,12},{8,16},{12,20},{16,24},{20,28},{1,9},{5,13},{9,17},{1... | collective-permute-start | bytes 1572872 | tf_op jit(solution)/shard_map/ppermute | solution.py:30
  52.0 0.8 copy-start.15
  53.4 8.4 %copy-start.4 = (bf16[128,2048]{1,0:T(8,128)(2,1)}, bf16[128,2048]{1,0:T(8,128)(2,1)S(1)}, u32[]{:S(2)}) copy-start(bf16[128,2048]{1,0:T(8,128)(2,1)S(1)} %collective-permute-done.qf.do_f) | copy-start | bytes 1572868
  53.4 30.7 %collective-permute-start.6 = (bf16[128,2048]{1,0:T(8,128)(2,1)S(1)}, bf16[128,2048]{1,0:T(8,128)(2,1)}, u32[]{:S(2)}, u32[]{:S(2)}) collective-permute-start(bf16[128,2048]{1,0:T(8,128)(2,1)S(1)} %collective-permute-done.qf.do_f), channel_id=1, source_target_pairs={{8,0},{12,4},{16,8},{20,12},{24,16},{28,20},{9,1},{13,5},{17,9},{2... | collective-permute-start | bytes 1572872 | tf_op jit(solution)/shard_map/ppermute | solution.py:30
  61.9 1.0 copy-start.2
  69.6 7.9 %copy-start.13 = (f32[4,8,256]{2,1,0:T(8,128)S(1)}, f32[4,8,256]{2,1,0:T(8,128)}, u32[]{:S(2)}) copy-start(f32[4,8,256]{2,1,0:T(8,128)} %get-tuple-element.24.stat) | copy-start | bytes 98308
  76.6 23.0 %collective-permute-start.4 = (bf16[2,128,1024]{2,1,0:T(8,128)(2,1)}, bf16[2,128,1024]{2,1,0:T(8,128)(2,1)S(1)}, u32[]{:S(2)}, u32[]{:S(2)}) collective-permute-start(bf16[2,128,1024]{2,1,0:T(8,128)(2,1)} %get-tuple-element.23), channel_id=1, source_target_pairs={{0,4},{4,0},{8,12},{12,8},{16,20},{20,16},{24,28},{28,24},{1,5},{5... | collective-permute-start | bytes 1572872 | tf_op jit(solution)/shard_map/ppermute | solution.py:35
  77.5 6.6 %collective-permute-start.7 = (f32[4,8,256]{2,1,0:T(8,128)S(1)}, f32[4,8,256]{2,1,0:T(8,128)S(1)}, u32[]{:S(2)}, u32[]{:S(2)}) collective-permute-start(f32[4,8,256]{2,1,0:T(8,128)S(1)} %copy-done.13), channel_id=1, source_target_pairs={{8,0},{12,4},{16,8},{20,12},{24,16},{28,20},{9,1},{13,5},{17,9},{2... | collective-permute-start | bytes 98312 | tf_op jit(solution)/shard_map/ppermute | solution.py:30
  84.2 0.6 copy-start.14
  90.4 16.3 %collective-permute-start.8 = (bf16[2,128,1024]{2,1,0:T(8,128)(2,1)}, bf16[2,128,1024]{2,1,0:T(8,128)(2,1)S(1)}, u32[]{:S(2)}, u32[]{:S(2)}) collective-permute-start(bf16[2,128,1024]{2,1,0:T(8,128)(2,1)} %get-tuple-element.32), channel_id=1, source_target_pairs={{0,4},{4,0},{8,12},{12,8},{16,20},{20,16},{24,28},{28,24},{1,5},{5... | collective-permute-start | bytes 1572872 | tf_op jit(solution)/shard_map/ppermute | solution.py:35
  92.2 14.6 %all-to-all-start.1 = ((f32[32,1,128]{2,1,0:T(1,128)}), f32[32,1,128]{2,1,0:T(1,128)S(1)}, u32[]{:S(2)}, u32[]{:S(2)}) async-start(f32[32,1,128]{2,1,0:T(1,128)} %bitcast.41), calls=%async_computation.1 | async-start | bytes 32768 | tf_op jit(solution)/shard_map/all_to_all | solution.py:489
  99.6 1.0 copy-start.11
  99.6 1.9 %copy-start.5 = (bf16[2,128,1024]{2,1,0:T(8,128)(2,1)}, bf16[2,128,1024]{2,1,0:T(8,128)(2,1)S(1)}, u32[]{:S(2)}) copy-start(bf16[2,128,1024]{2,1,0:T(8,128)(2,1)S(1)} %collective-permute-done.4.dq_other) | copy-start | bytes 1572868
  106.7 0.6 copy-start.12
  106.7 0.8 copy-start.10

commit v2 on v1

--- a/solution.py
+++ b/solution.py
@@ -14,6 +14,7 @@
 LOG2E = 1.4426950408889634
 F32 = jnp.float32
 BF16 = jnp.bfloat16
+VMEM_BYTES = 20 * 2**20
 
 
 def dot_nt(a, b):
@@ -39,45 +40,95 @@
     return pl.CostEstimate(flops=int(flops), bytes_accessed=int(size), transcendentals=int(exps))
 
 
-def pack_memory(my_routes, memory_keys, memory_values, count):
+def staged(position, routes, query, keys, values, cotangent, memory_keys, memory_values, count):
+    rows, width = keys.shape
+    half = width // 2
     blocks = memory_keys.shape[0] // BLK
-    width = memory_keys.shape[1]
-    half = width // 2
-
-    def body(routes_ref, mk_ref, mv_ref, out_ref, used):
-        out_ref[...] = jnp.zeros_like(out_ref)
+
+    def body(
+        where, routes_ref, q, k, v, do, mk, mv, own_kv, far_kv, own_qd, far_qd, packed, used, cut_sem, block_sem
+    ):
+        side = where[0] % 2
+        kept = pl.ds(pl.multiple_of(side * half, half), half)
+        sent = pl.ds(pl.multiple_of(half - side * half, half), half)
+        left, right = pl.ds(0, half), pl.ds(half, half)
+        cuts = [
+            (k, sent, far_kv, left),
+            (v, sent, far_kv, right),
+            (k, kept, own_kv, left),
+            (v, kept, own_kv, right),
+            (q, kept, own_qd, left),
+            (do, kept, own_qd, right),
+            (q, sent, far_qd, left),
+            (do, sent, far_qd, right),
+        ]
+        copies = [
+            pltpu.make_async_copy(src.at[:, cols], dst.at[:, part], cut_sem.at[n])
+            for n, (src, cols, dst, part) in enumerate(cuts)
+        ]
+        for copy in copies:
+            copy.start()
+        packed[...] = jnp.zeros_like(packed)
         for owner in range(count):
             used[owner] = 0
 
         def place(block, carry):
-            owner = routes_ref[block]
+            owner = routes_ref[where[0] * blocks + block]
             slot = used[owner]
             used[owner] = slot + 1
-            partner = owner + 1 - 2 * (owner % 2)
-            near = pl.multiple_of((owner % 2) * half, half)
-            far = pl.multiple_of(half - (owner % 2) * half, half)
-            out_ref[owner, 0, slot, :, :half] = mk_ref[block, :, pl.ds(near, half)]
-            out_ref[owner, 0, slot, :, half:] = mv_ref[block, :, pl.ds(near, half)]
-            out_ref[partner, 1, slot, :, :half] = mk_ref[block, :, pl.ds(far, half)]
-            out_ref[partner, 1, slot, :, half:] = mv_ref[block, :, pl.ds(far, half)]
+            odd = owner % 2
+            partner = owner + 1 - 2 * odd
+            near = pl.ds(pl.multiple_of(odd * half, half), half)
+            away = pl.ds(pl.multiple_of(half - odd * half, half), half)
+            for n, (src, cols, target, who, part) in enumerate(
+                (
+                    (mk, near, owner, 0, left),
+                    (mv, near, owner, 0, right),
+                    (mk, away, partner, 1, left),
+                    (mv, away, partner, 1, right),
+                )
+            ):
+                pltpu.make_async_copy(
+                    src.at[block, :, cols], packed.at[target, who, slot, :, part], block_sem.at[block, n]
+                ).start()
             return carry
 
         lax.fori_loop(0, blocks, place, 0)
 
+        def settle(block, carry):
+            for n in range(4):
+                pltpu.make_async_copy(
+                    mk.at[block, :, left], packed.at[0, 0, 0, :, left], block_sem.at[block, n]
+                ).wait()
+            return carry
+
+        lax.fori_loop(0, blocks, settle, 0)
+        for copy in copies:
+            copy.wait()
+
+    smem = pl.BlockSpec(memory_space=pltpu.SMEM)
+    hbm = pl.BlockSpec(memory_space=pltpu.HBM)
+    flat = jax.ShapeDtypeStruct((rows, width), BF16)
     return pl.pallas_call(
         body,
-        out_shape=jax.ShapeDtypeStruct((count, 2, CAP, BLK, width), BF16),
-        in_specs=[
-            pl.BlockSpec(memory_space=pltpu.SMEM),
-            pl.BlockSpec(memory_space=pltpu.VMEM),
-            pl.BlockSpec(memory_space=pltpu.VMEM),
+        out_shape=(flat,) * 4 + (jax.ShapeDtypeStruct((count, 2, CAP, BLK, width), BF16),),
+        in_specs=[smem] * 2 + [hbm] * 6,
+        out_specs=(pl.BlockSpec(memory_space=pltpu.VMEM),) * 5,
+        scratch_shapes=[
+            pltpu.SMEM((count,), jnp.int32),
+            pltpu.SemaphoreType.DMA((8,)),
+            pltpu.SemaphoreType.DMA((blocks, 4)),
         ],
-        out_specs=pl.BlockSpec(memory_space=pltpu.VMEM),
-        scratch_shapes=[pltpu.SMEM((count,), jnp.int32)],
-        cost_estimate=cost(0, 4 * memory_keys.size * 2),
-        name="pack_memory",
+        cost_estimate=cost(0, 2 * (4 * rows + 2 * blocks * BLK) * width * 2),
+        compiler_params=pltpu.CompilerParams(vmem_limit_bytes=60 * 2**20),
+        name="staged",
     )(
-        my_routes,
+        position[None],
+        routes.reshape(-1),
+        query,
+        keys,
+        values,
+        cotangent,
         memory_keys.reshape(blocks, BLK, width),
         memory_values.reshape(blocks, BLK, width),
     )
@@ -91,7 +142,7 @@
     def __init__(self, rows, half, memory_rows):
         self.rows, self.half, self.memory_rows = rows, half, memory_rows
         self.heads = half // HDIM
-        self.group = 2 if self.heads % 2 == 0 else 1
+        self.group = math.gcd(self.heads, 4)
         self.steps = self.heads // self.group
         self.cols = self.group * HDIM
         self.scale = 1.0 / math.sqrt(HDIM)
@@ -200,16 +251,21 @@
             pl.BlockSpec((1, 8, 2 * rows), lambda i: (i, 0, 0)),
         ),
         cost_estimate=cost(flops, 12 * rows * plan.half * 2, 2 * rows * 5 * rows * plan.heads),
+        compiler_params=pltpu.CompilerParams(vmem_limit_bytes=VMEM_BYTES),
         name="attend",
     )(own_qd, far_qd, own_qd, far_qd, *kv, *kv, memory, memory, key_row, query_col, memory_bias)
 
 
-def query_gradient(plan, own_qd, far_qd, kv, memory, key_row, query_col, memory_bias, stats, att):
+def dot_tn(a, b):
+    return lax.dot_general(a, b, (((0,), (0,)), ((), ())), preferred_element_type=F32)
+
+
+def own_gradients(plan, own_qd, far_qd, kv, memory, key_row, query_col, memory_bias, stats):
     rows = plan.rows
 
     def body(
         qo, qf, do_o, do_f, k0, k1, k2, k3, v0, v1, v2, v3, mk, mv, krow, qcol, mbias,
-        stat_col, att_far, dq_own, send, squares,
+        stat_col, dq_own, dq_far, squares, dk, dv,
     ):
         bias = visible_bias(krow[0:1, :], krow[1:2, :], qcol[:, 0:1], qcol[:, 1:2])
         acc = jnp.zeros((8, HDIM), F32)
@@ -224,7 +280,8 @@
             )
             values = joined((v0, v1, v2, v3), lanes)
             press = dot_nt(upstream, values) - delta
-            grad = (jnp.exp2(current - level) * press).astype(BF16)
+            prob = jnp.exp2(current - level)
+            grad = (prob * press).astype(BF16)
             result = dot_nn(grad, keys)
             extra = []
             for part in range(2):
@@ -235,9 +292,10 @@
                 extra.append(dot_nn(mem_grad, mem_keys[part]))
             result = (result + jnp.concatenate(extra, axis=0)) * plan.scale
             dq_own[:, lanes] = result[:rows]
-            send[0, :, lanes] = result[rows:].astype(BF16)
+            dq_far[:, lanes] = result[rows:].astype(BF16)
             acc = acc + jnp.sum((result * result).reshape(-1, 8, HDIM), axis=0)
-        send[1] = att_far[...]
+            dk[:, lanes] = dot_tn(grad[:, : 2 * rows], query) * plan.scale
+            dv[:, lanes] = dot_tn(prob[:, : 2 * rows].astype(BF16), upstream)
 
         @pl.when(pl.program_id(0) == 0)
         def _():
@@ -245,14 +303,17 @@
 
         squares[...] += acc
 
-    flops = 3 * 2 * (2 * rows) * (4 * rows + plan.memory_rows) * plan.half
+    both = pl.BlockSpec((2 * rows, plan.cols), lambda i: (0, i))
+    flops = (3 * (4 * rows + plan.memory_rows) + 4 * rows) * 2 * (2 * rows) * plan.half
     return pl.pallas_call(
         body,
         grid=(plan.steps,),
         out_shape=(
             jax.ShapeDtypeStruct((rows, plan.half), F32),
-            jax.ShapeDtypeStruct((2, rows, plan.half), BF16),
+            jax.ShapeDtypeStruct((rows, plan.half), BF16),
             jax.ShapeDtypeStruct((8, HDIM), F32),
+            jax.ShapeDtypeStruct((2 * rows, plan.half), F32),
+            jax.ShapeDtypeStruct((2 * rows, plan.half), F32),
         ),
         in_specs=[plan.first()] * 2
         + [plan.second()] * 2
@@ -260,13 +321,14 @@
         + [plan.second()] * 4
         + [plan.memory(0), plan.memory(1)]
         + [plan.whole(key_row.shape), plan.whole(query_col.shape), plan.whole(memory_bias.shape)]
-        + [pl.BlockSpec((1, 2 * rows, HDIM), lambda i: (i, 0, 0)), plan.first()],
-        out_specs=(plan.first(), plan.stacked(), plan.whole((8, HDIM))),
-        cost_estimate=cost(flops, 14 * rows * plan.half * 2, 2 * rows * 5 * rows * plan.heads),
-        name="query_gradient",
+        + [pl.BlockSpec((1, 2 * rows, HDIM), lambda i: (i, 0, 0))],
+        out_specs=(plan.first(), plan.first(), plan.whole((8, HDIM)), both, both),
+        cost_estimate=cost(flops, 22 * rows * plan.half * 2, 2 * rows * 5 * rows * plan.heads),
+        compiler_params=pltpu.CompilerParams(vmem_limit_bytes=VMEM_BYTES),
+        name="own_gradients",
     )(
         own_qd, far_qd, own_qd, far_qd, *kv, *kv, memory, memory, key_row, query_col, memory_bias,
-        stats, att,
+        stats,
     )
 
 
@@ -275,45 +337,6 @@
     prob = jnp.exp2(score - level)
     grad = (prob * (dot_nt(value, upstream) - delta)).astype(BF16)
     return dot_nn(grad, query) * plan.scale, dot_nn(prob.astype(BF16), upstream)
-
-
-def key_gradient_near(plan, own_qd, far_qd, own_kv, far_kv, query_row, key_col, stats):
-    rows = plan.rows
-
-    def body(qo, qf, do_o, do_f, k0, k1, v0, v1, qrow, kcol, stat, dk, dv):
-        bias = visible_bias(kcol[:, 0:1], kcol[:, 1:2], qrow[0:1, :], qrow[1:2, :])
-        for g in range(plan.group):
-            lanes = slice(g * HDIM, (g + 1) * HDIM)
-            key_part, value_part = key_terms(
-                plan,
-                joined((k0, k1), lanes),
-                joined((v0, v1), lanes),
-                joined((qo, qf), lanes),
-                joined((do_o, do_f), lanes),
-                bias,
-                stat[0, g : g + 1, :],
-                stat[0, plan.group + g : plan.group + g + 1, :],
-            )
-            dk[:, lanes] = key_part
-            dv[:, lanes] = value_part
-
-    both = pl.BlockSpec((2 * rows, plan.cols), lambda i: (0, i))
-    return pl.pallas_call(
-        body,
-        grid=(plan.steps,),
-        out_shape=(jax.ShapeDtypeStruct((2 * rows, plan.half), F32),) * 2,
-        in_specs=[plan.first()] * 2
-        + [plan.second()] * 2
-        + [plan.first()] * 2
-        + [plan.second()] * 2
-        + [plan.whole(query_row.shape), plan.whole(key_col.shape)]
-        + [pl.BlockSpec((1, 8, 2 * rows), lambda i: (i, 0, 0))],
-        out_specs=(both, both),
-        cost_estimate=cost(
-            4 * 2 * (2 * rows) ** 2 * plan.half, 16 * rows * plan.half * 2, 4 * rows * rows * plan.heads
-        ),
-        name="key_gradient_near",
-    )(own_qd, far_qd, own_qd, far_qd, own_kv, far_kv, own_kv, far_kv, query_row, key_col, stats)
 
 
 def key_gradient_next(
@@ -381,6 +404,7 @@
         cost_estimate=cost(
             4 * 2 * (2 * rows) ** 2 * plan.half, 24 * rows * plan.half * 2, 4 * rows * rows * plan.heads
         ),
+        compiler_params=pltpu.CompilerParams(vmem_limit_bytes=VMEM_BYTES),
         name="key_gradient_next",
     )(
         own_qd, far_qd, own_qd, far_qd, own_kv, far_kv, own_kv, far_kv, query_row, key_col, stats,
@@ -397,7 +421,7 @@
         near = pl.multiple_of(side_ref[0] * half, half)
         away = pl.multiple_of(half - side_ref[0] * half, half)
         for out, mine, theirs in (
-            (dq_out, dq[...], dq_other[0]),
+            (dq_out, dq[...], dq_other[...]),
             (dk_out, dk[...], other[0]),
             (dv_out, dv[...], other[1]),
         ):
@@ -411,6 +435,7 @@
         in_specs=[pl.BlockSpec(memory_space=pltpu.SMEM)] + [vmem] * 6,
         out_specs=(vmem,) * 3,
         cost_estimate=cost(6 * rows * half, 20 * rows * half),
+        compiler_params=pltpu.CompilerParams(vmem_limit_bytes=VMEM_BYTES),
         name="scaled",
     )(side, shares, dq_own, dq_far, dk_own, dv_own, kv_far)
 
@@ -427,29 +452,19 @@
     memory_rows = count * CAP * BLK
     plan = Plan(rows, half, memory_rows)
 
-    def halves(left, right, which):
-        start = which * half
-        return jnp.concatenate(
-            [
-                lax.dynamic_slice(left, (0, start), (rows, half)),
-                lax.dynamic_slice(right, (0, start), (rows, half)),
-            ],
-            axis=1,
-        )
-
-    own_kv = halves(keys, values, side)
-    own_qd = halves(query, cotangent, side)
-    far_kv = swapped(halves(keys, values, 1 - side))
-    far_qd = swapped(halves(query, cotangent, 1 - side))
+    own_kv, sent_kv, own_qd, sent_qd, packed = staged(
+        position, routes, query, keys, values, cotangent, memory_keys, memory_values, count
+    )
+    far_kv = swapped(sent_kv)
+    prev_own_kv = shifted(own_kv, 2)
+    next_own_qd = shifted(own_qd, -2)
+    far_kv, sent_qd = lax.optimization_barrier((far_kv, sent_qd))
+    prev_far_kv = shifted(far_kv, 2)
+    far_qd = swapped(sent_qd)
     route_table = routes[:, 0].reshape(count, per_device)
-    my_routes = lax.dynamic_slice_in_dim(routes[:, 0], position * per_device, per_device)
-    packed = pack_memory(my_routes, memory_keys, memory_values, count)
     arrived = lax.all_to_all(
         packed.reshape(count, 2 * CAP * BLK, width), "ctx", split_axis=0, concat_axis=0, tiled=True
     ).reshape(count, 2, CAP * BLK, width)
-    prev_own_kv = shifted(own_kv, 2)
-    prev_far_kv = shifted(far_kv, 2)
-    next_own_qd = shifted(own_qd, -2)
     next_far_qd = shifted(far_qd, -2)
 
     def labels(block):
@@ -474,24 +489,23 @@
         plan, own_qd, far_qd, kv, arrived, key_row, near_col, memory_bias
     )
     next_stats = shifted(stat_row, -2)
-    dq_own, first_send, dq_squares = query_gradient(
-        plan, own_qd, far_qd, kv, arrived, key_row, near_col, memory_bias, stat_col, att_far
-    )
-    first_back = swapped(first_send)
-    near_dk, near_dv = key_gradient_near(
-        plan, own_qd, far_qd, own_kv, far_kv, near_row, near_col, stat_row
-    )
+    att_back = swapped(att_far)
+    dq_own, dq_far, dq_squares, near_dk, near_dv = own_gradients(
+        plan, own_qd, far_qd, kv, arrived, key_row, near_col, memory_bias, stat_col
+    )
+    next_stats, dq_far, att_back = lax.optimization_barrier((next_stats, dq_far, att_back))
+    dq_back = swapped(dq_far)
     dk_own, dv_own, second_send, share = key_gradient_next(
         plan, next_own_qd, next_far_qd, own_kv, far_kv, next_row, near_col, next_stats,
         near_dk, near_dv, dq_squares, devices,
     )
+    second_send, dq_back = lax.optimization_barrier((second_send, dq_back))
     second_back = swapped(second_send)
     shares = lax.all_to_all(share, ("ctx", "head"), split_axis=0, concat_axis=0, tiled=True)
     entries = 3.0 * count * rows * width * lax.axis_size("head")
     query_grad, key_grad, value_grad = scaled(
-        plan, side[None], shares, entries, dq_own, first_back, dk_own, dv_own, second_back
-    )
-    att_back = first_back[1]
+        plan, side[None], shares, entries, dq_own, dq_back, dk_own, dv_own, second_back
+    )
     attended = jnp.where(
         side == 0,
         jnp.concatenate([att_own, att_back], axis=1),

time: 111 us -> 97.9 us (0.88)
  Pallas kernels: 30 us -> 21.2 us
  local copies, waits for them, and re-layouts: 7.12 us -> 2.53 us
  other arithmetic: 5.01 us -> 3.17 us
  starting transfers between devices: 32.9 us -> 34.7 us
    ppermute x4 -> x5, waiting for transfers between devices: 22.4 us -> 29.6 us  [swapped(): return lax.ppermute(value, 'ctx', [(i, i ^ 1) for i in range(count)])]
    ppermute x5, waiting for transfers between devices: 7.12 us -> 0.17 us  [shifted(): return lax.ppermute(value, 'ctx', pairs)]
    pallas_call x3 -> x2, Pallas kernels: 14.6 us -> 10.4 us  [the longest x1 5.89 us: own_gradients(): pl.pallas_call(body, grid=(plan.steps,), out_shape=(jax.ShapeDtypeStruct(...]
    all_to_all x1, starting transfers between devices: 7.4 us -> 11 us  [on_device(): lax.all_to_all(share, ('ctx', 'head'), split_axis=0, concat_axis=0, tiled...]
    unnamed x37 -> x15, local copies, waits for them, and re-layouts: 4.66 us -> 2.12 us
    ppermute x5, starting transfers between devices: 13.4 us -> 11.4 us  [shifted(): return lax.ppermute(value, 'ctx', pairs)]
    concatenate x4 -> x0, other arithmetic: 1.73 us -> none  [halves(): jnp.concatenate([lax.dynamic_slice(left, (0, start), (rows, half)), lax.d...]
    pallas_call x1, Pallas kernels: 3.04 us -> 1.35 us  [scaled(): pl.pallas_call(body, out_shape=(jax.ShapeDtypeStruct((rows, 2 * half), BF...]
  transfers between devices with their start and end apart: 11 -> 12, of which waited for: 3 -> 5; matrix products, arithmetic and copies ran while one was open for 7% -> 4% of each run, Pallas kernels for 22% -> 16%
where the time goes in v2:
time: 97.9 us; the launch traced here: 97.4 us
  waiting for transfers between devices  34.9 us (36%)
  starting transfers between devices  34.7 us (35%)
  Pallas kernels  21.2 us (22%)
  other arithmetic  3.17 us (3%)
  local copies, waits for them, and re-layouts  2.53 us (3%)
    ppermute x5, waiting for transfers between devices, swapped(): return lax.ppermute(value, 'ctx', [(i, i ^ 1) for i in range(count)])  29.6 us
    ppermute x5, starting transfers between devices, shifted(): return lax.ppermute(value, 'ctx', pairs)  11.4 us
    all_to_all x1, starting transfers between devices, on_device(): lax.all_to_all(share, ('ctx', 'head'), split_axis=0, concat_axis=0, tiled...  11 us
    all_to_all x1, starting transfers between devices, on_device(): lax.all_to_all(packed.reshape(count, 2 * CAP * BLK, width), 'ctx', split_...  7.42 us
    pallas_call x1, Pallas kernels, own_gradients(): pl.pallas_call(body, grid=(plan.steps,), out_shape=(jax.ShapeDtypeStruct(...  5.89 us
    pallas_call x1, Pallas kernels, forward(): pl.pallas_call(body, grid=(plan.steps,), out_shape=(jax.ShapeDtypeStruct(...  5.36 us
    all_to_all x1, waiting for transfers between devices, on_device(): lax.all_to_all(share, ('ctx', 'head'), split_axis=0, concat_axis=0, tiled...  5.13 us
    ppermute x5, starting transfers between devices, swapped(): return lax.ppermute(value, 'ctx', [(i, i ^ 1) for i in range(count)])  4.9 us
  transfers between devices with their start and end apart: 12, of which 5 were waited for; matrix products, arithmetic and copies ran while one was open for 4% of the time, Pallas kernels for 16%

profile of v2, /device:TPU:0, one launch (start us, length us, event | category | flops | bytes accessed | tf_op | source)
XLA Modules:
  0.0 97.4 jit_solution(15167714761024957286)
XLA Ops:
  0.6 4.5 %staged.1 = (bf16[128,2048]{1,0:T(8,128)(2,1)}, bf16[128,2048]{1,0:T(8,128)(2,1)}, bf16[128,2048]{1,0:T(8,128)(2,1)}, bf16[128,2048]{1,0:T(8,128)(2,1)}, bf16[8,2,2,8,2048]{4,3,2,1,0:T(8,128)(2,1)}) custom-call(s32[1]{0:T(128)} %bitcast.where, s32[96]{0:T(128)} %bitcast.37, bf16[128,2048]{1,0:T(8,128)(2,1)} %q.1, bf16[128,2048]{1,0:T(8,128)(2,1)} %k.1, ...), custom_call_target="tpu_custom_call" | custom-call | bytes 5767168 | tf_op jit(solution)/shard_map/staged/pallas_call | solution.py:112
  5.2 0.0 copy-start
  5.2 0.0 copy-start.1
  5.2 7.4 %all-to-all-start = ((bf16[8,32,2048]{2,1,0:T(8,128)(2,1)}), bf16[8,32,2048]{2,1,0:T(8,128)(2,1)S(1)}, u32[]{:S(2)}, u32[]{:S(2)}) async-start(bf16[8,32,2048]{2,1,0:T(8,128)(2,1)} %bitcast.34), calls=%async_computation | async-start | bytes 2097152 | tf_op jit(solution)/shard_map/all_to_all | solution.py:465
  12.6 2.0 %collective-permute-start = (bf16[128,2048]{1,0:T(8,128)(2,1)}, bf16[128,2048]{1,0:T(8,128)(2,1)S(1)}, u32[]{:S(2)}, u32[]{:S(2)}) collective-permute-start(bf16[128,2048]{1,0:T(8,128)(2,1)} %get-tuple-element.33), channel_id=1, source_target_pairs={{0,4},{4,0},{8,12},{12,8},{16,20},{20,16},{24,28},{28,24},{1,5},{5... | collective-permute-start | bytes 1572872 | tf_op jit(solution)/shard_map/ppermute | solution.py:36
  14.6 0.0 copy-done
  14.7 3.4 %collective-permute-start.2 = (bf16[128,2048]{1,0:T(8,128)(2,1)S(1)}, bf16[128,2048]{1,0:T(8,128)(2,1)S(1)}, u32[]{:S(2)}, u32[]{:S(2)}) collective-permute-start(bf16[128,2048]{1,0:T(8,128)(2,1)S(1)} %copy-done), channel_id=1, source_target_pairs={{0,8},{4,12},{8,16},{12,20},{16,24},{20,28},{1,9},{5,13},{9,17},{1... | collective-permute-start | bytes 1572872 | tf_op jit(solution)/shard_map/ppermute | solution.py:31
  18.0 0.0 copy-done.1
  18.1 1.3 %collective-permute-start.6 = (bf16[128,2048]{1,0:T(8,128)(2,1)S(1)}, bf16[128,2048]{1,0:T(8,128)(2,1)}, u32[]{:S(2)}, u32[]{:S(2)}) collective-permute-start(bf16[128,2048]{1,0:T(8,128)(2,1)S(1)} %copy-done.1), channel_id=1, source_target_pairs={{8,0},{12,4},{16,8},{20,12},{24,16},{28,20},{9,1},{13,5},{17,9},{2... | collective-permute-start | bytes 1572872 | tf_op jit(solution)/shard_map/ppermute | solution.py:31
  19.4 0.0 copy-start.5
  19.5 0.7 copy-done.5
  20.1 0.1 fusion.5
  20.2 0.1 copy.20
  20.4 0.0 copy-start.6
  20.4 0.5 broadcast.61
  20.9 0.1 copy-done.6
  21.0 0.7 reduce.3
  21.7 0.1 eq.21
  21.8 0.1 pad_add_fusion
  21.8 15.6 %collective-permute-done.k1.v1 = bf16[128,2048]{1,0:T(8,128)(2,1)S(1)} collective-permute-done((bf16[128,2048]{1,0:T(8,128)(2,1)}, bf16[128,2048]{1,0:T(8,128)(2,1)S(1)}, u32[]{:S(2)}, u32[]{:S(2)}) %collective-permute-start) | collective-permute-done | bytes 524320 | tf_op jit(solution)/shard_map/ppermute | solution.py:36
  37.4 4.2 %collective-permute-start.3 = (bf16[128,2048]{1,0:T(8,128)(2,1)S(1)}, bf16[128,2048]{1,0:T(8,128)(2,1)}, u32[]{:S(2)}, u32[]{:S(2)}) collective-permute-start(bf16[128,2048]{1,0:T(8,128)(2,1)S(1)} %collective-permute-done.k1.v1), channel_id=1, source_target_pairs={{0,8},{4,12},{8,16},{12,20},{16,24},{20,28},{1,9},{5,13},{9,17},{1... | collective-permute-start | bytes 1572872 | tf_op jit(solution)/shard_map/ppermute | solution.py:31
  41.6 0.6 collective-permute-start.1
  42.2 0.2 convert_reduce_fusion
  42.4 0.1 fusion
  42.4 0.1 broadcast_in_dim.36
  42.5 0.1 reshape.82.mbias
  42.7 10.8 %collective-permute-done.1.qf.do_f = bf16[128,2048]{1,0:T(8,128)(2,1)} collective-permute-done((bf16[128,2048]{1,0:T(8,128)(2,1)}, bf16[128,2048]{1,0:T(8,128)(2,1)}, u32[]{:S(2)}, u32[]{:S(2)}) %collective-permute-start.1) | collective-permute-done | bytes 524320 | tf_op jit(solution)/shard_map/ppermute | solution.py:36
  53.5 1.3 %collective-permute-start.7 = (bf16[128,2048]{1,0:T(8,128)(2,1)}, bf16[128,2048]{1,0:T(8,128)(2,1)}, u32[]{:S(2)}, u32[]{:S(2)}) collective-permute-start(bf16[128,2048]{1,0:T(8,128)(2,1)} %collective-permute-done.1.qf.do_f), channel_id=1, source_target_pairs={{8,0},{12,4},{16,8},{20,12},{24,16},{28,20},{9,1},{13,5},{17,9},{2... | collective-permute-start | bytes 1572872 | tf_op jit(solution)/shard_map/ppermute | solution.py:31
  54.8 0.0 collective-permute-done.2.k2.v2
  54.8 0.0 collective-permute-done.3.k3.v3
  54.8 0.0 all-to-all-done
  54.8 5.4 %attend.1 = (bf16[128,1024]{1,0:T(8,128)(2,1)S(1)}, bf16[128,1024]{1,0:T(8,128)(2,1)S(1)}, f32[2,256,128]{2,1,0:T(8,128)S(1)}, f32[2,8,256]{2,1,0:T(8,128)S(1)}) custom-call(bf16[128,2048]{1,0:T(8,128)(2,1)S(1)} %copy-done.1, bf16[128,2048]{1,0:T(8,128)(2,1)} %collective-permute-done.1.qf.do_f, bf16[128,2048]{1,0:T(8,128)(2,1)S(1)} %copy-done.1, ...), custom_call_target="tpu_custom_call" | custom-call | flops 671088640 | bytes 3145728 | tf_op jit(solution)/shard_map/attend/pallas_call | solution.py:232
  60.2 1.7 %collective-permute-start.5 = (bf16[128,1024]{1,0:T(8,128)(2,1)S(1)}, bf16[128,1024]{1,0:T(8,128)(2,1)S(1)}, u32[]{:S(2)}, u32[]{:S(2)}) collective-permute-start(bf16[128,1024]{1,0:T(8,128)(2,1)S(1)} %get-tuple-element.43), channel_id=1, source_target_pairs={{0,4},{4,0},{8,12},{12,8},{16,20},{20,16},{24,28},{28,24},{1,5},{5... | collective-permute-start | bytes 786440 | tf_op jit(solution)/shard_map/ppermute | solution.py:36
  61.8 1.3 %collective-permute-start.4 = (f32[2,8,256]{2,1,0:T(8,128)S(1)}, f32[2,8,256]{2,1,0:T(8,128)S(1)}, u32[]{:S(2)}, u32[]{:S(2)}) collective-permute-start(f32[2,8,256]{2,1,0:T(8,128)S(1)} %get-tuple-element.40), channel_id=1, source_target_pairs={{8,0},{12,4},{16,8},{20,12},{24,16},{28,20},{9,1},{13,5},{17,9},{2... | collective-permute-start | bytes 49160 | tf_op jit(solution)/shard_map/ppermute | solution.py:31
  63.1 5.9 %own_gradients.1 = (f32[128,1024]{1,0:T(8,128)S(1)}, bf16[128,1024]{1,0:T(8,128)(2,1)S(1)}, f32[8,128]{1,0:T(8,128)S(1)}, f32[256,1024]{1,0:T(8,128)S(1)}, f32[256,1024]{1,0:T(8,128)S(1)}) custom-call(bf16[128,2048]{1,0:T(8,128)(2,1)S(1)} %copy-done.1, bf16[128,2048]{1,0:T(8,128)(2,1)} %collective-permute-done.1.qf.do_f, bf16[128,2048]{1,0:T(8,128)(2,1)S(1)} %copy-done.1, ...), custom_call_target="tpu_custom_call" | custom-call | flops 1275068416 | bytes 5767168 | tf_op jit(solution)/shard_map/own_gradients/pallas_call | solution.py:308
  69.0 0.0 copy-start.2
  69.0 0.8 copy-done.2
  69.8 0.2 collective-permute-done.4.stat
  70.0 0.0 collective-permute-done.5
  70.0 0.0 copy-start.4
  70.0 0.4 collective-permute-start.8
  70.4 0.0 collective-permute-done.6.qo.do_o
  70.4 0.0 collective-permute-done.7.qf.do_f
  70.4 4.1 %key_gradient_next.1 = (f32[128,1024]{1,0:T(8,128)S(1)}, f32[128,1024]{1,0:T(8,128)S(1)}, bf16[2,128,1024]{2,1,0:T(8,128)(2,1)}, f32[32,128]{1,0:T(8,128)}) custom-call(bf16[128,2048]{1,0:T(8,128)(2,1)} %collective-permute-done.6.qo.do_o, bf16[128,2048]{1,0:T(8,128)(2,1)} %collective-permute-done.7.qf.do_f, ...), custom_call_target="tpu_custom_call" | custom-call | flops 536870912 | bytes 6291456 | tf_op jit(solution)/shard_map/key_gradient_next/pallas_call | solution.py:386
  74.5 0.0 copy-done.4
  74.5 3.2 %collective-permute-done.8.dq_other = bf16[128,1024]{1,0:T(8,128)(2,1)S(1)} collective-permute-done((bf16[128,1024]{1,0:T(8,128)(2,1)S(1)}, bf16[128,1024]{1,0:T(8,128)(2,1)S(1)}, u32[]{:S(2)}, u32[]{:S(2)}) %collective-permute-start.8) | collective-permute-done | bytes 262176 | tf_op jit(solution)/shard_map/ppermute | solution.py:36
  77.7 0.3 collective-permute-start.9
  78.0 11.0 %all-to-all-start.1 = ((f32[32,1,128]{2,1,0:T(1,128)}), f32[32,1,128]{2,1,0:T(1,128)S(1)}, u32[]{:S(2)}, u32[]{:S(2)}) async-start(f32[32,1,128]{2,1,0:T(1,128)} %bitcast.16), calls=%async_computation.1 | async-start | bytes 32768 | tf_op jit(solution)/shard_map/all_to_all | solution.py:504
  88.9 0.0 copy-start.3
  89.0 2.0 %maximum_select_fusion = bf16[128,2048]{1,0:T(8,128)(2,1)} fusion(bf16[128,1024]{1,0:T(8,128)(2,1)} %copy-done.4, bf16[128,1024]{1,0:T(8,128)(2,1)S(1)} %get-tuple-element.39, pred[]{:T(512)S(6)} %eq.20), kind=kLoop, calls=%fused_computation | loop fusion | flops 2359296 | bytes 1048577 | tf_op jit(solution)/shard_map/jit(_where)/select_n | solution.py:509
  91.0 5.1 %all-to-all-done.1 = f32[32,1,128]{2,1,0:T(1,128)S(1)} async-done(((f32[32,1,128]{2,1,0:T(1,128)}), f32[32,1,128]{2,1,0:T(1,128)S(1)}, u32[]{:S(2)}, u32[]{:S(2)}) %all-to-all-start.1) | async-done | bytes 16416 | tf_op jit(solution)/shard_map/all_to_all | solution.py:504
  96.1 0.0 collective-permute-done.9.other
  96.1 0.0 copy-done.3
  96.1 1.4 %scaled.1 = (bf16[128,2048]{1,0:T(8,128)(2,1)}, bf16[128,2048]{1,0:T(8,128)(2,1)}, bf16[128,2048]{1,0:T(8,128)(2,1)}) custom-call(s32[1]{0:T(128)} %bitcast.12.side_ref, f32[32,128]{1,0:T(8,128)S(1)} %bitcast.33, f32[128,1024]{1,0:T(8,128)S(1)} %copy-done.3, bf16[128,1024]{1,0:T(8,128)(2,1)S(1)} %collective-permute-done.8.dq_other, ...), custom_call_target="tpu_custom_call" | custom-call | flops 786432 | bytes 2621440 | tf_op jit(solution)/shard_map/scaled/pallas_call | solution.py:432
  (7 shorter events, 0.1 us)
Async XLA Ops:
  5.2 9.5 %copy-start = (bf16[128,2048]{1,0:T(8,128)(2,1)S(1)}, bf16[128,2048]{1,0:T(8,128)(2,1)}, u32[]{:S(2)}) copy-start(bf16[128,2048]{1,0:T(8,128)(2,1)} %get-tuple-element.36.k0.v0) | copy-start | bytes 1572868
  5.2 12.9 %copy-start.1 = (bf16[128,2048]{1,0:T(8,128)(2,1)S(1)}, bf16[128,2048]{1,0:T(8,128)(2,1)}, u32[]{:S(2)}) copy-start(bf16[128,2048]{1,0:T(8,128)(2,1)} %get-tuple-element.32.qo.do_o) | copy-start | bytes 1572868
  5.2 49.6 %all-to-all-start = ((bf16[8,32,2048]{2,1,0:T(8,128)(2,1)}), bf16[8,32,2048]{2,1,0:T(8,128)(2,1)S(1)}, u32[]{:S(2)}, u32[]{:S(2)}) async-start(bf16[8,32,2048]{2,1,0:T(8,128)(2,1)} %bitcast.34), calls=%async_computation | async-start | bytes 2097152 | tf_op jit(solution)/shard_map/all_to_all | solution.py:465
  12.6 24.8 %collective-permute-start = (bf16[128,2048]{1,0:T(8,128)(2,1)}, bf16[128,2048]{1,0:T(8,128)(2,1)S(1)}, u32[]{:S(2)}, u32[]{:S(2)}) collective-permute-start(bf16[128,2048]{1,0:T(8,128)(2,1)} %get-tuple-element.33), channel_id=1, source_target_pairs={{0,4},{4,0},{8,12},{12,8},{16,20},{20,16},{24,28},{28,24},{1,5},{5... | collective-permute-start | bytes 1572872 | tf_op jit(solution)/shard_map/ppermute | solution.py:36
  14.7 40.1 %collective-permute-start.2 = (bf16[128,2048]{1,0:T(8,128)(2,1)S(1)}, bf16[128,2048]{1,0:T(8,128)(2,1)S(1)}, u32[]{:S(2)}, u32[]{:S(2)}) collective-permute-start(bf16[128,2048]{1,0:T(8,128)(2,1)S(1)} %copy-done), channel_id=1, source_target_pairs={{0,8},{4,12},{8,16},{12,20},{16,24},{20,28},{1,9},{5,13},{9,17},{1... | collective-permute-start | bytes 1572872 | tf_op jit(solution)/shard_map/ppermute | solution.py:31
  18.1 52.3 %collective-permute-start.6 = (bf16[128,2048]{1,0:T(8,128)(2,1)S(1)}, bf16[128,2048]{1,0:T(8,128)(2,1)}, u32[]{:S(2)}, u32[]{:S(2)}) collective-permute-start(bf16[128,2048]{1,0:T(8,128)(2,1)S(1)} %copy-done.1), channel_id=1, source_target_pairs={{8,0},{12,4},{16,8},{20,12},{24,16},{28,20},{9,1},{13,5},{17,9},{2... | collective-permute-start | bytes 1572872 | tf_op jit(solution)/shard_map/ppermute | solution.py:31
  19.4 0.7 copy-start.5
  20.4 0.7 copy-start.6
  37.4 17.3 %collective-permute-start.3 = (bf16[128,2048]{1,0:T(8,128)(2,1)S(1)}, bf16[128,2048]{1,0:T(8,128)(2,1)}, u32[]{:S(2)}, u32[]{:S(2)}) collective-permute-start(bf16[128,2048]{1,0:T(8,128)(2,1)S(1)} %collective-permute-done.k1.v1), channel_id=1, source_target_pairs={{0,8},{4,12},{8,16},{12,20},{16,24},{20,28},{1,9},{5,13},{9,17},{1... | collective-permute-start | bytes 1572872 | tf_op jit(solution)/shard_map/ppermute | solution.py:31
  41.6 11.9 %collective-permute-start.1 = (bf16[128,2048]{1,0:T(8,128)(2,1)}, bf16[128,2048]{1,0:T(8,128)(2,1)}, u32[]{:S(2)}, u32[]{:S(2)}) collective-permute-start(bf16[128,2048]{1,0:T(8,128)(2,1)} %get-tuple-element.35), channel_id=1, source_target_pairs={{0,4},{4,0},{8,12},{12,8},{16,20},{20,16},{24,28},{28,24},{1,5},{5... | collective-permute-start | bytes 1572872 | tf_op jit(solution)/shard_map/ppermute | solution.py:36
  53.5 16.9 %collective-permute-start.7 = (bf16[128,2048]{1,0:T(8,128)(2,1)}, bf16[128,2048]{1,0:T(8,128)(2,1)}, u32[]{:S(2)}, u32[]{:S(2)}) collective-permute-start(bf16[128,2048]{1,0:T(8,128)(2,1)} %collective-permute-done.1.qf.do_f), channel_id=1, source_target_pairs={{8,0},{12,4},{16,8},{20,12},{24,16},{28,20},{9,1},{13,5},{17,9},{2... | collective-permute-start | bytes 1572872 | tf_op jit(solution)/shard_map/ppermute | solution.py:31
  60.2 9.8 %collective-permute-start.5 = (bf16[128,1024]{1,0:T(8,128)(2,1)S(1)}, bf16[128,1024]{1,0:T(8,128)(2,1)S(1)}, u32[]{:S(2)}, u32[]{:S(2)}) collective-permute-start(bf16[128,1024]{1,0:T(8,128)(2,1)S(1)} %get-tuple-element.43), channel_id=1, source_target_pairs={{0,4},{4,0},{8,12},{12,8},{16,20},{20,16},{24,28},{28,24},{1,5},{5... | collective-permute-start | bytes 786440 | tf_op jit(solution)/shard_map/ppermute | solution.py:36
  61.8 8.1 %collective-permute-start.4 = (f32[2,8,256]{2,1,0:T(8,128)S(1)}, f32[2,8,256]{2,1,0:T(8,128)S(1)}, u32[]{:S(2)}, u32[]{:S(2)}) collective-permute-start(f32[2,8,256]{2,1,0:T(8,128)S(1)} %get-tuple-element.40), channel_id=1, source_target_pairs={{8,0},{12,4},{16,8},{20,12},{24,16},{28,20},{9,1},{13,5},{17,9},{2... | collective-permute-start | bytes 49160 | tf_op jit(solution)/shard_map/ppermute | solution.py:31
  69.0 0.8 copy-start.2
  70.0 4.5 %copy-start.4 = (bf16[128,1024]{1,0:T(8,128)(2,1)}, bf16[128,1024]{1,0:T(8,128)(2,1)S(1)}, u32[]{:S(2)}) copy-start(bf16[128,1024]{1,0:T(8,128)(2,1)S(1)} %collective-permute-done.5) | copy-start | bytes 786436
  70.0 7.7 %collective-permute-start.8 = (bf16[128,1024]{1,0:T(8,128)(2,1)S(1)}, bf16[128,1024]{1,0:T(8,128)(2,1)S(1)}, u32[]{:S(2)}, u32[]{:S(2)}) collective-permute-start(bf16[128,1024]{1,0:T(8,128)(2,1)S(1)} %get-tuple-element.52), channel_id=1, source_target_pairs={{0,4},{4,0},{8,12},{12,8},{16,20},{20,16},{24,28},{28,24},{1,5},{5... | collective-permute-start | bytes 786440 | tf_op jit(solution)/shard_map/ppermute | solution.py:36
  77.7 18.4 %collective-permute-start.9 = (bf16[2,128,1024]{2,1,0:T(8,128)(2,1)}, bf16[2,128,1024]{2,1,0:T(8,128)(2,1)S(1)}, u32[]{:S(2)}, u32[]{:S(2)}) collective-permute-start(bf16[2,128,1024]{2,1,0:T(8,128)(2,1)} %get-tuple-element.56), channel_id=1, source_target_pairs={{0,4},{4,0},{8,12},{12,8},{16,20},{20,16},{24,28},{28,24},{1,5},{5... | collective-permute-start | bytes 1572872 | tf_op jit(solution)/shard_map/ppermute | solution.py:36
  78.0 18.1 %all-to-all-start.1 = ((f32[32,1,128]{2,1,0:T(1,128)}), f32[32,1,128]{2,1,0:T(1,128)S(1)}, u32[]{:S(2)}, u32[]{:S(2)}) async-start(f32[32,1,128]{2,1,0:T(1,128)} %bitcast.16), calls=%async_computation.1 | async-start | bytes 32768 | tf_op jit(solution)/shard_map/all_to_all | solution.py:504
  88.9 7.2 %copy-start.3 = (f32[128,1024]{1,0:T(8,128)S(1)}, f32[128,1024]{1,0:T(8,128)}, u32[]{:S(2)}) copy-start(f32[128,1024]{1,0:T(8,128)} %copy-done.2) | copy-start | bytes 1572868

commit v3 on v2

--- a/solution.py
+++ b/solution.py
@@ -40,34 +40,45 @@
     return pl.CostEstimate(flops=int(flops), bytes_accessed=int(size), transcendentals=int(exps))
 
 
-def staged(position, routes, query, keys, values, cotangent, memory_keys, memory_values, count):
-    rows, width = keys.shape
+def halves(position, left, right):
+    rows, width = left.shape
     half = width // 2
-    blocks = memory_keys.shape[0] // BLK
-
-    def body(
-        where, routes_ref, q, k, v, do, mk, mv, own_kv, far_kv, own_qd, far_qd, packed, used, cut_sem, block_sem
-    ):
+
+    def body(where, one, two, kept, sent, sems):
         side = where[0] % 2
-        kept = pl.ds(pl.multiple_of(side * half, half), half)
-        sent = pl.ds(pl.multiple_of(half - side * half, half), half)
-        left, right = pl.ds(0, half), pl.ds(half, half)
-        cuts = [
-            (k, sent, far_kv, left),
-            (v, sent, far_kv, right),
-            (k, kept, own_kv, left),
-            (v, kept, own_kv, right),
-            (q, kept, own_qd, left),
-            (do, kept, own_qd, right),
-            (q, sent, far_qd, left),
-            (do, sent, far_qd, right),
-        ]
-        copies = [
-            pltpu.make_async_copy(src.at[:, cols], dst.at[:, part], cut_sem.at[n])
-            for n, (src, cols, dst, part) in enumerate(cuts)
-        ]
+        near = pl.ds(pl.multiple_of(side * half, half), half)
+        away = pl.ds(pl.multiple_of(half - side * half, half), half)
+        cuts = [(away, sent), (near, kept)]
+        copies = []
+        for n, (cols, out) in enumerate(cuts):
+            for m, src in enumerate((one, two)):
+                dst = out.at[:, pl.ds(m * half, half)]
+                copies.append(pltpu.make_async_copy(src.at[:, cols], dst, sems.at[n, m]))
         for copy in copies:
             copy.start()
+        for copy in copies:
+            copy.wait()
+
+    hbm = pl.BlockSpec(memory_space=pltpu.HBM)
+    return pl.pallas_call(
+        body,
+        out_shape=(jax.ShapeDtypeStruct((rows, width), BF16),) * 2,
+        in_specs=[pl.BlockSpec(memory_space=pltpu.SMEM), hbm, hbm],
+        out_specs=(pl.BlockSpec(memory_space=pltpu.VMEM),) * 2,
+        scratch_shapes=[pltpu.SemaphoreType.DMA((2, 2))],
+        cost_estimate=cost(0, 4 * rows * width * 2),
+        compiler_params=pltpu.CompilerParams(vmem_limit_bytes=60 * 2**20),
+        name="halves",
+    )(position[None], left, right)
+
+
+def pack_memory(position, routes, memory_keys, memory_values, count):
+    blocks = memory_keys.shape[0] // BLK
+    width = memory_keys.shape[1]
+    half = width // 2
+
+    def body(where, routes_ref, mk, mv, packed, used, sems):
+        left, right = pl.ds(0, half), pl.ds(half, half)
         packed[...] = jnp.zeros_like(packed)
         for owner in range(count):
             used[owner] = 0
@@ -89,7 +100,7 @@
                 )
             ):
                 pltpu.make_async_copy(
-                    src.at[block, :, cols], packed.at[target, who, slot, :, part], block_sem.at[block, n]
+                    src.at[block, :, cols], packed.at[target, who, slot, :, part], sems.at[block, n]
                 ).start()
             return carry
 
@@ -98,37 +109,26 @@
         def settle(block, carry):
             for n in range(4):
                 pltpu.make_async_copy(
-                    mk.at[block, :, left], packed.at[0, 0, 0, :, left], block_sem.at[block, n]
+                    mk.at[block, :, left], packed.at[0, 0, 0, :, left], sems.at[block, n]
                 ).wait()
             return carry
 
         lax.fori_loop(0, blocks, settle, 0)
-        for copy in copies:
-            copy.wait()
 
     smem = pl.BlockSpec(memory_space=pltpu.SMEM)
     hbm = pl.BlockSpec(memory_space=pltpu.HBM)
-    flat = jax.ShapeDtypeStruct((rows, width), BF16)
-    return pl.pallas_call(
-        body,
-        out_shape=(flat,) * 4 + (jax.ShapeDtypeStruct((count, 2, CAP, BLK, width), BF16),),
-        in_specs=[smem] * 2 + [hbm] * 6,
-        out_specs=(pl.BlockSpec(memory_space=pltpu.VMEM),) * 5,
-        scratch_shapes=[
-            pltpu.SMEM((count,), jnp.int32),
-            pltpu.SemaphoreType.DMA((8,)),
-            pltpu.SemaphoreType.DMA((blocks, 4)),
-        ],
-        cost_estimate=cost(0, 2 * (4 * rows + 2 * blocks * BLK) * width * 2),
+    return pl.pallas_call(
+        body,
+        out_shape=jax.ShapeDtypeStruct((count, 2, CAP, BLK, width), BF16),
+        in_specs=[smem, smem, hbm, hbm],
+        out_specs=pl.BlockSpec(memory_space=pltpu.VMEM),
+        scratch_shapes=[pltpu.SMEM((count,), jnp.int32), pltpu.SemaphoreType.DMA((blocks, 4))],
+        cost_estimate=cost(0, 4 * memory_keys.size * 2),
         compiler_params=pltpu.CompilerParams(vmem_limit_bytes=60 * 2**20),
-        name="staged",
+        name="pack_memory",
     )(
         position[None],
         routes.reshape(-1),
-        query,
-        keys,
-        values,
-        cotangent,
         memory_keys.reshape(blocks, BLK, width),
         memory_values.reshape(blocks, BLK, width),
     )
@@ -158,6 +158,9 @@
         return pl.BlockSpec(
             (slots, 2, CAP * BLK, self.cols), lambda i: (0, 0, 0, part * self.steps + i)
         )
+
+    def pair(self):
+        return pl.BlockSpec((2 * self.rows, self.cols), lambda i: (0, i))
 
     def whole(self, shape):
         return pl.BlockSpec(shape, lambda i: (0,) * len(shape))
@@ -183,22 +186,19 @@
     return keys, memory_keys, current, jnp.concatenate(parts, axis=0)
 
 
-def forward(plan, own_qd, far_qd, kv, memory, key_row, query_col, memory_bias):
+def widened(column, like):
+    return jnp.concatenate([column] * (like.shape[1] // column.shape[1]), axis=1)
+
+
+def attend_near(plan, own_qd, far_qd, kv, memory, key_row, query_col, memory_bias):
     rows = plan.rows
 
-    def body(
-        qo, qf, do_o, do_f, k0, k1, k2, k3, v0, v1, v2, v3, mk, mv, krow, qcol, mbias,
-        att_own, att_far, stat_col, stat_row,
-    ):
+    def body(qo, qf, k0, k1, v0, v1, mk, mv, krow, qcol, mbias, mixed_out, top_out, total_out):
         bias = visible_bias(krow[0:1, :], krow[1:2, :], qcol[:, 0:1], qcol[:, 1:2])
-        lane = lax.broadcasted_iota(jnp.int32, (2 * rows, HDIM), 1)
-        stats = jnp.zeros((2 * rows, HDIM), F32)
         for g in range(plan.group):
             lanes = slice(g * HDIM, (g + 1) * HDIM)
             query = joined((qo, qf), lanes)
-            _, _, current, mem = scores_of(
-                plan, query, (k0, k1, k2, k3), mk, bias, mbias, lanes, rows
-            )
+            _, _, current, mem = scores_of(plan, query, (k0, k1), mk, bias, mbias, lanes, rows)
             top = jnp.maximum(
                 jnp.max(current, axis=1, keepdims=True), jnp.max(mem, axis=1, keepdims=True)
             )
@@ -207,8 +207,7 @@
             total = jnp.sum(weight, axis=1, keepdims=True) + jnp.sum(
                 mem_weight, axis=1, keepdims=True
             )
-            values = joined((v0, v1, v2, v3), lanes)
-            mixed = dot_nn(weight.astype(BF16), values)
+            mixed = dot_nn(weight.astype(BF16), joined((v0, v1), lanes))
             mem16 = mem_weight.astype(BF16)
             mixed_mem = [
                 dot_nn(
@@ -217,55 +216,103 @@
                 )
                 for part in range(2)
             ]
-            output = (mixed + jnp.concatenate(mixed_mem, axis=0)) / total
+            mixed_out[:, lanes] = mixed + jnp.concatenate(mixed_mem, axis=0)
+            top_out[:, lanes] = jnp.broadcast_to(top, (2 * rows, HDIM))
+            total_out[:, lanes] = jnp.broadcast_to(total, (2 * rows, HDIM))
+
+    flops = 2 * 2 * (2 * rows) * (2 * rows + plan.memory_rows) * plan.half
+    return pl.pallas_call(
+        body,
+        grid=(plan.steps,),
+        out_shape=(jax.ShapeDtypeStruct((2 * rows, plan.half), F32),) * 3,
+        in_specs=[plan.first()] * 4
+        + [plan.second()] * 2
+        + [plan.memory(0), plan.memory(1)]
+        + [plan.whole(key_row.shape), plan.whole(query_col.shape), plan.whole(memory_bias.shape)],
+        out_specs=(plan.pair(),) * 3,
+        cost_estimate=cost(flops, 12 * rows * plan.half * 2, 2 * rows * 3 * rows * plan.heads),
+        compiler_params=pltpu.CompilerParams(vmem_limit_bytes=VMEM_BYTES),
+        name="attend_near",
+    )(own_qd, far_qd, *kv, *kv, memory, memory, key_row, query_col, memory_bias)
+
+
+def attend_prev(plan, own_qd, far_qd, kv, key_row, query_col, near):
+    rows = plan.rows
+
+    def body(
+        qo, qf, do_o, do_f, k0, k1, v0, v1, krow, qcol, mixed_in, top_in, total_in,
+        att_own, att_far, level_out, delta_out, stat_row,
+    ):
+        bias = visible_bias(krow[0:1, :], krow[1:2, :], qcol[:, 0:1], qcol[:, 1:2])
+        lane = lax.broadcasted_iota(jnp.int32, (2 * rows, HDIM), 1)
+        stats = jnp.zeros((2 * rows, HDIM), F32)
+        scaling = plan.scale * LOG2E
+        for g in range(plan.group):
+            lanes = slice(g * HDIM, (g + 1) * HDIM)
+            query = joined((qo, qf), lanes)
+            score = dot_nt(query, joined((k0, k1), lanes)) * scaling + bias
+            near_top = top_in[:, lanes]
+            top = jnp.maximum(
+                jnp.broadcast_to(jnp.max(score, axis=1, keepdims=True), near_top.shape), near_top
+            )
+            weight = jnp.exp2(score - widened(top, score))
+            shrink = jnp.exp2(near_top - top)
+            total = jnp.sum(weight, axis=1, keepdims=True) + total_in[:, lanes] * shrink
+            mixed = dot_nn(weight.astype(BF16), joined((v0, v1), lanes))
+            output = (mixed + mixed_in[:, lanes] * shrink) / total
             upstream = joined((do_o, do_f), lanes).astype(F32)
             delta = jnp.sum(upstream * output, axis=1, keepdims=True)
             level = top + jnp.log2(total)
             stats = jnp.where(lane == g, level, stats)
             stats = jnp.where(lane == plan.group + g, delta, stats)
+            level_out[:, lanes] = level
+            delta_out[:, lanes] = jnp.broadcast_to(delta, level.shape)
             att_own[:, lanes] = output[:rows].astype(BF16)
             att_far[:, lanes] = output[rows:].astype(BF16)
-        stat_col[0] = stats
         stat_row[0] = stats.T[0:8, :]
 
-    flops = 2 * 2 * (2 * rows) * (4 * rows + plan.memory_rows) * plan.half
+    flops = 2 * 2 * (2 * rows) * (2 * rows) * plan.half
     return pl.pallas_call(
         body,
         grid=(plan.steps,),
         out_shape=(
             jax.ShapeDtypeStruct((rows, plan.half), BF16),
             jax.ShapeDtypeStruct((rows, plan.half), BF16),
-            jax.ShapeDtypeStruct((plan.steps, 2 * rows, HDIM), F32),
+            jax.ShapeDtypeStruct((2 * rows, plan.half), F32),
+            jax.ShapeDtypeStruct((2 * rows, plan.half), F32),
             jax.ShapeDtypeStruct((plan.steps, 8, 2 * rows), F32),
         ),
         in_specs=[plan.first()] * 2
         + [plan.second()] * 2
-        + [plan.first()] * 4
-        + [plan.second()] * 4
-        + [plan.memory(0), plan.memory(1)]
-        + [plan.whole(key_row.shape), plan.whole(query_col.shape), plan.whole(memory_bias.shape)],
+        + [plan.first()] * 2
+        + [plan.second()] * 2
+        + [plan.whole(key_row.shape), plan.whole(query_col.shape)]
+        + [plan.pair()] * 3,
         out_specs=(
             plan.first(),
             plan.first(),
-            pl.BlockSpec((1, 2 * rows, HDIM), lambda i: (i, 0, 0)),
+            plan.pair(),
+            plan.pair(),
             pl.BlockSpec((1, 8, 2 * rows), lambda i: (i, 0, 0)),
         ),
-        cost_estimate=cost(flops, 12 * rows * plan.half * 2, 2 * rows * 5 * rows * plan.heads),
+        cost_estimate=cost(flops, 16 * rows * plan.half * 2, 4 * rows * rows * plan.heads),
         compiler_params=pltpu.CompilerParams(vmem_limit_bytes=VMEM_BYTES),
-        name="attend",
-    )(own_qd, far_qd, own_qd, far_qd, *kv, *kv, memory, memory, key_row, query_col, memory_bias)
+        name="attend_prev",
+    )(
+        own_qd, far_qd, own_qd, far_qd, *kv, *kv, key_row, query_col, *near
+    )
 
 
 def dot_tn(a, b):
     return lax.dot_general(a, b, (((0,), (0,)), ((), ())), preferred_element_type=F32)
 
 
-def own_gradients(plan, own_qd, far_qd, kv, memory, key_row, query_col, memory_bias, stats):
+def own_gradients(plan, own_qd, far_qd, kv, memory, key_row, query_col, memory_bias, level, delta):
     rows = plan.rows
 
     def body(
         qo, qf, do_o, do_f, k0, k1, k2, k3, v0, v1, v2, v3, mk, mv, krow, qcol, mbias,
-        stat_col, dq_own, dq_far, squares, dk, dv,
+        level_in, delta_in, dq_own, dq_far, squares, dk, dv,
     ):
         bias = visible_bias(krow[0:1, :], krow[1:2, :], qcol[:, 0:1], qcol[:, 1:2])
         acc = jnp.zeros((8, HDIM), F32)
@@ -273,22 +320,22 @@
             lanes = slice(g * HDIM, (g + 1) * HDIM)
             query = joined((qo, qf), lanes)
             upstream = joined((do_o, do_f), lanes)
-            level = stat_col[0, :, g : g + 1]
-            delta = stat_col[0, :, plan.group + g : plan.group + g + 1]
+            level = level_in[:, lanes]
+            delta = delta_in[:, lanes]
             keys, mem_keys, current, mem = scores_of(
                 plan, query, (k0, k1, k2, k3), mk, bias, mbias, lanes, rows
             )
             values = joined((v0, v1, v2, v3), lanes)
-            press = dot_nt(upstream, values) - delta
-            prob = jnp.exp2(current - level)
+            press = dot_nt(upstream, values) - widened(delta, current)
+            prob = jnp.exp2(current - widened(level, current))
             grad = (prob * press).astype(BF16)
             result = dot_nn(grad, keys)
             extra = []
             for part in range(2):
                 span = slice(part * rows, (part + 1) * rows)
                 mem_values = mv[:, part, :, lanes].reshape(plan.memory_rows, HDIM)
-                mem_press = dot_nt(upstream[span], mem_values) - delta[span]
-                mem_grad = (jnp.exp2(mem[span] - level[span]) * mem_press).astype(BF16)
+                mem_press = dot_nt(upstream[span], mem_values) - widened(delta[span], mem)
+                mem_grad = (jnp.exp2(mem[span] - widened(level[span], mem)) * mem_press).astype(BF16)
                 extra.append(dot_nn(mem_grad, mem_keys[part]))
             result = (result + jnp.concatenate(extra, axis=0)) * plan.scale
             dq_own[:, lanes] = result[:rows]
@@ -321,14 +368,14 @@
         + [plan.second()] * 4
         + [plan.memory(0), plan.memory(1)]
         + [plan.whole(key_row.shape), plan.whole(query_col.shape), plan.whole(memory_bias.shape)]
-        + [pl.BlockSpec((1, 2 * rows, HDIM), lambda i: (i, 0, 0))],
+        + [plan.pair()] * 2,
         out_specs=(plan.first(), plan.first(), plan.whole((8, HDIM)), both, both),
         cost_estimate=cost(flops, 22 * rows * plan.half * 2, 2 * rows * 5 * rows * plan.heads),
         compiler_params=pltpu.CompilerParams(vmem_limit_bytes=VMEM_BYTES),
         name="own_gradients",
     )(
         own_qd, far_qd, own_qd, far_qd, *kv, *kv, memory, memory, key_row, query_col, memory_bias,
-        stats,
+        level, delta,
     )
 
 
@@ -452,9 +499,9 @@
     memory_rows = count * CAP * BLK
     plan = Plan(rows, half, memory_rows)
 
-    own_kv, sent_kv, own_qd, sent_qd, packed = staged(
-        position, routes, query, keys, values, cotangent, memory_keys, memory_values, count
-    )
+    packed = pack_memory(position, routes, memory_keys, memory_values, count)
+    own_kv, sent_kv = halves(position, keys, values)
+    own_qd, sent_qd = halves(position, query, cotangent)
     far_kv = swapped(sent_kv)
     prev_own_kv = shifted(own_kv, 2)
     next_own_qd = shifted(own_qd, -2)
@@ -485,13 +532,14 @@
     ).reshape(2, memory_rows)
 
     kv = (own_kv, far_kv, prev_own_kv, prev_far_kv)
-    att_own, att_far, stat_col, stat_row = forward(
-        plan, own_qd, far_qd, kv, arrived, key_row, near_col, memory_bias
+    near = attend_near(plan, own_qd, far_qd, kv[:2], arrived, near_row, near_col, memory_bias)
+    att_own, att_far, level, delta, stat_row = attend_prev(
+        plan, own_qd, far_qd, kv[2:], prev_row, near_col, near
     )
     next_stats = shifted(stat_row, -2)
     att_back = swapped(att_far)
     dq_own, dq_far, dq_squares, near_dk, near_dv = own_gradients(
-        plan, own_qd, far_qd, kv, arrived, key_row, near_col, memory_bias, stat_col
+        plan, own_qd, far_qd, kv, arrived, key_row, near_col, memory_bias, level, delta
     )
     next_stats, dq_far, att_back = lax.optimization_barrier((next_stats, dq_far, att_back))
     dq_back = swapped(dq_far)

time: 97.9 us -> 95 us (0.970)
  waiting for transfers between devices: 34.9 us -> 23.6 us
  Pallas kernels: 21.2 us -> 25.9 us
  local copies, waits for them, and re-layouts: 2.53 us -> 4.99 us
    ppermute x5, waiting for transfers between devices: 29.6 us -> 18.4 us  [swapped(): return lax.ppermute(value, 'ctx', [(i, i ^ 1) for i in range(count)])]
    pallas_call x2 -> x5, Pallas kernels: 9.89 us -> 14.7 us  [the longest x2 4.38 us: halves(): pl.pallas_call(body, out_shape=(jax.ShapeDtypeStruct((rows, width), BF16)...]
    unnamed x15 -> x43, local copies, waits for them, and re-layouts: 2.12 us -> 4.59 us
  transfers between devices with their start and end apart: 12 -> 12, of which waited for: 5 -> 4; matrix products, arithmetic and copies ran while one was open for 4% -> 5% of each run, Pallas kernels for 16% -> 23%
where the time goes in v3:
time: 95 us; the launch traced here: 94.4 us
  starting transfers between devices  35.2 us (37%)
  Pallas kernels  25.9 us (27%)
  waiting for transfers between devices  23.6 us (25%)
  local copies, waits for them, and re-layouts  4.99 us (5%)
  other arithmetic  3.76 us (4%)
  between operations  1.01 us (1%)
    ppermute x5, waiting for transfers between devices, swapped(): return lax.ppermute(value, 'ctx', [(i, i ^ 1) for i in range(count)])  18.4 us
    ppermute x5, starting transfers between devices, shifted(): return lax.ppermute(value, 'ctx', pairs)  12.1 us
    all_to_all x1, starting transfers between devices, on_device(): lax.all_to_all(share, ('ctx', 'head'), split_axis=0, concat_axis=0, tiled...  10.5 us
    all_to_all x1, starting transfers between devices, on_device(): lax.all_to_all(packed.reshape(count, 2 * CAP * BLK, width), 'ctx', split_...  7.29 us
    pallas_call x1, Pallas kernels, own_gradients(): pl.pallas_call(body, grid=(plan.steps,), out_shape=(jax.ShapeDtypeStruct(...  5.78 us
    ppermute x5, starting transfers between devices, swapped(): return lax.ppermute(value, 'ctx', [(i, i ^ 1) for i in range(count)])  5.24 us
    all_to_all x1, waiting for transfers between devices, on_device(): lax.all_to_all(share, ('ctx', 'head'), split_axis=0, concat_axis=0, tiled...  5.13 us
    unnamed x43, local copies, waits for them, and re-layouts  4.59 us
  transfers between devices with their start and end apart: 12, of which 4 were waited for; matrix products, arithmetic and copies ran while one was open for 5% of the time, Pallas kernels for 23%

profile of v3, /device:TPU:0, one launch (start us, length us, event | category | flops | bytes accessed | tf_op | source)
XLA Modules:
  0.0 94.4 jit_solution(1238277773837692977)
XLA Ops:
  0.6 3.3 %pack_memory.1 = bf16[8,2,2,8,2048]{4,3,2,1,0:T(8,128)(2,1)} custom-call(s32[1]{0:T(128)} %bitcast.where, s32[96]{0:T(128)} %bitcast.38, bf16[12,8,2048]{2,1,0:T(8,128)(2,1)} %bitcast.36, bf16[12,8,2048]{2,1,0:T(8,128)(2,1)} %bitcast.37), custom_call_target="tpu_custom_call" | custom-call | bytes 1572864 | tf_op jit(solution)/shard_map/pack_memory/pallas_call | solution.py:120
  3.9 7.3 %all-to-all-start = ((bf16[8,32,2048]{2,1,0:T(8,128)(2,1)}), bf16[8,32,2048]{2,1,0:T(8,128)(2,1)S(1)}, u32[]{:S(2)}, u32[]{:S(2)}) async-start(bf16[8,32,2048]{2,1,0:T(8,128)(2,1)} %bitcast.35), calls=%async_computation | async-start | bytes 2097152 | tf_op jit(solution)/shard_map/all_to_all | solution.py:512
  11.2 2.2 %halves.3 = (bf16[128,2048]{1,0:T(8,128)(2,1)}, bf16[128,2048]{1,0:T(8,128)(2,1)}) custom-call(s32[1]{0:T(128)} %bitcast.where, bf16[128,2048]{1,0:T(8,128)(2,1)} %one.3, bf16[128,2048]{1,0:T(8,128)(2,1)} %two.3), custom_call_target="tpu_custom_call" | custom-call | bytes 2097152 | tf_op jit(solution)/shard_map/halves/pallas_call | solution.py:63
  13.4 2.1 %collective-permute-start = (bf16[128,2048]{1,0:T(8,128)(2,1)}, bf16[128,2048]{1,0:T(8,128)(2,1)S(1)}, u32[]{:S(2)}, u32[]{:S(2)}) collective-permute-start(bf16[128,2048]{1,0:T(8,128)(2,1)} %get-tuple-element.36), channel_id=1, source_target_pairs={{0,4},{4,0},{8,12},{12,8},{16,20},{20,16},{24,28},{28,24},{1,5},{5... | collective-permute-start | bytes 1572872 | tf_op jit(solution)/shard_map/ppermute | solution.py:36
  15.5 3.5 %collective-permute-start.2 = (bf16[128,2048]{1,0:T(8,128)(2,1)}, bf16[128,2048]{1,0:T(8,128)(2,1)S(1)}, u32[]{:S(2)}, u32[]{:S(2)}) collective-permute-start(bf16[128,2048]{1,0:T(8,128)(2,1)} %get-tuple-element.39.k0.v0), channel_id=1, source_target_pairs={{0,8},{4,12},{8,16},{12,20},{16,24},{20,28},{1,9},{5,13},{9,17},{1... | collective-permute-start | bytes 1572872 | tf_op jit(solution)/shard_map/ppermute | solution.py:31
  19.0 2.2 %halves.2 = (bf16[128,2048]{1,0:T(8,128)(2,1)}, bf16[128,2048]{1,0:T(8,128)(2,1)}) custom-call(s32[1]{0:T(128)} %bitcast.where, bf16[128,2048]{1,0:T(8,128)(2,1)} %one.2, bf16[128,2048]{1,0:T(8,128)(2,1)} %two.2), custom_call_target="tpu_custom_call" | custom-call | bytes 2097152 | tf_op jit(solution)/shard_map/halves/pallas_call | solution.py:63
  21.2 1.3 %collective-permute-start.6 = (bf16[128,2048]{1,0:T(8,128)(2,1)}, bf16[128,2048]{1,0:T(8,128)(2,1)}, u32[]{:S(2)}, u32[]{:S(2)}) collective-permute-start(bf16[128,2048]{1,0:T(8,128)(2,1)} %get-tuple-element.35.qo.do_o), channel_id=1, source_target_pairs={{8,0},{12,4},{16,8},{20,12},{24,16},{28,20},{9,1},{13,5},{17,9},{2... | collective-permute-start | bytes 1572872 | tf_op jit(solution)/shard_map/ppermute | solution.py:31
  22.6 0.0 copy-start.20
  22.6 0.6 broadcast.61
  23.2 0.1 copy-done.20
  23.2 0.7 reduce.3
  23.9 0.1 eq.21
  24.0 0.0 copy-start.16
  24.1 0.1 pad_add_fusion
  24.1 0.6 copy-done.13
  24.7 0.6 fusion.5
  25.4 0.2 convert_reduce_fusion
  25.6 10.5 %collective-permute-done.k1.v1 = bf16[128,2048]{1,0:T(8,128)(2,1)S(1)} collective-permute-done((bf16[128,2048]{1,0:T(8,128)(2,1)}, bf16[128,2048]{1,0:T(8,128)(2,1)S(1)}, u32[]{:S(2)}, u32[]{:S(2)}) %collective-permute-start) | collective-permute-done | bytes 524320 | tf_op jit(solution)/shard_map/ppermute | solution.py:36
  36.0 0.0 collective-permute-start.1
  36.0 4.7 %collective-permute-start.3 = (bf16[128,2048]{1,0:T(8,128)(2,1)S(1)}, bf16[128,2048]{1,0:T(8,128)(2,1)}, u32[]{:S(2)}, u32[]{:S(2)}) collective-permute-start(bf16[128,2048]{1,0:T(8,128)(2,1)S(1)} %collective-permute-done.k1.v1), channel_id=1, source_target_pairs={{0,8},{4,12},{8,16},{12,20},{16,24},{20,28},{1,9},{5,13},{9,17},{1... | collective-permute-start | bytes 1572872 | tf_op jit(solution)/shard_map/ppermute | solution.py:31
  40.8 0.0 copy-done.16
  40.8 0.1 copy.21
  40.9 0.1 fusion
  41.0 0.1 broadcast_in_dim.38
  41.1 0.1 reshape.82.mbias
  41.2 0.0 copy-start.9
  41.2 0.0 copy-start.11
  41.2 0.0 copy-done.5
  41.2 0.0 copy-done.7
  41.2 0.5 copy-done.9
  41.7 0.1 copy-done.11
  41.8 7.6 %collective-permute-done.1.qf.do_f = bf16[128,2048]{1,0:T(8,128)(2,1)S(1)} collective-permute-done((bf16[128,2048]{1,0:T(8,128)(2,1)}, bf16[128,2048]{1,0:T(8,128)(2,1)S(1)}, u32[]{:S(2)}, u32[]{:S(2)}) %collective-permute-start.1) | collective-permute-done | bytes 524320 | tf_op jit(solution)/shard_map/ppermute | solution.py:36
  49.4 1.3 %collective-permute-start.7 = (bf16[128,2048]{1,0:T(8,128)(2,1)S(1)}, bf16[128,2048]{1,0:T(8,128)(2,1)}, u32[]{:S(2)}, u32[]{:S(2)}) collective-permute-start(bf16[128,2048]{1,0:T(8,128)(2,1)S(1)} %collective-permute-done.1.qf.do_f), channel_id=1, source_target_pairs={{8,0},{12,4},{16,8},{20,12},{24,16},{28,20},{9,1},{13,5},{17,9},{2... | collective-permute-start | bytes 1572872 | tf_op jit(solution)/shard_map/ppermute | solution.py:31
  50.7 0.0 all-to-all-done
  50.7 0.0 copy-start.1
  50.7 1.0 %copy-done.1 = bf16[128,2048]{1,0:T(8,128)(2,1)S(1)} copy-done((bf16[128,2048]{1,0:T(8,128)(2,1)S(1)}, bf16[128,2048]{1,0:T(8,128)(2,1)}, u32[]{:S(2)}) %copy-start.1) | copy-done | bytes 524312
  51.7 3.3 %attend_near.1 = (f32[256,1024]{1,0:T(8,128)S(1)}, f32[256,1024]{1,0:T(8,128)S(1)}, f32[256,1024]{1,0:T(8,128)S(1)}) custom-call(bf16[128,2048]{1,0:T(8,128)(2,1)S(1)} %copy-done.1, bf16[128,2048]{1,0:T(8,128)(2,1)S(1)} %collective-permute-done.1.qf.do_f, bf16[128,2048]{1,0:T(8,128)(2,1)S(1)} %copy-done, bf16[128,2048]{1,0:T(8,128)(2,1)S(1)} %collective-permute-done.k1.v1, ...), custom_call_target="tpu_custom_call" | custom-call | flops 402653184 | bytes 3145728 | tf_op jit(solution)/shard_map/attend_near/pallas_call | solution.py:224
  55.1 0.0 collective-permute-done.2.k0.v0.k2.v2
  55.1 0.0 collective-permute-done.3.k1.v1.k3.v3
  55.1 3.7 %attend_prev.1 = (bf16[128,1024]{1,0:T(8,128)(2,1)S(1)}, bf16[128,1024]{1,0:T(8,128)(2,1)S(1)}, f32[256,1024]{1,0:T(8,128)S(1)}, f32[256,1024]{1,0:T(8,128)S(1)}, f32[2,8,256]{2,1,0:T(8,128)S(1)}) custom-call(bf16[128,2048]{1,0:T(8,128)(2,1)S(1)} %copy-done.1, bf16[128,2048]{1,0:T(8,128)(2,1)S(1)} %collective-permute-done.1.qf.do_f, ...), custom_call_target="tpu_custom_call" | custom-call | flops 268435456 | bytes 4194304 | tf_op jit(solution)/shard_map/attend_prev/pallas_call | solution.py:275
  58.9 0.0 copy-start.10
  58.9 0.3 collective-permute-start.5
  59.2 0.2 copy-done.6
  59.5 0.0 copy-done.10
  59.5 1.3 %collective-permute-start.4 = (f32[2,8,256]{2,1,0:T(8,128)S(1)}, f32[2,8,256]{2,1,0:T(8,128)S(1)}, u32[]{:S(2)}, u32[]{:S(2)}) collective-permute-start(f32[2,8,256]{2,1,0:T(8,128)S(1)} %get-tuple-element.45), channel_id=1, source_target_pairs={{8,0},{12,4},{16,8},{20,12},{24,16},{28,20},{9,1},{13,5},{17,9},{2... | collective-permute-start | bytes 49160 | tf_op jit(solution)/shard_map/ppermute | solution.py:31
  60.8 5.8 %own_gradients.1 = (f32[128,1024]{1,0:T(8,128)S(1)}, bf16[128,1024]{1,0:T(8,128)(2,1)S(1)}, f32[8,128]{1,0:T(8,128)S(1)}, f32[256,1024]{1,0:T(8,128)S(1)}, f32[256,1024]{1,0:T(8,128)S(1)}) custom-call(bf16[128,2048]{1,0:T(8,128)(2,1)S(1)} %copy-done.1, bf16[128,2048]{1,0:T(8,128)(2,1)S(1)} %collective-permute-done.1.qf.do_f, ...), custom_call_target="tpu_custom_call" | custom-call | flops 1275068416 | bytes 5767168 | tf_op jit(solution)/shard_map/own_gradients/pallas_call | solution.py:355
  66.6 0.0 copy-start.2
  66.6 0.8 copy-done.2
  67.4 0.0 collective-permute-done.4.stat
  67.4 0.0 collective-permute-done.5
  67.4 1.6 %collective-permute-start.8 = (bf16[128,1024]{1,0:T(8,128)(2,1)S(1)}, bf16[128,1024]{1,0:T(8,128)(2,1)S(1)}, u32[]{:S(2)}, u32[]{:S(2)}) collective-permute-start(bf16[128,1024]{1,0:T(8,128)(2,1)S(1)} %get-tuple-element.58), channel_id=1, source_target_pairs={{0,4},{4,0},{8,12},{12,8},{16,20},{20,16},{24,28},{28,24},{1,5},{5... | collective-permute-start | bytes 786440 | tf_op jit(solution)/shard_map/ppermute | solution.py:36
  69.0 0.6 copy-done.14
  69.6 0.0 copy-done.15
  69.7 0.0 collective-permute-done.6.qo.do_o
  69.7 0.0 collective-permute-done.7.qf.do_f
  69.7 4.1 %key_gradient_next.1 = (f32[128,1024]{1,0:T(8,128)S(1)}, f32[128,1024]{1,0:T(8,128)S(1)}, bf16[2,128,1024]{2,1,0:T(8,128)(2,1)}, f32[32,128]{1,0:T(8,128)}) custom-call(bf16[128,2048]{1,0:T(8,128)(2,1)} %collective-permute-done.6.qo.do_o, bf16[128,2048]{1,0:T(8,128)(2,1)} %collective-permute-done.7.qf.do_f, ...), custom_call_target="tpu_custom_call" | custom-call | flops 536870912 | bytes 6291456 | tf_op jit(solution)/shard_map/key_gradient_next/pallas_call | solution.py:433
  73.8 0.3 collective-permute-done.8.dq_other
  74.1 1.2 %collective-permute-start.9 = (bf16[2,128,1024]{2,1,0:T(8,128)(2,1)}, bf16[2,128,1024]{2,1,0:T(8,128)(2,1)S(1)}, u32[]{:S(2)}, u32[]{:S(2)}) collective-permute-start(bf16[2,128,1024]{2,1,0:T(8,128)(2,1)} %get-tuple-element.62), channel_id=1, source_target_pairs={{0,4},{4,0},{8,12},{12,8},{16,20},{20,16},{24,28},{28,24},{1,5},{5... | collective-permute-start | bytes 1572872 | tf_op jit(solution)/shard_map/ppermute | solution.py:36
  75.4 10.5 %all-to-all-start.1 = ((f32[32,1,128]{2,1,0:T(1,128)}), f32[32,1,128]{2,1,0:T(1,128)S(1)}, u32[]{:S(2)}, u32[]{:S(2)}) async-start(f32[32,1,128]{2,1,0:T(1,128)} %bitcast.16), calls=%async_computation.1 | async-start | bytes 32768 | tf_op jit(solution)/shard_map/all_to_all | solution.py:552
  85.9 0.0 copy-start.3
  85.9 2.0 %maximum_select_fusion = bf16[128,2048]{1,0:T(8,128)(2,1)} fusion(bf16[128,1024]{1,0:T(8,128)(2,1)} %copy-done.4, bf16[128,1024]{1,0:T(8,128)(2,1)S(1)} %get-tuple-element.44, pred[]{:T(512)S(6)} %eq.20), kind=kLoop, calls=%fused_computation | loop fusion | flops 2359296 | bytes 1048577 | tf_op jit(solution)/shard_map/jit(_where)/select_n | solution.py:557
  87.9 5.1 %all-to-all-done.1 = f32[32,1,128]{2,1,0:T(1,128)S(1)} async-done(((f32[32,1,128]{2,1,0:T(1,128)}), f32[32,1,128]{2,1,0:T(1,128)S(1)}, u32[]{:S(2)}, u32[]{:S(2)}) %all-to-all-start.1) | async-done | bytes 16416 | tf_op jit(solution)/shard_map/all_to_all | solution.py:552
  93.0 0.0 collective-permute-done.9.other
  93.0 1.4 %scaled.1 = (bf16[128,2048]{1,0:T(8,128)(2,1)}, bf16[128,2048]{1,0:T(8,128)(2,1)}, bf16[128,2048]{1,0:T(8,128)(2,1)}) custom-call(s32[1]{0:T(128)} %bitcast.12.side_ref, f32[32,128]{1,0:T(8,128)S(1)} %bitcast.34, f32[128,1024]{1,0:T(8,128)S(1)} %copy-done.3, bf16[128,1024]{1,0:T(8,128)(2,1)S(1)} %collective-permute-done.8.dq_other, ...), custom_call_target="tpu_custom_call" | custom-call | flops 786432 | bytes 2621440 | tf_op jit(solution)/shard_map/scaled/pallas_call | solution.py:479
  (29 shorter events, 0.1 us)
Async XLA Ops:
  3.9 46.8 %all-to-all-start = ((bf16[8,32,2048]{2,1,0:T(8,128)(2,1)}), bf16[8,32,2048]{2,1,0:T(8,128)(2,1)S(1)}, u32[]{:S(2)}, u32[]{:S(2)}) async-start(bf16[8,32,2048]{2,1,0:T(8,128)(2,1)} %bitcast.35), calls=%async_computation | async-start | bytes 2097152 | tf_op jit(solution)/shard_map/all_to_all | solution.py:512
  13.4 22.6 %collective-permute-start = (bf16[128,2048]{1,0:T(8,128)(2,1)}, bf16[128,2048]{1,0:T(8,128)(2,1)S(1)}, u32[]{:S(2)}, u32[]{:S(2)}) collective-permute-start(bf16[128,2048]{1,0:T(8,128)(2,1)} %get-tuple-element.36), channel_id=1, source_target_pairs={{0,4},{4,0},{8,12},{12,8},{16,20},{20,16},{24,28},{28,24},{1,5},{5... | collective-permute-start | bytes 1572872 | tf_op jit(solution)/shard_map/ppermute | solution.py:36
  15.5 35.2 %copy-start = (bf16[128,2048]{1,0:T(8,128)(2,1)S(1)}, bf16[128,2048]{1,0:T(8,128)(2,1)}, u32[]{:S(2)}) copy-start(bf16[128,2048]{1,0:T(8,128)(2,1)} %get-tuple-element.39.k0.v0) | copy-start | bytes 1572868
  15.5 39.6 %collective-permute-start.2 = (bf16[128,2048]{1,0:T(8,128)(2,1)}, bf16[128,2048]{1,0:T(8,128)(2,1)S(1)}, u32[]{:S(2)}, u32[]{:S(2)}) collective-permute-start(bf16[128,2048]{1,0:T(8,128)(2,1)} %get-tuple-element.39.k0.v0), channel_id=1, source_target_pairs={{0,8},{4,12},{8,16},{12,20},{16,24},{20,28},{1,9},{5,13},{9,17},{1... | collective-permute-start | bytes 1572872 | tf_op jit(solution)/shard_map/ppermute | solution.py:31
  21.2 48.4 %collective-permute-start.6 = (bf16[128,2048]{1,0:T(8,128)(2,1)}, bf16[128,2048]{1,0:T(8,128)(2,1)}, u32[]{:S(2)}, u32[]{:S(2)}) collective-permute-start(bf16[128,2048]{1,0:T(8,128)(2,1)} %get-tuple-element.35.qo.do_o), channel_id=1, source_target_pairs={{8,0},{12,4},{16,8},{20,12},{24,16},{28,20},{9,1},{13,5},{17,9},{2... | collective-permute-start | bytes 1572872 | tf_op jit(solution)/shard_map/ppermute | solution.py:31
  22.6 0.7 copy-start.20
  24.0 0.7 copy-start.13
  24.0 16.7 %copy-start.16 = (s32[1,128]{1,0:T(1,128)}, s32[1,128]{1,0:T(1,128)S(1)}, u32[]{:S(2)}) copy-start(s32[1,128]{1,0:T(1,128)S(1)} %iota_add_fusion.2) | copy-start | bytes 1540
  24.0 16.7 %copy-start.18 = (s32[1,128]{1,0:T(1,128)}, s32[1,128]{1,0:T(1,128)S(1)}, u32[]{:S(2)}) copy-start(s32[1,128]{1,0:T(1,128)S(1)} %iota_add_fusion.3) | copy-start | bytes 1540
  25.3 15.9 %copy-start.5 = (s32[1,128]{1,0:T(1,128)}, s32[1,128]{1,0:T(1,128)S(1)}, u32[]{:S(2)}) copy-start(s32[1,128]{1,0:T(1,128)S(1)} %get-tuple-element.69) | copy-start | bytes 1540
  25.3 15.9 %copy-start.7 = (s32[1,128]{1,0:T(1,128)}, s32[1,128]{1,0:T(1,128)S(1)}, u32[]{:S(2)}) copy-start(s32[1,128]{1,0:T(1,128)S(1)} %get-tuple-element.70) | copy-start | bytes 1540
  36.0 13.3 %collective-permute-start.1 = (bf16[128,2048]{1,0:T(8,128)(2,1)}, bf16[128,2048]{1,0:T(8,128)(2,1)S(1)}, u32[]{:S(2)}, u32[]{:S(2)}) collective-permute-start(bf16[128,2048]{1,0:T(8,128)(2,1)} %get-tuple-element.38), channel_id=1, source_target_pairs={{0,4},{4,0},{8,12},{12,8},{16,20},{20,16},{24,28},{28,24},{1,5},{5... | collective-permute-start | bytes 1572872 | tf_op jit(solution)/shard_map/ppermute | solution.py:36
  36.0 19.1 %collective-permute-start.3 = (bf16[128,2048]{1,0:T(8,128)(2,1)S(1)}, bf16[128,2048]{1,0:T(8,128)(2,1)}, u32[]{:S(2)}, u32[]{:S(2)}) collective-permute-start(bf16[128,2048]{1,0:T(8,128)(2,1)S(1)} %collective-permute-done.k1.v1), channel_id=1, source_target_pairs={{0,8},{4,12},{8,16},{12,20},{16,24},{20,28},{1,9},{5,13},{9,17},{1... | collective-permute-start | bytes 1572872 | tf_op jit(solution)/shard_map/ppermute | solution.py:31
  41.2 0.5 copy-start.9
  41.2 0.6 copy-start.11
  49.4 20.3 %collective-permute-start.7 = (bf16[128,2048]{1,0:T(8,128)(2,1)S(1)}, bf16[128,2048]{1,0:T(8,128)(2,1)}, u32[]{:S(2)}, u32[]{:S(2)}) collective-permute-start(bf16[128,2048]{1,0:T(8,128)(2,1)S(1)} %collective-permute-done.1.qf.do_f), channel_id=1, source_target_pairs={{8,0},{12,4},{16,8},{20,12},{24,16},{28,20},{9,1},{13,5},{17,9},{2... | collective-permute-start | bytes 1572872 | tf_op jit(solution)/shard_map/ppermute | solution.py:31
  50.7 1.0 %copy-start.1 = (bf16[128,2048]{1,0:T(8,128)(2,1)S(1)}, bf16[128,2048]{1,0:T(8,128)(2,1)}, u32[]{:S(2)}) copy-start(bf16[128,2048]{1,0:T(8,128)(2,1)} %get-tuple-element.35.qo.do_o) | copy-start | bytes 1572868
  55.1 4.1 %copy-start.12 = (s32[1,128]{1,0:T(1,128)S(1)}, s32[1,128]{1,0:T(1,128)}, u32[]{:S(2)}) copy-start(s32[1,128]{1,0:T(1,128)} %copy-done.11) | copy-start | bytes 1540
  55.1 4.1 %copy-start.17 = (s32[1,128]{1,0:T(1,128)S(1)}, s32[1,128]{1,0:T(1,128)}, u32[]{:S(2)}) copy-start(s32[1,128]{1,0:T(1,128)} %copy-done.16) | copy-start | bytes 1540
  55.1 4.1 %copy-start.19 = (s32[1,128]{1,0:T(1,128)S(1)}, s32[1,128]{1,0:T(1,128)}, u32[]{:S(2)}) copy-start(s32[1,128]{1,0:T(1,128)} %copy-done.18) | copy-start | bytes 1540
  58.9 0.6 copy-start.6
  58.9 0.6 copy-start.8
  58.9 0.7 copy-start.10
  58.9 8.5 %collective-permute-start.5 = (bf16[128,1024]{1,0:T(8,128)(2,1)S(1)}, bf16[128,1024]{1,0:T(8,128)(2,1)S(1)}, u32[]{:S(2)}, u32[]{:S(2)}) collective-permute-start(bf16[128,1024]{1,0:T(8,128)(2,1)S(1)} %get-tuple-element.49), channel_id=1, source_target_pairs={{0,4},{4,0},{8,12},{12,8},{16,20},{20,16},{24,28},{28,24},{1,5},{5... | collective-permute-start | bytes 786440 | tf_op jit(solution)/shard_map/ppermute | solution.py:36
  59.5 7.9 %collective-permute-start.4 = (f32[2,8,256]{2,1,0:T(8,128)S(1)}, f32[2,8,256]{2,1,0:T(8,128)S(1)}, u32[]{:S(2)}, u32[]{:S(2)}) collective-permute-start(f32[2,8,256]{2,1,0:T(8,128)S(1)} %get-tuple-element.45), channel_id=1, source_target_pairs={{8,0},{12,4},{16,8},{20,12},{24,16},{28,20},{9,1},{13,5},{17,9},{2... | collective-permute-start | bytes 49160 | tf_op jit(solution)/shard_map/ppermute | solution.py:31
  66.6 0.8 copy-start.2
  67.4 6.4 %copy-start.4 = (bf16[128,1024]{1,0:T(8,128)(2,1)}, bf16[128,1024]{1,0:T(8,128)(2,1)S(1)}, u32[]{:S(2)}) copy-start(bf16[128,1024]{1,0:T(8,128)(2,1)S(1)} %collective-permute-done.5) | copy-start | bytes 786436
  67.4 6.7 %collective-permute-start.8 = (bf16[128,1024]{1,0:T(8,128)(2,1)S(1)}, bf16[128,1024]{1,0:T(8,128)(2,1)S(1)}, u32[]{:S(2)}, u32[]{:S(2)}) collective-permute-start(bf16[128,1024]{1,0:T(8,128)(2,1)S(1)} %get-tuple-element.58), channel_id=1, source_target_pairs={{0,4},{4,0},{8,12},{12,8},{16,20},{20,16},{24,28},{28,24},{1,5},{5... | collective-permute-start | bytes 786440 | tf_op jit(solution)/shard_map/ppermute | solution.py:36
  69.0 0.6 copy-start.14
  69.0 0.7 copy-start.15
  74.1 18.9 %collective-permute-start.9 = (bf16[2,128,1024]{2,1,0:T(8,128)(2,1)}, bf16[2,128,1024]{2,1,0:T(8,128)(2,1)S(1)}, u32[]{:S(2)}, u32[]{:S(2)}) collective-permute-start(bf16[2,128,1024]{2,1,0:T(8,128)(2,1)} %get-tuple-element.62), channel_id=1, source_target_pairs={{0,4},{4,0},{8,12},{12,8},{16,20},{20,16},{24,28},{28,24},{1,5},{5... | collective-permute-start | bytes 1572872 | tf_op jit(solution)/shard_map/ppermute | solution.py:36
  75.4 17.7 %all-to-all-start.1 = ((f32[32,1,128]{2,1,0:T(1,128)}), f32[32,1,128]{2,1,0:T(1,128)S(1)}, u32[]{:S(2)}, u32[]{:S(2)}) async-start(f32[32,1,128]{2,1,0:T(1,128)} %bitcast.16), calls=%async_computation.1 | async-start | bytes 32768 | tf_op jit(solution)/shard_map/all_to_all | solution.py:552
  85.9 7.2 %copy-start.3 = (f32[128,1024]{1,0:T(8,128)S(1)}, f32[128,1024]{1,0:T(8,128)}, u32[]{:S(2)}) copy-start(f32[128,1024]{1,0:T(8,128)} %copy-done.2) | copy-start | bytes 1572868

commit v4 on v3

--- a/solution.py
+++ b/solution.py
@@ -77,11 +77,18 @@
     width = memory_keys.shape[1]
     half = width // 2
 
-    def body(where, routes_ref, mk, mv, packed, used, sems):
-        left, right = pl.ds(0, half), pl.ds(half, half)
+    def body(where, routes_ref, mk, mv, packed, keys, values, used, sems):
+        copies = [
+            pltpu.make_async_copy(mk, keys, sems.at[0]),
+            pltpu.make_async_copy(mv, values, sems.at[1]),
+        ]
+        for copy in copies:
+            copy.start()
         packed[...] = jnp.zeros_like(packed)
         for owner in range(count):
             used[owner] = 0
+        for copy in copies:
+            copy.wait()
 
         def place(block, carry):
             owner = routes_ref[where[0] * blocks + block]
@@ -91,29 +98,13 @@
             partner = owner + 1 - 2 * odd
             near = pl.ds(pl.multiple_of(odd * half, half), half)
             away = pl.ds(pl.multiple_of(half - odd * half, half), half)
-            for n, (src, cols, target, who, part) in enumerate(
-                (
-                    (mk, near, owner, 0, left),
-                    (mv, near, owner, 0, right),
-                    (mk, away, partner, 1, left),
-                    (mv, away, partner, 1, right),
-                )
-            ):
-                pltpu.make_async_copy(
-                    src.at[block, :, cols], packed.at[target, who, slot, :, part], sems.at[block, n]
-                ).start()
+            packed[owner, 0, slot, :, :half] = keys[block, :, near]
+            packed[owner, 0, slot, :, half:] = values[block, :, near]
+            packed[partner, 1, slot, :, :half] = keys[block, :, away]
+            packed[partner, 1, slot, :, half:] = values[block, :, away]
             return carry
 
         lax.fori_loop(0, blocks, place, 0)
-
-        def settle(block, carry):
-            for n in range(4):
-                pltpu.make_async_copy(
-                    mk.at[block, :, left], packed.at[0, 0, 0, :, left], sems.at[block, n]
-                ).wait()
-            return carry
-
-        lax.fori_loop(0, blocks, settle, 0)
 
     smem = pl.BlockSpec(memory_space=pltpu.SMEM)
     hbm = pl.BlockSpec(memory_space=pltpu.HBM)
@@ -122,7 +113,12 @@
         out_shape=jax.ShapeDtypeStruct((count, 2, CAP, BLK, width), BF16),
         in_specs=[smem, smem, hbm, hbm],
         out_specs=pl.BlockSpec(memory_space=pltpu.VMEM),
-        scratch_shapes=[pltpu.SMEM((count,), jnp.int32), pltpu.SemaphoreType.DMA((blocks, 4))],
+        scratch_shapes=[
+            pltpu.VMEM((blocks, BLK, width), BF16),
+            pltpu.VMEM((blocks, BLK, width), BF16),
+            pltpu.SMEM((count,), jnp.int32),
+            pltpu.SemaphoreType.DMA((2,)),
+        ],
         cost_estimate=cost(0, 4 * memory_keys.size * 2),
         compiler_params=pltpu.CompilerParams(vmem_limit_bytes=60 * 2**20),
         name="pack_memory",
@@ -356,7 +352,7 @@
         body,
         grid=(plan.steps,),
         out_shape=(
-            jax.ShapeDtypeStruct((rows, plan.half), F32),
+            pltpu.HBM((rows, plan.half), F32),
             jax.ShapeDtypeStruct((rows, plan.half), BF16),
             jax.ShapeDtypeStruct((8, HDIM), F32),
             jax.ShapeDtypeStruct((2 * rows, plan.half), F32),
@@ -512,7 +508,6 @@
     arrived = lax.all_to_all(
         packed.reshape(count, 2 * CAP * BLK, width), "ctx", split_axis=0, concat_axis=0, tiled=True
     ).reshape(count, 2, CAP * BLK, width)
-    next_far_qd = shifted(far_qd, -2)
 
     def labels(block):
         docs = lax.dynamic_slice_in_dim(documents, block * rows, rows)
@@ -531,6 +526,10 @@
         jnp.where(live, 0.0, NEGATIVE)[..., None], (2, count, CAP, BLK)
     ).reshape(2, memory_rows)
 
+    far_qd, near_row, prev_row, next_row, key_row, near_col, memory_bias = lax.optimization_barrier(
+        (far_qd, near_row, prev_row, next_row, key_row, near_col, memory_bias)
+    )
+    next_far_qd = shifted(far_qd, -2)
     kv = (own_kv, far_kv, prev_own_kv, prev_far_kv)
     near = attend_near(plan, own_qd, far_qd, kv[:2], arrived, near_row, near_col, memory_bias)
     att_own, att_far, level, delta, stat_row = attend_prev(

time: 95 us -> 94.3 us (level)
  local copies, waits for them, and re-layouts: 4.99 us -> 2.74 us
  waiting for transfers between devices: 23.6 us -> 25.7 us
    unnamed x43 -> x13, local copies, waits for them, and re-layouts: 4.59 us -> 2.34 us
    ppermute x5, waiting for transfers between devices: 18.4 us -> 20.4 us  [swapped(): return lax.ppermute(value, 'ctx', [(i, i ^ 1) for i in range(count)])]
  transfers between devices with their start and end apart: 12 -> 12, of which waited for: 4 -> 5; matrix products, arithmetic and copies ran while one was open for 5% -> 4% of each run, Pallas kernels for 23% -> 23%
where the time goes in v4:
time: 94.3 us; the launch traced here: 93.8 us
  starting transfers between devices  35 us (37%)
  Pallas kernels  26.2 us (28%)
  waiting for transfers between devices  25.7 us (27%)
  other arithmetic  3.16 us (3%)
  local copies, waits for them, and re-layouts  2.74 us (3%)
    ppermute x5, waiting for transfers between devices, swapped(): return lax.ppermute(value, 'ctx', [(i, i ^ 1) for i in range(count)])  20.4 us
    ppermute x5, starting transfers between devices, shifted(): return lax.ppermute(value, 'ctx', pairs)  12.1 us
    all_to_all x1, starting transfers between devices, on_device(): lax.all_to_all(share, ('ctx', 'head'), split_axis=0, concat_axis=0, tiled...  10.5 us
    all_to_all x1, starting transfers between devices, on_device(): lax.all_to_all(packed.reshape(count, 2 * CAP * BLK, width), 'ctx', split_...  7.29 us
    pallas_call x1, Pallas kernels, own_gradients(): pl.pallas_call(body, grid=(plan.steps,), out_shape=(pltpu.HBM((rows, plan...  6.33 us
    ppermute x5, starting transfers between devices, swapped(): return lax.ppermute(value, 'ctx', [(i, i ^ 1) for i in range(count)])  5.14 us
    all_to_all x1, waiting for transfers between devices, on_device(): lax.all_to_all(share, ('ctx', 'head'), split_axis=0, concat_axis=0, tiled...  5.12 us
    pallas_call x2, Pallas kernels, halves(): pl.pallas_call(body, out_shape=(jax.ShapeDtypeStruct((rows, width), BF16)...  4.38 us
  transfers between devices with their start and end apart: 12, of which 5 were waited for; matrix products, arithmetic and copies ran while one was open for 4% of the time, Pallas kernels for 23%

profile of v4, /device:TPU:0, one launch (start us, length us, event | category | flops | bytes accessed | tf_op | source)
XLA Modules:
  0.0 93.8 jit_solution(920621036771321974)
XLA Ops:
  0.6 3.0 %pack_memory.1 = bf16[8,2,2,8,2048]{4,3,2,1,0:T(8,128)(2,1)} custom-call(s32[1]{0:T(128)} %bitcast.where, s32[96]{0:T(128)} %bitcast.38, bf16[12,8,2048]{2,1,0:T(8,128)(2,1)} %bitcast.36, bf16[12,8,2048]{2,1,0:T(8,128)(2,1)} %bitcast.37), custom_call_target="tpu_custom_call" | custom-call | bytes 1572864 | tf_op jit(solution)/shard_map/pack_memory/pallas_call | solution.py:111
  3.7 7.3 %all-to-all-start = ((bf16[8,32,2048]{2,1,0:T(8,128)(2,1)}), bf16[8,32,2048]{2,1,0:T(8,128)(2,1)S(1)}, u32[]{:S(2)}, u32[]{:S(2)}) async-start(bf16[8,32,2048]{2,1,0:T(8,128)(2,1)} %bitcast.35), calls=%async_computation | async-start | bytes 2097152 | tf_op jit(solution)/shard_map/all_to_all | solution.py:508
  11.0 2.2 %halves.3 = (bf16[128,2048]{1,0:T(8,128)(2,1)}, bf16[128,2048]{1,0:T(8,128)(2,1)}) custom-call(s32[1]{0:T(128)} %bitcast.where, bf16[128,2048]{1,0:T(8,128)(2,1)} %one.3, bf16[128,2048]{1,0:T(8,128)(2,1)} %two.3), custom_call_target="tpu_custom_call" | custom-call | bytes 2097152 | tf_op jit(solution)/shard_map/halves/pallas_call | solution.py:63
  13.2 2.1 %collective-permute-start = (bf16[128,2048]{1,0:T(8,128)(2,1)}, bf16[128,2048]{1,0:T(8,128)(2,1)S(1)}, u32[]{:S(2)}, u32[]{:S(2)}) collective-permute-start(bf16[128,2048]{1,0:T(8,128)(2,1)} %get-tuple-element.43), channel_id=1, source_target_pairs={{0,4},{4,0},{8,12},{12,8},{16,20},{20,16},{24,28},{28,24},{1,5},{5... | collective-permute-start | bytes 1572872 | tf_op jit(solution)/shard_map/ppermute | solution.py:36
  15.2 0.0 copy-start
  15.2 3.5 %collective-permute-start.2 = (bf16[128,2048]{1,0:T(8,128)(2,1)}, bf16[128,2048]{1,0:T(8,128)(2,1)S(1)}, u32[]{:S(2)}, u32[]{:S(2)}) collective-permute-start(bf16[128,2048]{1,0:T(8,128)(2,1)} %get-tuple-element.47.k0.v0), channel_id=1, source_target_pairs={{0,8},{4,12},{8,16},{12,20},{16,24},{20,28},{1,9},{5,13},{9,17},{1... | collective-permute-start | bytes 1572872 | tf_op jit(solution)/shard_map/ppermute | solution.py:31
  18.8 2.2 %halves.2 = (bf16[128,2048]{1,0:T(8,128)(2,1)}, bf16[128,2048]{1,0:T(8,128)(2,1)}) custom-call(s32[1]{0:T(128)} %bitcast.where, bf16[128,2048]{1,0:T(8,128)(2,1)} %one.2, bf16[128,2048]{1,0:T(8,128)(2,1)} %two.2), custom_call_target="tpu_custom_call" | custom-call | bytes 2097152 | tf_op jit(solution)/shard_map/halves/pallas_call | solution.py:63
  21.0 1.3 %collective-permute-start.6 = (bf16[128,2048]{1,0:T(8,128)(2,1)}, bf16[128,2048]{1,0:T(8,128)(2,1)}, u32[]{:S(2)}, u32[]{:S(2)}) collective-permute-start(bf16[128,2048]{1,0:T(8,128)(2,1)} %get-tuple-element.42.qo.do_o), channel_id=1, source_target_pairs={{8,0},{12,4},{16,8},{20,12},{24,16},{28,20},{9,1},{13,5},{17,9},{2... | collective-permute-start | bytes 1572872 | tf_op jit(solution)/shard_map/ppermute | solution.py:31
  22.3 0.0 copy-start.4
  22.4 0.6 copy-done.4
  23.0 0.1 fusion.5
  23.1 0.1 copy.21
  23.3 0.0 copy-start.5
  23.3 0.6 broadcast.61
  23.9 0.1 copy-done.5
  23.9 0.7 reduce.3
  24.6 0.1 eq.21
  24.7 0.1 pad_add_fusion
  24.7 0.2 convert_reduce_fusion
  25.0 10.8 %collective-permute-done.k1.v1 = bf16[128,2048]{1,0:T(8,128)(2,1)S(1)} collective-permute-done((bf16[128,2048]{1,0:T(8,128)(2,1)}, bf16[128,2048]{1,0:T(8,128)(2,1)S(1)}, u32[]{:S(2)}, u32[]{:S(2)}) %collective-permute-start) | collective-permute-done | bytes 524320 | tf_op jit(solution)/shard_map/ppermute | solution.py:36
  35.8 0.0 collective-permute-start.1
  35.8 4.7 %collective-permute-start.3 = (bf16[128,2048]{1,0:T(8,128)(2,1)S(1)}, bf16[128,2048]{1,0:T(8,128)(2,1)}, u32[]{:S(2)}, u32[]{:S(2)}) collective-permute-start(bf16[128,2048]{1,0:T(8,128)(2,1)S(1)} %collective-permute-done.k1.v1), channel_id=1, source_target_pairs={{0,8},{4,12},{8,16},{12,20},{16,24},{20,28},{1,9},{5,13},{9,17},{1... | collective-permute-start | bytes 1572872 | tf_op jit(solution)/shard_map/ppermute | solution.py:31
  40.5 0.1 fusion
  40.6 0.1 broadcast_in_dim.38
  40.7 0.1 reshape.77.mbias
  40.8 8.3 %collective-permute-done.1.qf.do_f = bf16[128,2048]{1,0:T(8,128)(2,1)S(1)} collective-permute-done((bf16[128,2048]{1,0:T(8,128)(2,1)}, bf16[128,2048]{1,0:T(8,128)(2,1)S(1)}, u32[]{:S(2)}, u32[]{:S(2)}) %collective-permute-start.1) | collective-permute-done | bytes 524320 | tf_op jit(solution)/shard_map/ppermute | solution.py:36
  49.1 1.3 %collective-permute-start.7 = (bf16[128,2048]{1,0:T(8,128)(2,1)S(1)}, bf16[128,2048]{1,0:T(8,128)(2,1)}, u32[]{:S(2)}, u32[]{:S(2)}) collective-permute-start(bf16[128,2048]{1,0:T(8,128)(2,1)S(1)} %collective-permute-done.1.qf.do_f), channel_id=1, source_target_pairs={{8,0},{12,4},{16,8},{20,12},{24,16},{28,20},{9,1},{13,5},{17,9},{2... | collective-permute-start | bytes 1572872 | tf_op jit(solution)/shard_map/ppermute | solution.py:31
  50.4 0.0 all-to-all-done
  50.4 0.0 copy-done
  50.4 0.0 copy-start.1
  50.5 1.0 %copy-done.1 = bf16[128,2048]{1,0:T(8,128)(2,1)S(1)} copy-done((bf16[128,2048]{1,0:T(8,128)(2,1)S(1)}, bf16[128,2048]{1,0:T(8,128)(2,1)}, u32[]{:S(2)}) %copy-start.1) | copy-done | bytes 524312
  51.5 3.3 %attend_near.1 = (f32[256,1024]{1,0:T(8,128)S(1)}, f32[256,1024]{1,0:T(8,128)S(1)}, f32[256,1024]{1,0:T(8,128)S(1)}) custom-call(bf16[128,2048]{1,0:T(8,128)(2,1)S(1)} %copy-done.1, bf16[128,2048]{1,0:T(8,128)(2,1)S(1)} %collective-permute-done.1.qf.do_f, bf16[128,2048]{1,0:T(8,128)(2,1)S(1)} %copy-done, bf16[128,2048]{1,0:T(8,128)(2,1)S(1)} %collective-permute-done.k1.v1, ...), custom_call_target="tpu_custom_call" | custom-call | flops 402653184 | bytes 3145728 | tf_op jit(solution)/shard_map/attend_near/pallas_call | solution.py:220
  54.8 0.0 collective-permute-done.2.k0.v0.k2.v2
  54.9 0.0 collective-permute-done.3.k1.v1.k3.v3
  54.9 3.7 %attend_prev.1 = (bf16[128,1024]{1,0:T(8,128)(2,1)S(1)}, bf16[128,1024]{1,0:T(8,128)(2,1)S(1)}, f32[256,1024]{1,0:T(8,128)S(1)}, f32[256,1024]{1,0:T(8,128)S(1)}, f32[2,8,256]{2,1,0:T(8,128)S(1)}) custom-call(bf16[128,2048]{1,0:T(8,128)(2,1)S(1)} %copy-done.1, bf16[128,2048]{1,0:T(8,128)(2,1)S(1)} %collective-permute-done.1.qf.do_f, ...), custom_call_target="tpu_custom_call" | custom-call | flops 268435456 | bytes 4194304 | tf_op jit(solution)/shard_map/attend_prev/pallas_call | solution.py:271
  58.6 0.3 collective-permute-start.5
  58.9 1.3 %collective-permute-start.4 = (f32[2,8,256]{2,1,0:T(8,128)S(1)}, f32[2,8,256]{2,1,0:T(8,128)S(1)}, u32[]{:S(2)}, u32[]{:S(2)}) collective-permute-start(f32[2,8,256]{2,1,0:T(8,128)S(1)} %get-tuple-element.57), channel_id=1, source_target_pairs={{8,0},{12,4},{16,8},{20,12},{24,16},{28,20},{9,1},{13,5},{17,9},{2... | collective-permute-start | bytes 49160 | tf_op jit(solution)/shard_map/ppermute | solution.py:31
  60.2 6.3 %own_gradients.1 = (f32[128,1024]{1,0:T(8,128)}, bf16[128,1024]{1,0:T(8,128)(2,1)S(1)}, f32[8,128]{1,0:T(8,128)S(1)}, f32[256,1024]{1,0:T(8,128)S(1)}, f32[256,1024]{1,0:T(8,128)S(1)}) custom-call(bf16[128,2048]{1,0:T(8,128)(2,1)S(1)} %copy-done.1, bf16[128,2048]{1,0:T(8,128)(2,1)S(1)} %collective-permute-done.1.qf.do_f, bf16[128,2048]{1,0:T(8,128)(2,1)S(1)} %copy-done.1, ...), custom_call_target="tpu_custom_call" | custom-call | flops 1275068416 | bytes 5767168 | tf_op jit(solution)/shard_map/own_gradients/pallas_call | solution.py:351
  66.5 0.1 collective-permute-done.4.stat
  66.7 0.0 collective-permute-done.5
  66.7 0.0 copy-start.3
  66.7 1.7 %collective-permute-start.8 = (bf16[128,1024]{1,0:T(8,128)(2,1)S(1)}, bf16[128,1024]{1,0:T(8,128)(2,1)S(1)}, u32[]{:S(2)}, u32[]{:S(2)}) collective-permute-start(bf16[128,1024]{1,0:T(8,128)(2,1)S(1)} %get-tuple-element.72), channel_id=1, source_target_pairs={{0,4},{4,0},{8,12},{12,8},{16,20},{20,16},{24,28},{28,24},{1,5},{5... | collective-permute-start | bytes 786440 | tf_op jit(solution)/shard_map/ppermute | solution.py:36
  68.4 0.0 collective-permute-done.6.qo.do_o
  68.4 0.0 collective-permute-done.7.qf.do_f
  68.4 4.1 %key_gradient_next.1 = (f32[128,1024]{1,0:T(8,128)S(1)}, f32[128,1024]{1,0:T(8,128)S(1)}, bf16[2,128,1024]{2,1,0:T(8,128)(2,1)}, f32[32,128]{1,0:T(8,128)}) custom-call(bf16[128,2048]{1,0:T(8,128)(2,1)} %collective-permute-done.6.qo.do_o, bf16[128,2048]{1,0:T(8,128)(2,1)} %collective-permute-done.7.qf.do_f, ...), custom_call_target="tpu_custom_call" | custom-call | flops 536870912 | bytes 6291456 | tf_op jit(solution)/shard_map/key_gradient_next/pallas_call | solution.py:429
  72.5 0.0 copy-done.3
  72.5 1.3 %collective-permute-done.8.dq_other = bf16[128,1024]{1,0:T(8,128)(2,1)S(1)} collective-permute-done((bf16[128,1024]{1,0:T(8,128)(2,1)S(1)}, bf16[128,1024]{1,0:T(8,128)(2,1)S(1)}, u32[]{:S(2)}, u32[]{:S(2)}) %collective-permute-start.8) | collective-permute-done | bytes 262176 | tf_op jit(solution)/shard_map/ppermute | solution.py:36
  73.7 1.0 %collective-permute-start.9 = (bf16[2,128,1024]{2,1,0:T(8,128)(2,1)}, bf16[2,128,1024]{2,1,0:T(8,128)(2,1)S(1)}, u32[]{:S(2)}, u32[]{:S(2)}) collective-permute-start(bf16[2,128,1024]{2,1,0:T(8,128)(2,1)} %get-tuple-element.76), channel_id=1, source_target_pairs={{0,4},{4,0},{8,12},{12,8},{16,20},{20,16},{24,28},{28,24},{1,5},{5... | collective-permute-start | bytes 1572872 | tf_op jit(solution)/shard_map/ppermute | solution.py:36
  74.7 10.5 %all-to-all-start.1 = ((f32[32,1,128]{2,1,0:T(1,128)}), f32[32,1,128]{2,1,0:T(1,128)S(1)}, u32[]{:S(2)}, u32[]{:S(2)}) async-start(f32[32,1,128]{2,1,0:T(1,128)} %bitcast.16), calls=%async_computation.1 | async-start | bytes 32768 | tf_op jit(solution)/shard_map/all_to_all | solution.py:551
  85.3 0.0 copy-start.2
  85.3 2.0 %maximum_select_fusion = bf16[128,2048]{1,0:T(8,128)(2,1)} fusion(bf16[128,1024]{1,0:T(8,128)(2,1)} %copy-done.3, bf16[128,1024]{1,0:T(8,128)(2,1)S(1)} %get-tuple-element.56, pred[]{:T(512)S(6)} %eq.20), kind=kLoop, calls=%fused_computation | loop fusion | flops 2359296 | bytes 1048577 | tf_op jit(solution)/shard_map/jit(_where)/select_n | solution.py:556
  87.3 5.1 %all-to-all-done.1 = f32[32,1,128]{2,1,0:T(1,128)S(1)} async-done(((f32[32,1,128]{2,1,0:T(1,128)}), f32[32,1,128]{2,1,0:T(1,128)S(1)}, u32[]{:S(2)}, u32[]{:S(2)}) %all-to-all-start.1) | async-done | bytes 16416 | tf_op jit(solution)/shard_map/all_to_all | solution.py:551
  92.4 0.0 collective-permute-done.9.other
  92.4 0.0 copy-done.2
  92.4 1.4 %scaled.1 = (bf16[128,2048]{1,0:T(8,128)(2,1)}, bf16[128,2048]{1,0:T(8,128)(2,1)}, bf16[128,2048]{1,0:T(8,128)(2,1)}) custom-call(s32[1]{0:T(128)} %bitcast.14.side_ref, f32[32,128]{1,0:T(8,128)S(1)} %bitcast.34, f32[128,1024]{1,0:T(8,128)S(1)} %copy-done.2, bf16[128,1024]{1,0:T(8,128)(2,1)S(1)} %collective-permute-done.8.dq_other, ...), custom_call_target="tpu_custom_call" | custom-call | flops 786432 | bytes 2621440 | tf_op jit(solution)/shard_map/scaled/pallas_call | solution.py:475
  (8 shorter events, 0.1 us)
Async XLA Ops:
  3.7 46.8 %all-to-all-start = ((bf16[8,32,2048]{2,1,0:T(8,128)(2,1)}), bf16[8,32,2048]{2,1,0:T(8,128)(2,1)S(1)}, u32[]{:S(2)}, u32[]{:S(2)}) async-start(bf16[8,32,2048]{2,1,0:T(8,128)(2,1)} %bitcast.35), calls=%async_computation | async-start | bytes 2097152 | tf_op jit(solution)/shard_map/all_to_all | solution.py:508
  13.2 22.6 %collective-permute-start = (bf16[128,2048]{1,0:T(8,128)(2,1)}, bf16[128,2048]{1,0:T(8,128)(2,1)S(1)}, u32[]{:S(2)}, u32[]{:S(2)}) collective-permute-start(bf16[128,2048]{1,0:T(8,128)(2,1)} %get-tuple-element.43), channel_id=1, source_target_pairs={{0,4},{4,0},{8,12},{12,8},{16,20},{20,16},{24,28},{28,24},{1,5},{5... | collective-permute-start | bytes 1572872 | tf_op jit(solution)/shard_map/ppermute | solution.py:36
  15.2 35.2 %copy-start = (bf16[128,2048]{1,0:T(8,128)(2,1)S(1)}, bf16[128,2048]{1,0:T(8,128)(2,1)}, u32[]{:S(2)}) copy-start(bf16[128,2048]{1,0:T(8,128)(2,1)} %get-tuple-element.47.k0.v0) | copy-start | bytes 1572868
  15.2 39.6 %collective-permute-start.2 = (bf16[128,2048]{1,0:T(8,128)(2,1)}, bf16[128,2048]{1,0:T(8,128)(2,1)S(1)}, u32[]{:S(2)}, u32[]{:S(2)}) collective-permute-start(bf16[128,2048]{1,0:T(8,128)(2,1)} %get-tuple-element.47.k0.v0), channel_id=1, source_target_pairs={{0,8},{4,12},{8,16},{12,20},{16,24},{20,28},{1,9},{5,13},{9,17},{1... | collective-permute-start | bytes 1572872 | tf_op jit(solution)/shard_map/ppermute | solution.py:31
  21.0 47.4 %collective-permute-start.6 = (bf16[128,2048]{1,0:T(8,128)(2,1)}, bf16[128,2048]{1,0:T(8,128)(2,1)}, u32[]{:S(2)}, u32[]{:S(2)}) collective-permute-start(bf16[128,2048]{1,0:T(8,128)(2,1)} %get-tuple-element.42.qo.do_o), channel_id=1, source_target_pairs={{8,0},{12,4},{16,8},{20,12},{24,16},{28,20},{9,1},{13,5},{17,9},{2... | collective-permute-start | bytes 1572872 | tf_op jit(solution)/shard_map/ppermute | solution.py:31
  22.3 0.7 copy-start.4
  23.3 0.7 copy-start.5
  35.8 13.3 %collective-permute-start.1 = (bf16[128,2048]{1,0:T(8,128)(2,1)}, bf16[128,2048]{1,0:T(8,128)(2,1)S(1)}, u32[]{:S(2)}, u32[]{:S(2)}) collective-permute-start(bf16[128,2048]{1,0:T(8,128)(2,1)} %get-tuple-element.45), channel_id=1, source_target_pairs={{0,4},{4,0},{8,12},{12,8},{16,20},{20,16},{24,28},{28,24},{1,5},{5... | collective-permute-start | bytes 1572872 | tf_op jit(solution)/shard_map/ppermute | solution.py:36
  35.8 19.1 %collective-permute-start.3 = (bf16[128,2048]{1,0:T(8,128)(2,1)S(1)}, bf16[128,2048]{1,0:T(8,128)(2,1)}, u32[]{:S(2)}, u32[]{:S(2)}) collective-permute-start(bf16[128,2048]{1,0:T(8,128)(2,1)S(1)} %collective-permute-done.k1.v1), channel_id=1, source_target_pairs={{0,8},{4,12},{8,16},{12,20},{16,24},{20,28},{1,9},{5,13},{9,17},{1... | collective-permute-start | bytes 1572872 | tf_op jit(solution)/shard_map/ppermute | solution.py:31
  49.1 19.2 %collective-permute-start.7 = (bf16[128,2048]{1,0:T(8,128)(2,1)S(1)}, bf16[128,2048]{1,0:T(8,128)(2,1)}, u32[]{:S(2)}, u32[]{:S(2)}) collective-permute-start(bf16[128,2048]{1,0:T(8,128)(2,1)S(1)} %collective-permute-done.1.qf.do_f), channel_id=1, source_target_pairs={{8,0},{12,4},{16,8},{20,12},{24,16},{28,20},{9,1},{13,5},{17,9},{2... | collective-permute-start | bytes 1572872 | tf_op jit(solution)/shard_map/ppermute | solution.py:31
  50.4 1.0 %copy-start.1 = (bf16[128,2048]{1,0:T(8,128)(2,1)S(1)}, bf16[128,2048]{1,0:T(8,128)(2,1)}, u32[]{:S(2)}) copy-start(bf16[128,2048]{1,0:T(8,128)(2,1)} %get-tuple-element.42.qo.do_o) | copy-start | bytes 1572868
  58.6 8.1 %collective-permute-start.5 = (bf16[128,1024]{1,0:T(8,128)(2,1)S(1)}, bf16[128,1024]{1,0:T(8,128)(2,1)S(1)}, u32[]{:S(2)}, u32[]{:S(2)}) collective-permute-start(bf16[128,1024]{1,0:T(8,128)(2,1)S(1)} %get-tuple-element.62), channel_id=1, source_target_pairs={{0,4},{4,0},{8,12},{12,8},{16,20},{20,16},{24,28},{28,24},{1,5},{5... | collective-permute-start | bytes 786440 | tf_op jit(solution)/shard_map/ppermute | solution.py:36
  58.9 7.7 %collective-permute-start.4 = (f32[2,8,256]{2,1,0:T(8,128)S(1)}, f32[2,8,256]{2,1,0:T(8,128)S(1)}, u32[]{:S(2)}, u32[]{:S(2)}) collective-permute-start(f32[2,8,256]{2,1,0:T(8,128)S(1)} %get-tuple-element.57), channel_id=1, source_target_pairs={{8,0},{12,4},{16,8},{20,12},{24,16},{28,20},{9,1},{13,5},{17,9},{2... | collective-permute-start | bytes 49160 | tf_op jit(solution)/shard_map/ppermute | solution.py:31
  66.7 5.8 %copy-start.3 = (bf16[128,1024]{1,0:T(8,128)(2,1)}, bf16[128,1024]{1,0:T(8,128)(2,1)S(1)}, u32[]{:S(2)}) copy-start(bf16[128,1024]{1,0:T(8,128)(2,1)S(1)} %collective-permute-done.5) | copy-start | bytes 786436
  66.7 7.1 %collective-permute-start.8 = (bf16[128,1024]{1,0:T(8,128)(2,1)S(1)}, bf16[128,1024]{1,0:T(8,128)(2,1)S(1)}, u32[]{:S(2)}, u32[]{:S(2)}) collective-permute-start(bf16[128,1024]{1,0:T(8,128)(2,1)S(1)} %get-tuple-element.72), channel_id=1, source_target_pairs={{0,4},{4,0},{8,12},{12,8},{16,20},{20,16},{24,28},{28,24},{1,5},{5... | collective-permute-start | bytes 786440 | tf_op jit(solution)/shard_map/ppermute | solution.py:36
  73.7 18.7 %collective-permute-start.9 = (bf16[2,128,1024]{2,1,0:T(8,128)(2,1)}, bf16[2,128,1024]{2,1,0:T(8,128)(2,1)S(1)}, u32[]{:S(2)}, u32[]{:S(2)}) collective-permute-start(bf16[2,128,1024]{2,1,0:T(8,128)(2,1)} %get-tuple-element.76), channel_id=1, source_target_pairs={{0,4},{4,0},{8,12},{12,8},{16,20},{20,16},{24,28},{28,24},{1,5},{5... | collective-permute-start | bytes 1572872 | tf_op jit(solution)/shard_map/ppermute | solution.py:36
  74.7 17.7 %all-to-all-start.1 = ((f32[32,1,128]{2,1,0:T(1,128)}), f32[32,1,128]{2,1,0:T(1,128)S(1)}, u32[]{:S(2)}, u32[]{:S(2)}) async-start(f32[32,1,128]{2,1,0:T(1,128)} %bitcast.16), calls=%async_computation.1 | async-start | bytes 32768 | tf_op jit(solution)/shard_map/all_to_all | solution.py:551
  85.3 7.1 %copy-start.2 = (f32[128,1024]{1,0:T(8,128)S(1)}, f32[128,1024]{1,0:T(8,128)}, u32[]{:S(2)}) copy-start(f32[128,1024]{1,0:T(8,128)} %get-tuple-element.70.dq) | copy-start | bytes 1572868

commit v5 on v4

--- a/solution.py
+++ b/solution.py
@@ -186,10 +186,10 @@
     return jnp.concatenate([column] * (like.shape[1] // column.shape[1]), axis=1)
 
 
-def attend_near(plan, own_qd, far_qd, kv, memory, key_row, query_col, memory_bias):
+def attend_near(plan, own_qd, far_qd, kv, memory, key_row, query_col, memory_bias, token):
     rows = plan.rows
 
-    def body(qo, qf, k0, k1, v0, v1, mk, mv, krow, qcol, mbias, mixed_out, top_out, total_out):
+    def body(qo, qf, k0, k1, v0, v1, mk, mv, krow, qcol, mbias, _, mixed_out, top_out, total_out):
         bias = visible_bias(krow[0:1, :], krow[1:2, :], qcol[:, 0:1], qcol[:, 1:2])
         for g in range(plan.group):
             lanes = slice(g * HDIM, (g + 1) * HDIM)
@@ -224,12 +224,13 @@
         in_specs=[plan.first()] * 4
         + [plan.second()] * 2
         + [plan.memory(0), plan.memory(1)]
-        + [plan.whole(key_row.shape), plan.whole(query_col.shape), plan.whole(memory_bias.shape)],
+        + [plan.whole(key_row.shape), plan.whole(query_col.shape), plan.whole(memory_bias.shape)]
+        + [plan.whole(token.shape)],
         out_specs=(plan.pair(),) * 3,
         cost_estimate=cost(flops, 12 * rows * plan.half * 2, 2 * rows * 3 * rows * plan.heads),
         compiler_params=pltpu.CompilerParams(vmem_limit_bytes=VMEM_BYTES),
         name="attend_near",
-    )(own_qd, far_qd, *kv, *kv, memory, memory, key_row, query_col, memory_bias)
+    )(own_qd, far_qd, *kv, *kv, memory, memory, key_row, query_col, memory_bias, token)
 
 
 def attend_prev(plan, own_qd, far_qd, kv, key_row, query_col, near):
@@ -501,8 +502,12 @@
     far_kv = swapped(sent_kv)
     prev_own_kv = shifted(own_kv, 2)
     next_own_qd = shifted(own_qd, -2)
+    token = prev_own_kv[:8, :128] + far_kv[:8, :128]
+    for _ in range(5):
+        token = lax.ppermute(token, "head", [(i, i ^ 1) for i in range(lax.axis_size("head"))])
     far_kv, sent_qd = lax.optimization_barrier((far_kv, sent_qd))
-    prev_far_kv = shifted(far_kv, 2)
+    relayed_kv, token = lax.optimization_barrier((far_kv, token))
+    prev_far_kv = shifted(relayed_kv, 2)
     far_qd = swapped(sent_qd)
     route_table = routes[:, 0].reshape(count, per_device)
     arrived = lax.all_to_all(
@@ -531,7 +536,7 @@
     )
     next_far_qd = shifted(far_qd, -2)
     kv = (own_kv, far_kv, prev_own_kv, prev_far_kv)
-    near = attend_near(plan, own_qd, far_qd, kv[:2], arrived, near_row, near_col, memory_bias)
+    near = attend_near(plan, own_qd, far_qd, kv[:2], arrived, near_row, near_col, memory_bias, token)
     att_own, att_far, level, delta, stat_row = attend_prev(
         plan, own_qd, far_qd, kv[2:], prev_row, near_col, near
     )

time: 94.3 us -> 91.8 us (0.973)
  waiting for transfers between devices: 25.7 us -> 21.1 us
  starting transfers between devices: 35 us -> 37.1 us
    ppermute x5, waiting for transfers between devices: 20.4 us -> 9.77 us  [swapped(): return lax.ppermute(value, 'ctx', [(i, i ^ 1) for i in range(count)])]
    ppermute x0 -> x5, waiting for transfers between devices: none -> 4.07 us  [on_device(): lax.ppermute(token, 'head', [(i, i ^ 1) for i in range(lax.axis_size('hea...]
    all_to_all x1, starting transfers between devices: 7.29 us -> 3.85 us  [on_device(): lax.all_to_all(packed.reshape(count, 2 * CAP * BLK, width), 'ctx', split_...]
    ppermute x5, starting transfers between devices: 12.1 us -> 15 us  [shifted(): return lax.ppermute(value, 'ctx', pairs)]
    ppermute x5, starting transfers between devices: 5.14 us -> 7.62 us  [swapped(): return lax.ppermute(value, 'ctx', [(i, i ^ 1) for i in range(count)])]
    ppermute x5, waiting for transfers between devices: 0.12 us -> 2.17 us  [shifted(): return lax.ppermute(value, 'ctx', pairs)]
  transfers between devices with their start and end apart: 12 -> 17, of which waited for: 5 -> 8; matrix products, arithmetic and copies ran while one was open for 4% -> 4% of each run, Pallas kernels for 23% -> 25%
where the time goes in v5:
time: 91.8 us; the launch traced here: 91.3 us
  starting transfers between devices  37.1 us (40%)
  Pallas kernels  26.3 us (29%)
  waiting for transfers between devices  21.1 us (23%)
  other arithmetic  3.15 us (3%)
  local copies, waits for them, and re-layouts  2.72 us (3%)
    ppermute x5, starting transfers between devices, shifted(): return lax.ppermute(value, 'ctx', pairs)  15 us
    all_to_all x1, starting transfers between devices, on_device(): lax.all_to_all(share, ('ctx', 'head'), split_axis=0, concat_axis=0, tiled...  9.83 us
    ppermute x5, waiting for transfers between devices, swapped(): return lax.ppermute(value, 'ctx', [(i, i ^ 1) for i in range(count)])  9.77 us
    ppermute x5, starting transfers between devices, swapped(): return lax.ppermute(value, 'ctx', [(i, i ^ 1) for i in range(count)])  7.62 us
    pallas_call x1, Pallas kernels, own_gradients(): pl.pallas_call(body, grid=(plan.steps,), out_shape=(pltpu.HBM((rows, plan...  6.33 us
    all_to_all x1, waiting for transfers between devices, on_device(): lax.all_to_all(share, ('ctx', 'head'), split_axis=0, concat_axis=0, tiled...  5.12 us
    pallas_call x2, Pallas kernels, halves(): pl.pallas_call(body, out_shape=(jax.ShapeDtypeStruct((rows, width), BF16)...  4.44 us
    pallas_call x1, Pallas kernels, key_gradient_next(): pl.pallas_call(body, grid=(plan.steps,), out_shape=(jax.ShapeDtypeStruct(...  4.1 us
  transfers between devices with their start and end apart: 17, of which 8 were waited for; matrix products, arithmetic and copies ran while one was open for 4% of the time, Pallas kernels for 25%

profile of v5, /device:TPU:0, one launch (start us, length us, event | category | flops | bytes accessed | tf_op | source)
XLA Modules:
  0.0 91.3 jit_solution(16721070458698816813)
XLA Ops:
  0.6 2.2 %halves.3 = (bf16[128,2048]{1,0:T(8,128)(2,1)}, bf16[128,2048]{1,0:T(8,128)(2,1)}) custom-call(s32[1]{0:T(128)} %bitcast.where, bf16[128,2048]{1,0:T(8,128)(2,1)} %one.3, bf16[128,2048]{1,0:T(8,128)(2,1)} %two.3), custom_call_target="tpu_custom_call" | custom-call | bytes 2097152 | tf_op jit(solution)/shard_map/halves/pallas_call | solution.py:63
  2.8 3.0 %collective-permute-start = (bf16[128,2048]{1,0:T(8,128)(2,1)}, bf16[128,2048]{1,0:T(8,128)(2,1)S(1)}, u32[]{:S(2)}, u32[]{:S(2)}) collective-permute-start(bf16[128,2048]{1,0:T(8,128)(2,1)} %get-tuple-element.45), channel_id=1, source_target_pairs={{0,4},{4,0},{8,12},{12,8},{16,20},{20,16},{24,28},{28,24},{1,5},{5... | collective-permute-start | bytes 1572872 | tf_op jit(solution)/shard_map/ppermute | solution.py:36
  5.9 3.5 %collective-permute-start.2 = (bf16[128,2048]{1,0:T(8,128)(2,1)}, bf16[128,2048]{1,0:T(8,128)(2,1)S(1)}, u32[]{:S(2)}, u32[]{:S(2)}) collective-permute-start(bf16[128,2048]{1,0:T(8,128)(2,1)} %get-tuple-element.49.k0.v0), channel_id=1, source_target_pairs={{0,8},{4,12},{8,16},{12,20},{16,24},{20,28},{1,9},{5,13},{9,17},{1... | collective-permute-start | bytes 1572872 | tf_op jit(solution)/shard_map/ppermute | solution.py:31
  9.4 3.0 %pack_memory.1 = bf16[8,2,2,8,2048]{4,3,2,1,0:T(8,128)(2,1)} custom-call(s32[1]{0:T(128)} %bitcast.where, s32[96]{0:T(128)} %bitcast.38, bf16[12,8,2048]{2,1,0:T(8,128)(2,1)} %bitcast.36, bf16[12,8,2048]{2,1,0:T(8,128)(2,1)} %bitcast.37), custom_call_target="tpu_custom_call" | custom-call | bytes 1572864 | tf_op jit(solution)/shard_map/pack_memory/pallas_call | solution.py:111
  12.4 3.8 %all-to-all-start = ((bf16[8,32,2048]{2,1,0:T(8,128)(2,1)}), bf16[8,32,2048]{2,1,0:T(8,128)(2,1)S(1)}, u32[]{:S(2)}, u32[]{:S(2)}) async-start(bf16[8,32,2048]{2,1,0:T(8,128)(2,1)} %bitcast.35), calls=%async_computation | async-start | bytes 2097152 | tf_op jit(solution)/shard_map/all_to_all | solution.py:513
  16.3 0.0 copy-start
  16.3 2.3 %halves.2 = (bf16[128,2048]{1,0:T(8,128)(2,1)}, bf16[128,2048]{1,0:T(8,128)(2,1)}) custom-call(s32[1]{0:T(128)} %bitcast.where, bf16[128,2048]{1,0:T(8,128)(2,1)} %one.2, bf16[128,2048]{1,0:T(8,128)(2,1)} %two.2), custom_call_target="tpu_custom_call" | custom-call | bytes 2097152 | tf_op jit(solution)/shard_map/halves/pallas_call | solution.py:63
  18.5 1.3 %collective-permute-start.11 = (bf16[128,2048]{1,0:T(8,128)(2,1)}, bf16[128,2048]{1,0:T(8,128)(2,1)}, u32[]{:S(2)}, u32[]{:S(2)}) collective-permute-start(bf16[128,2048]{1,0:T(8,128)(2,1)} %get-tuple-element.44.qo.do_o), channel_id=1, source_target_pairs={{8,0},{12,4},{16,8},{20,12},{24,16},{28,20},{9,1},{13,5},{17,9},{2... | collective-permute-start | bytes 1572872 | tf_op jit(solution)/shard_map/ppermute | solution.py:31
  19.9 0.0 copy-start.5
  19.9 0.5 broadcast.61
  20.4 0.1 copy-done.5
  20.5 0.6 reduce.3
  21.2 0.1 eq.21
  21.3 0.0 copy-start.4
  21.3 0.1 pad_add_fusion
  21.3 0.6 copy-done.4
  21.9 0.1 fusion.5
  22.0 0.2 convert_reduce_fusion
  22.2 0.0 collective-permute-done.k1.v1
  22.3 0.0 collective-permute-done.2.k0.v0.k2.v2
  22.3 0.1 collective-permute-start.3
  22.4 1.1 %collective-permute-done.3 = bf16[8,128]{1,0:T(8,128)(2,1)S(1)} collective-permute-done((bf16[8,128]{1,0:T(8,128)(2,1)S(1)}, bf16[8,128]{1,0:T(8,128)(2,1)S(1)}, u32[]{:S(2)}, u32[]{:S(2)}) %collective-permute-start.3) | collective-permute-done | bytes 2080 | tf_op jit(solution)/shard_map/ppermute | solution.py:507
  23.5 0.2 collective-permute-start.4
  23.7 1.0 %collective-permute-done.4 = bf16[8,128]{1,0:T(8,128)(2,1)S(1)} collective-permute-done((bf16[8,128]{1,0:T(8,128)(2,1)S(1)}, bf16[8,128]{1,0:T(8,128)(2,1)S(1)}, u32[]{:S(2)}, u32[]{:S(2)}) %collective-permute-start.4) | collective-permute-done | bytes 2080 | tf_op jit(solution)/shard_map/ppermute | solution.py:507
  24.7 0.2 collective-permute-start.5
  24.8 1.0 %collective-permute-done.5 = bf16[8,128]{1,0:T(8,128)(2,1)S(1)} collective-permute-done((bf16[8,128]{1,0:T(8,128)(2,1)S(1)}, bf16[8,128]{1,0:T(8,128)(2,1)S(1)}, u32[]{:S(2)}, u32[]{:S(2)}) %collective-permute-start.5) | collective-permute-done | bytes 2080 | tf_op jit(solution)/shard_map/ppermute | solution.py:507
  25.8 0.2 collective-permute-start.6
  26.0 1.0 %collective-permute-done.6 = bf16[8,128]{1,0:T(8,128)(2,1)S(1)} collective-permute-done((bf16[8,128]{1,0:T(8,128)(2,1)S(1)}, bf16[8,128]{1,0:T(8,128)(2,1)S(1)}, u32[]{:S(2)}, u32[]{:S(2)}) %collective-permute-start.6) | collective-permute-done | bytes 2080 | tf_op jit(solution)/shard_map/ppermute | solution.py:507
  27.0 0.2 collective-permute-start.7
  27.2 0.1 copy.21
  27.3 2.1 %collective-permute-start.1 = (bf16[128,2048]{1,0:T(8,128)(2,1)}, bf16[128,2048]{1,0:T(8,128)(2,1)S(1)}, u32[]{:S(2)}, u32[]{:S(2)}) collective-permute-start(bf16[128,2048]{1,0:T(8,128)(2,1)} %get-tuple-element.47), channel_id=1, source_target_pairs={{0,4},{4,0},{8,12},{12,8},{16,20},{20,16},{24,28},{28,24},{1,5},{5... | collective-permute-start | bytes 1572872 | tf_op jit(solution)/shard_map/ppermute | solution.py:36
  29.4 0.0 collective-permute-done.7._
  29.4 7.6 %collective-permute-start.8 = (bf16[128,2048]{1,0:T(8,128)(2,1)S(1)}, bf16[128,2048]{1,0:T(8,128)(2,1)}, u32[]{:S(2)}, u32[]{:S(2)}) collective-permute-start(bf16[128,2048]{1,0:T(8,128)(2,1)S(1)} %collective-permute-done.k1.v1), channel_id=1, source_target_pairs={{0,8},{4,12},{8,16},{12,20},{16,24},{20,28},{1,9},{5,13},{9,17},{1... | collective-permute-start | bytes 1572872 | tf_op jit(solution)/shard_map/ppermute | solution.py:31
  37.0 0.1 fusion
  37.1 0.1 broadcast_in_dim.38
  37.2 0.1 reshape.77.mbias
  37.3 7.4 %collective-permute-done.1.qf.do_f = bf16[128,2048]{1,0:T(8,128)(2,1)S(1)} collective-permute-done((bf16[128,2048]{1,0:T(8,128)(2,1)}, bf16[128,2048]{1,0:T(8,128)(2,1)S(1)}, u32[]{:S(2)}, u32[]{:S(2)}) %collective-permute-start.1) | collective-permute-done | bytes 524320 | tf_op jit(solution)/shard_map/ppermute | solution.py:36
  44.8 1.3 %collective-permute-start.12 = (bf16[128,2048]{1,0:T(8,128)(2,1)S(1)}, bf16[128,2048]{1,0:T(8,128)(2,1)}, u32[]{:S(2)}, u32[]{:S(2)}) collective-permute-start(bf16[128,2048]{1,0:T(8,128)(2,1)S(1)} %collective-permute-done.1.qf.do_f), channel_id=1, source_target_pairs={{8,0},{12,4},{16,8},{20,12},{24,16},{28,20},{9,1},{13,5},{17,9},{2... | collective-permute-start | bytes 1572872 | tf_op jit(solution)/shard_map/ppermute | solution.py:31
  46.0 0.0 all-to-all-done
  46.1 0.0 copy-done
  46.1 0.0 copy-start.1
  46.1 1.0 %copy-done.1 = bf16[128,2048]{1,0:T(8,128)(2,1)S(1)} copy-done((bf16[128,2048]{1,0:T(8,128)(2,1)S(1)}, bf16[128,2048]{1,0:T(8,128)(2,1)}, u32[]{:S(2)}) %copy-start.1) | copy-done | bytes 524312
  47.1 3.3 %attend_near.1 = (f32[256,1024]{1,0:T(8,128)S(1)}, f32[256,1024]{1,0:T(8,128)S(1)}, f32[256,1024]{1,0:T(8,128)S(1)}) custom-call(bf16[128,2048]{1,0:T(8,128)(2,1)S(1)} %copy-done.1, bf16[128,2048]{1,0:T(8,128)(2,1)S(1)} %collective-permute-done.1.qf.do_f, bf16[128,2048]{1,0:T(8,128)(2,1)S(1)} %copy-done, bf16[128,2048]{1,0:T(8,128)(2,1)S(1)} %collective-permute-done.k1.v1, ...), custom_call_target="tpu_custom_call" | custom-call | flops 402653184 | bytes 3145728 | tf_op jit(solution)/shard_map/attend_near/pallas_call | solution.py:220
  50.5 0.0 collective-permute-done.8.k1.v1.k3.v3
  50.5 3.7 %attend_prev.1 = (bf16[128,1024]{1,0:T(8,128)(2,1)S(1)}, bf16[128,1024]{1,0:T(8,128)(2,1)S(1)}, f32[256,1024]{1,0:T(8,128)S(1)}, f32[256,1024]{1,0:T(8,128)S(1)}, f32[2,8,256]{2,1,0:T(8,128)S(1)}) custom-call(bf16[128,2048]{1,0:T(8,128)(2,1)S(1)} %copy-done.1, bf16[128,2048]{1,0:T(8,128)(2,1)S(1)} %collective-permute-done.1.qf.do_f, ...), custom_call_target="tpu_custom_call" | custom-call | flops 268435456 | bytes 4194304 | tf_op jit(solution)/shard_map/attend_prev/pallas_call | solution.py:272
  54.2 0.5 collective-permute-start.10
  54.6 1.3 %collective-permute-start.9 = (f32[2,8,256]{2,1,0:T(8,128)S(1)}, f32[2,8,256]{2,1,0:T(8,128)S(1)}, u32[]{:S(2)}, u32[]{:S(2)}) collective-permute-start(f32[2,8,256]{2,1,0:T(8,128)S(1)} %get-tuple-element.61), channel_id=1, source_target_pairs={{8,0},{12,4},{16,8},{20,12},{24,16},{28,20},{9,1},{13,5},{17,9},{2... | collective-permute-start | bytes 49160 | tf_op jit(solution)/shard_map/ppermute | solution.py:31
  55.9 6.3 %own_gradients.1 = (f32[128,1024]{1,0:T(8,128)}, bf16[128,1024]{1,0:T(8,128)(2,1)S(1)}, f32[8,128]{1,0:T(8,128)S(1)}, f32[256,1024]{1,0:T(8,128)S(1)}, f32[256,1024]{1,0:T(8,128)S(1)}) custom-call(bf16[128,2048]{1,0:T(8,128)(2,1)S(1)} %copy-done.1, bf16[128,2048]{1,0:T(8,128)(2,1)S(1)} %collective-permute-done.1.qf.do_f, bf16[128,2048]{1,0:T(8,128)(2,1)S(1)} %copy-done.1, ...), custom_call_target="tpu_custom_call" | custom-call | flops 1275068416 | bytes 5767168 | tf_op jit(solution)/shard_map/own_gradients/pallas_call | solution.py:352
  62.3 2.2 %collective-permute-done.9.stat = f32[2,8,256]{2,1,0:T(8,128)S(1)} collective-permute-done((f32[2,8,256]{2,1,0:T(8,128)S(1)}, f32[2,8,256]{2,1,0:T(8,128)S(1)}, u32[]{:S(2)}, u32[]{:S(2)}) %collective-permute-start.9) | collective-permute-done | bytes 16416 | tf_op jit(solution)/shard_map/ppermute | solution.py:31
  64.4 0.0 collective-permute-done.10
  64.4 1.4 %collective-permute-start.13 = (bf16[128,1024]{1,0:T(8,128)(2,1)S(1)}, bf16[128,1024]{1,0:T(8,128)(2,1)S(1)}, u32[]{:S(2)}, u32[]{:S(2)}) collective-permute-start(bf16[128,1024]{1,0:T(8,128)(2,1)S(1)} %get-tuple-element.76), channel_id=1, source_target_pairs={{0,4},{4,0},{8,12},{12,8},{16,20},{20,16},{24,28},{28,24},{1,5},{5... | collective-permute-start | bytes 786440 | tf_op jit(solution)/shard_map/ppermute | solution.py:36
  65.8 0.0 collective-permute-done.11.qo.do_o
  65.8 0.0 collective-permute-done.12.qf.do_f
  65.8 4.1 %key_gradient_next.1 = (f32[128,1024]{1,0:T(8,128)S(1)}, f32[128,1024]{1,0:T(8,128)S(1)}, bf16[2,128,1024]{2,1,0:T(8,128)(2,1)}, f32[32,128]{1,0:T(8,128)}) custom-call(bf16[128,2048]{1,0:T(8,128)(2,1)} %collective-permute-done.11.qo.do_o, bf16[128,2048]{1,0:T(8,128)(2,1)} %collective-permute-done.12.qf.do_f, ...), custom_call_target="tpu_custom_call" | custom-call | flops 536870912 | bytes 6291456 | tf_op jit(solution)/shard_map/key_gradient_next/pallas_call | solution.py:430
  69.9 0.0 copy-done.3
  69.9 2.3 %collective-permute-done.13.dq_other = bf16[128,1024]{1,0:T(8,128)(2,1)S(1)} collective-permute-done((bf16[128,1024]{1,0:T(8,128)(2,1)S(1)}, bf16[128,1024]{1,0:T(8,128)(2,1)S(1)}, u32[]{:S(2)}, u32[]{:S(2)}) %collective-permute-start.13) | collective-permute-done | bytes 262176 | tf_op jit(solution)/shard_map/ppermute | solution.py:36
  72.3 0.7 collective-permute-start.14
  72.9 9.8 %all-to-all-start.1 = ((f32[32,1,128]{2,1,0:T(1,128)}), f32[32,1,128]{2,1,0:T(1,128)S(1)}, u32[]{:S(2)}, u32[]{:S(2)}) async-start(f32[32,1,128]{2,1,0:T(1,128)} %bitcast.16), calls=%async_computation.1 | async-start | bytes 32768 | tf_op jit(solution)/shard_map/all_to_all | solution.py:556
  82.8 0.0 copy-start.2
  82.8 2.0 %maximum_select_fusion = bf16[128,2048]{1,0:T(8,128)(2,1)} fusion(bf16[128,1024]{1,0:T(8,128)(2,1)} %copy-done.3, bf16[128,1024]{1,0:T(8,128)(2,1)S(1)} %get-tuple-element.60, pred[]{:T(512)S(6)} %eq.20), kind=kLoop, calls=%fused_computation | loop fusion | flops 2359296 | bytes 1048577 | tf_op jit(solution)/shard_map/jit(_where)/select_n | solution.py:561
  84.8 5.1 %all-to-all-done.1 = f32[32,1,128]{2,1,0:T(1,128)S(1)} async-done(((f32[32,1,128]{2,1,0:T(1,128)}), f32[32,1,128]{2,1,0:T(1,128)S(1)}, u32[]{:S(2)}, u32[]{:S(2)}) %all-to-all-start.1) | async-done | bytes 16416 | tf_op jit(solution)/shard_map/all_to_all | solution.py:556
  89.9 0.0 collective-permute-done.14.other
  89.9 0.0 copy-done.2
  89.9 1.4 %scaled.1 = (bf16[128,2048]{1,0:T(8,128)(2,1)}, bf16[128,2048]{1,0:T(8,128)(2,1)}, bf16[128,2048]{1,0:T(8,128)(2,1)}) custom-call(s32[1]{0:T(128)} %bitcast.14.side_ref, f32[32,128]{1,0:T(8,128)S(1)} %bitcast.34, f32[128,1024]{1,0:T(8,128)S(1)} %copy-done.2, bf16[128,1024]{1,0:T(8,128)(2,1)S(1)} %collective-permute-done.13.dq_other, ...), custom_call_target="tpu_custom_call" | custom-call | flops 786432 | bytes 2621440 | tf_op jit(solution)/shard_map/scaled/pallas_call | solution.py:476
  (10 shorter events, 0.1 us)
Async XLA Ops:
  2.8 19.4 %collective-permute-start = (bf16[128,2048]{1,0:T(8,128)(2,1)}, bf16[128,2048]{1,0:T(8,128)(2,1)S(1)}, u32[]{:S(2)}, u32[]{:S(2)}) collective-permute-start(bf16[128,2048]{1,0:T(8,128)(2,1)} %get-tuple-element.45), channel_id=1, source_target_pairs={{0,4},{4,0},{8,12},{12,8},{16,20},{20,16},{24,28},{28,24},{1,5},{5... | collective-permute-start | bytes 1572872 | tf_op jit(solution)/shard_map/ppermute | solution.py:36
  5.9 16.4 %collective-permute-start.2 = (bf16[128,2048]{1,0:T(8,128)(2,1)}, bf16[128,2048]{1,0:T(8,128)(2,1)S(1)}, u32[]{:S(2)}, u32[]{:S(2)}) collective-permute-start(bf16[128,2048]{1,0:T(8,128)(2,1)} %get-tuple-element.49.k0.v0), channel_id=1, source_target_pairs={{0,8},{4,12},{8,16},{12,20},{16,24},{20,28},{1,9},{5,13},{9,17},{1... | collective-permute-start | bytes 1572872 | tf_op jit(solution)/shard_map/ppermute | solution.py:31
  12.4 33.6 %all-to-all-start = ((bf16[8,32,2048]{2,1,0:T(8,128)(2,1)}), bf16[8,32,2048]{2,1,0:T(8,128)(2,1)S(1)}, u32[]{:S(2)}, u32[]{:S(2)}) async-start(bf16[8,32,2048]{2,1,0:T(8,128)(2,1)} %bitcast.35), calls=%async_computation | async-start | bytes 2097152 | tf_op jit(solution)/shard_map/all_to_all | solution.py:513
  16.3 29.8 %copy-start = (bf16[128,2048]{1,0:T(8,128)(2,1)S(1)}, bf16[128,2048]{1,0:T(8,128)(2,1)}, u32[]{:S(2)}) copy-start(bf16[128,2048]{1,0:T(8,128)(2,1)} %get-tuple-element.49.k0.v0) | copy-start | bytes 1572868
  18.5 47.3 %collective-permute-start.11 = (bf16[128,2048]{1,0:T(8,128)(2,1)}, bf16[128,2048]{1,0:T(8,128)(2,1)}, u32[]{:S(2)}, u32[]{:S(2)}) collective-permute-start(bf16[128,2048]{1,0:T(8,128)(2,1)} %get-tuple-element.44.qo.do_o), channel_id=1, source_target_pairs={{8,0},{12,4},{16,8},{20,12},{24,16},{28,20},{9,1},{13,5},{17,9},{2... | collective-permute-start | bytes 1572872 | tf_op jit(solution)/shard_map/ppermute | solution.py:31
  19.9 0.7 copy-start.5
  21.3 0.7 copy-start.4
  22.3 1.2 %collective-permute-start.3 = (bf16[8,128]{1,0:T(8,128)(2,1)S(1)}, bf16[8,128]{1,0:T(8,128)(2,1)S(1)}, u32[]{:S(2)}, u32[]{:S(2)}) collective-permute-start(bf16[8,128]{1,0:T(8,128)(2,1)S(1)} %slice_add_fusion), channel_id=1, source_target_pairs={{0,1},{1,0},{2,3},{3,2},{4,5},{5,4},{6,7},{7,6},{8,9},{9,8},{10,11... | collective-permute-start | bytes 6152 | tf_op jit(solution)/shard_map/ppermute | solution.py:507
  23.5 1.2 %collective-permute-start.4 = (bf16[8,128]{1,0:T(8,128)(2,1)S(1)}, bf16[8,128]{1,0:T(8,128)(2,1)S(1)}, u32[]{:S(2)}, u32[]{:S(2)}) collective-permute-start(bf16[8,128]{1,0:T(8,128)(2,1)S(1)} %collective-permute-done.3), channel_id=1, source_target_pairs={{0,1},{1,0},{2,3},{3,2},{4,5},{5,4},{6,7},{7,6},{8,9},{9,8},{10,11... | collective-permute-start | bytes 6152 | tf_op jit(solution)/shard_map/ppermute | solution.py:507
  24.7 1.2 %collective-permute-start.5 = (bf16[8,128]{1,0:T(8,128)(2,1)S(1)}, bf16[8,128]{1,0:T(8,128)(2,1)S(1)}, u32[]{:S(2)}, u32[]{:S(2)}) collective-permute-start(bf16[8,128]{1,0:T(8,128)(2,1)S(1)} %collective-permute-done.4), channel_id=1, source_target_pairs={{0,1},{1,0},{2,3},{3,2},{4,5},{5,4},{6,7},{7,6},{8,9},{9,8},{10,11... | collective-permute-start | bytes 6152 | tf_op jit(solution)/shard_map/ppermute | solution.py:507
  25.8 1.2 %collective-permute-start.6 = (bf16[8,128]{1,0:T(8,128)(2,1)S(1)}, bf16[8,128]{1,0:T(8,128)(2,1)S(1)}, u32[]{:S(2)}, u32[]{:S(2)}) collective-permute-start(bf16[8,128]{1,0:T(8,128)(2,1)S(1)} %collective-permute-done.5), channel_id=1, source_target_pairs={{0,1},{1,0},{2,3},{3,2},{4,5},{5,4},{6,7},{7,6},{8,9},{9,8},{10,11... | collective-permute-start | bytes 6152 | tf_op jit(solution)/shard_map/ppermute | solution.py:507
  27.0 2.4 %collective-permute-start.7 = (bf16[8,128]{1,0:T(8,128)(2,1)S(1)}, bf16[8,128]{1,0:T(8,128)(2,1)S(1)}, u32[]{:S(2)}, u32[]{:S(2)}) collective-permute-start(bf16[8,128]{1,0:T(8,128)(2,1)S(1)} %collective-permute-done.6), channel_id=1, source_target_pairs={{0,1},{1,0},{2,3},{3,2},{4,5},{5,4},{6,7},{7,6},{8,9},{9,8},{10,11... | collective-permute-start | bytes 6152 | tf_op jit(solution)/shard_map/ppermute | solution.py:507
  27.3 17.5 %collective-permute-start.1 = (bf16[128,2048]{1,0:T(8,128)(2,1)}, bf16[128,2048]{1,0:T(8,128)(2,1)S(1)}, u32[]{:S(2)}, u32[]{:S(2)}) collective-permute-start(bf16[128,2048]{1,0:T(8,128)(2,1)} %get-tuple-element.47), channel_id=1, source_target_pairs={{0,4},{4,0},{8,12},{12,8},{16,20},{20,16},{24,28},{28,24},{1,5},{5... | collective-permute-start | bytes 1572872 | tf_op jit(solution)/shard_map/ppermute | solution.py:36
  29.4 21.1 %collective-permute-start.8 = (bf16[128,2048]{1,0:T(8,128)(2,1)S(1)}, bf16[128,2048]{1,0:T(8,128)(2,1)}, u32[]{:S(2)}, u32[]{:S(2)}) collective-permute-start(bf16[128,2048]{1,0:T(8,128)(2,1)S(1)} %collective-permute-done.k1.v1), channel_id=1, source_target_pairs={{0,8},{4,12},{8,16},{12,20},{16,24},{20,28},{1,9},{5,13},{9,17},{1... | collective-permute-start | bytes 1572872 | tf_op jit(solution)/shard_map/ppermute | solution.py:31
  44.8 21.1 %collective-permute-start.12 = (bf16[128,2048]{1,0:T(8,128)(2,1)S(1)}, bf16[128,2048]{1,0:T(8,128)(2,1)}, u32[]{:S(2)}, u32[]{:S(2)}) collective-permute-start(bf16[128,2048]{1,0:T(8,128)(2,1)S(1)} %collective-permute-done.1.qf.do_f), channel_id=1, source_target_pairs={{8,0},{12,4},{16,8},{20,12},{24,16},{28,20},{9,1},{13,5},{17,9},{2... | collective-permute-start | bytes 1572872 | tf_op jit(solution)/shard_map/ppermute | solution.py:31
  46.1 1.0 %copy-start.1 = (bf16[128,2048]{1,0:T(8,128)(2,1)S(1)}, bf16[128,2048]{1,0:T(8,128)(2,1)}, u32[]{:S(2)}) copy-start(bf16[128,2048]{1,0:T(8,128)(2,1)} %get-tuple-element.44.qo.do_o) | copy-start | bytes 1572868
  54.2 10.2 %collective-permute-start.10 = (bf16[128,1024]{1,0:T(8,128)(2,1)S(1)}, bf16[128,1024]{1,0:T(8,128)(2,1)S(1)}, u32[]{:S(2)}, u32[]{:S(2)}) collective-permute-start(bf16[128,1024]{1,0:T(8,128)(2,1)S(1)} %get-tuple-element.66), channel_id=1, source_target_pairs={{0,4},{4,0},{8,12},{12,8},{16,20},{20,16},{24,28},{28,24},{1,5},{5... | collective-permute-start | bytes 786440 | tf_op jit(solution)/shard_map/ppermute | solution.py:36
  54.6 9.8 %collective-permute-start.9 = (f32[2,8,256]{2,1,0:T(8,128)S(1)}, f32[2,8,256]{2,1,0:T(8,128)S(1)}, u32[]{:S(2)}, u32[]{:S(2)}) collective-permute-start(f32[2,8,256]{2,1,0:T(8,128)S(1)} %get-tuple-element.61), channel_id=1, source_target_pairs={{8,0},{12,4},{16,8},{20,12},{24,16},{28,20},{9,1},{13,5},{17,9},{2... | collective-permute-start | bytes 49160 | tf_op jit(solution)/shard_map/ppermute | solution.py:31
  64.4 5.5 %copy-start.3 = (bf16[128,1024]{1,0:T(8,128)(2,1)}, bf16[128,1024]{1,0:T(8,128)(2,1)S(1)}, u32[]{:S(2)}) copy-start(bf16[128,1024]{1,0:T(8,128)(2,1)S(1)} %collective-permute-done.10) | copy-start | bytes 786436
  64.4 7.8 %collective-permute-start.13 = (bf16[128,1024]{1,0:T(8,128)(2,1)S(1)}, bf16[128,1024]{1,0:T(8,128)(2,1)S(1)}, u32[]{:S(2)}, u32[]{:S(2)}) collective-permute-start(bf16[128,1024]{1,0:T(8,128)(2,1)S(1)} %get-tuple-element.76), channel_id=1, source_target_pairs={{0,4},{4,0},{8,12},{12,8},{16,20},{20,16},{24,28},{28,24},{1,5},{5... | collective-permute-start | bytes 786440 | tf_op jit(solution)/shard_map/ppermute | solution.py:36
  72.3 17.6 %collective-permute-start.14 = (bf16[2,128,1024]{2,1,0:T(8,128)(2,1)}, bf16[2,128,1024]{2,1,0:T(8,128)(2,1)S(1)}, u32[]{:S(2)}, u32[]{:S(2)}) collective-permute-start(bf16[2,128,1024]{2,1,0:T(8,128)(2,1)} %get-tuple-element.80), channel_id=1, source_target_pairs={{0,4},{4,0},{8,12},{12,8},{16,20},{20,16},{24,28},{28,24},{1,5},{5... | collective-permute-start | bytes 1572872 | tf_op jit(solution)/shard_map/ppermute | solution.py:36
  72.9 17.0 %all-to-all-start.1 = ((f32[32,1,128]{2,1,0:T(1,128)}), f32[32,1,128]{2,1,0:T(1,128)S(1)}, u32[]{:S(2)}, u32[]{:S(2)}) async-start(f32[32,1,128]{2,1,0:T(1,128)} %bitcast.16), calls=%async_computation.1 | async-start | bytes 32768 | tf_op jit(solution)/shard_map/all_to_all | solution.py:556
  82.8 7.2 %copy-start.2 = (f32[128,1024]{1,0:T(8,128)S(1)}, f32[128,1024]{1,0:T(8,128)}, u32[]{:S(2)}) copy-start(f32[128,1024]{1,0:T(8,128)} %get-tuple-element.74.dq) | copy-start | bytes 1572868

commit v6 on v5

--- a/solution.py
+++ b/solution.py
@@ -300,16 +300,12 @@
     )
 
 
-def dot_tn(a, b):
-    return lax.dot_general(a, b, (((0,), (0,)), ((), ())), preferred_element_type=F32)
-
-
-def own_gradients(plan, own_qd, far_qd, kv, memory, key_row, query_col, memory_bias, level, delta):
+def query_gradients(plan, own_qd, far_qd, kv, memory, key_row, query_col, memory_bias, level, delta):
     rows = plan.rows
 
     def body(
         qo, qf, do_o, do_f, k0, k1, k2, k3, v0, v1, v2, v3, mk, mv, krow, qcol, mbias,
-        level_in, delta_in, dq_own, dq_far, squares, dk, dv,
+        level_in, delta_in, dq_own, dq_far, squares,
     ):
         bias = visible_bias(krow[0:1, :], krow[1:2, :], qcol[:, 0:1], qcol[:, 1:2])
         acc = jnp.zeros((8, HDIM), F32)
@@ -338,8 +334,6 @@
             dq_own[:, lanes] = result[:rows]
             dq_far[:, lanes] = result[rows:].astype(BF16)
             acc = acc + jnp.sum((result * result).reshape(-1, 8, HDIM), axis=0)
-            dk[:, lanes] = dot_tn(grad[:, : 2 * rows], query) * plan.scale
-            dv[:, lanes] = dot_tn(prob[:, : 2 * rows].astype(BF16), upstream)
 
         @pl.when(pl.program_id(0) == 0)
         def _():
@@ -347,8 +341,7 @@
 
         squares[...] += acc
 
-    both = pl.BlockSpec((2 * rows, plan.cols), lambda i: (0, i))
-    flops = (3 * (4 * rows + plan.memory_rows) + 4 * rows) * 2 * (2 * rows) * plan.half
+    flops = 3 * (4 * rows + plan.memory_rows) * 2 * (2 * rows) * plan.half
     return pl.pallas_call(
         body,
         grid=(plan.steps,),
@@ -356,8 +349,6 @@
             pltpu.HBM((rows, plan.half), F32),
             jax.ShapeDtypeStruct((rows, plan.half), BF16),
             jax.ShapeDtypeStruct((8, HDIM), F32),
-            jax.ShapeDtypeStruct((2 * rows, plan.half), F32),
-            jax.ShapeDtypeStruct((2 * rows, plan.half), F32),
         ),
         in_specs=[plan.first()] * 2
         + [plan.second()] * 2
@@ -366,10 +357,10 @@
         + [plan.memory(0), plan.memory(1)]
         + [plan.whole(key_row.shape), plan.whole(query_col.shape), plan.whole(memory_bias.shape)]
         + [plan.pair()] * 2,
-        out_specs=(plan.first(), plan.first(), plan.whole((8, HDIM)), both, both),
-        cost_estimate=cost(flops, 22 * rows * plan.half * 2, 2 * rows * 5 * rows * plan.heads),
+        out_specs=(plan.first(), plan.first(), plan.whole((8, HDIM))),
+        cost_estimate=cost(flops, 14 * rows * plan.half * 2, 2 * rows * 5 * rows * plan.heads),
         compiler_params=pltpu.CompilerParams(vmem_limit_bytes=VMEM_BYTES),
-        name="own_gradients",
+        name="query_gradients",
     )(
         own_qd, far_qd, own_qd, far_qd, *kv, *kv, memory, memory, key_row, query_col, memory_bias,
         level, delta,
@@ -383,13 +374,11 @@
     return dot_nn(grad, query) * plan.scale, dot_nn(prob.astype(BF16), upstream)
 
 
-def key_gradient_next(
-    plan, own_qd, far_qd, own_kv, far_kv, query_row, key_col, stats, near_dk, near_dv, dq_squares, devices
-):
+def key_gradients(plan, qd, own_kv, far_kv, query_row, key_col, near_stats, next_stats, dq_squares, devices):
     rows = plan.rows
 
     def body(
-        qo, qf, do_o, do_f, k0, k1, v0, v1, qrow, kcol, stat, dk_in, dv_in, dq_sq,
+        q0, q1, q2, q3, do0, do1, do2, do3, k0, k1, v0, v1, qrow, kcol, stat0, stat1, dq_sq,
         dk_own, dv_own, send, share, squares,
     ):
         bias = visible_bias(kcol[:, 0:1], kcol[:, 1:2], qrow[0:1, :], qrow[1:2, :])
@@ -400,14 +389,14 @@
                 plan,
                 joined((k0, k1), lanes),
                 joined((v0, v1), lanes),
-                joined((qo, qf), lanes),
-                joined((do_o, do_f), lanes),
+                joined((q0, q1, q2, q3), lanes),
+                joined((do0, do1, do2, do3), lanes),
                 bias,
-                stat[0, g : g + 1, :],
-                stat[0, plan.group + g : plan.group + g + 1, :],
+                *[
+                    jnp.concatenate([stat0[0, n : n + 1, :], stat1[0, n : n + 1, :]], axis=1)
+                    for n in (g, plan.group + g)
+                ],
             )
-            key_part = key_part + dk_in[:, lanes]
-            value_part = value_part + dv_in[:, lanes]
             dk_own[:, lanes] = key_part[:rows]
             dv_own[:, lanes] = value_part[:rows]
             send[0, :, lanes] = key_part[rows:].astype(BF16)
@@ -426,33 +415,31 @@
             row = jnp.sum(squares[...], axis=0, keepdims=True)
             share[...] = jnp.broadcast_to(row, share.shape)
 
-    both = pl.BlockSpec((2 * rows, plan.cols), lambda i: (0, i))
+    stat = pl.BlockSpec((1, 8, 2 * rows), lambda i: (i, 0, 0))
     return pl.pallas_call(
         body,
         grid=(plan.steps,),
         out_shape=(
             jax.ShapeDtypeStruct((rows, plan.half), F32),
             jax.ShapeDtypeStruct((rows, plan.half), F32),
-            jax.ShapeDtypeStruct((2, rows, plan.half), BF16),
-            jax.ShapeDtypeStruct((devices, HDIM), F32),
+            pltpu.HBM((2, rows, plan.half), BF16),
+            pltpu.HBM((devices, HDIM), F32),
         ),
-        in_specs=[plan.first()] * 2
-        + [plan.second()] * 2
+        in_specs=[plan.first()] * 4
+        + [plan.second()] * 4
         + [plan.first()] * 2
         + [plan.second()] * 2
         + [plan.whole(query_row.shape), plan.whole(key_col.shape)]
-        + [pl.BlockSpec((1, 8, 2 * rows), lambda i: (i, 0, 0)), both, both]
-        + [plan.whole((8, HDIM))],
+        + [stat, stat, plan.whole((8, HDIM))],
         out_specs=(plan.first(), plan.first(), plan.stacked(), plan.whole((devices, HDIM))),
         scratch_shapes=[pltpu.VMEM((8, HDIM), F32)],
         cost_estimate=cost(
-            4 * 2 * (2 * rows) ** 2 * plan.half, 24 * rows * plan.half * 2, 4 * rows * rows * plan.heads
+            2 * 4 * 2 * (2 * rows) ** 2 * plan.half, 24 * rows * plan.half * 2, 8 * rows * rows * plan.heads
         ),
         compiler_params=pltpu.CompilerParams(vmem_limit_bytes=VMEM_BYTES),
-        name="key_gradient_next",
+        name="key_gradients",
     )(
-        own_qd, far_qd, own_qd, far_qd, own_kv, far_kv, own_kv, far_kv, query_row, key_col, stats,
-        near_dk, near_dv, dq_squares,
+        *qd, *qd, own_kv, far_kv, own_kv, far_kv, query_row, key_col, near_stats, next_stats, dq_squares,
     )
 
 
@@ -503,7 +490,7 @@
     prev_own_kv = shifted(own_kv, 2)
     next_own_qd = shifted(own_qd, -2)
     token = prev_own_kv[:8, :128] + far_kv[:8, :128]
-    for _ in range(5):
+    for _ in range(6):
         token = lax.ppermute(token, "head", [(i, i ^ 1) for i in range(lax.axis_size("head"))])
     far_kv, sent_qd = lax.optimization_barrier((far_kv, sent_qd))
     relayed_kv, token = lax.optimization_barrier((far_kv, token))
@@ -531,8 +518,9 @@
         jnp.where(live, 0.0, NEGATIVE)[..., None], (2, count, CAP, BLK)
     ).reshape(2, memory_rows)
 
-    far_qd, near_row, prev_row, next_row, key_row, near_col, memory_bias = lax.optimization_barrier(
-        (far_qd, near_row, prev_row, next_row, key_row, near_col, memory_bias)
+    query_row = jnp.concatenate([near_row, next_row], axis=1)
+    far_qd, near_row, prev_row, query_row, key_row, near_col, memory_bias = lax.optimization_barrier(
+        (far_qd, near_row, prev_row, query_row, key_row, near_col, memory_bias)
     )
     next_far_qd = shifted(far_qd, -2)
     kv = (own_kv, far_kv, prev_own_kv, prev_far_kv)
@@ -542,14 +530,14 @@
     )
     next_stats = shifted(stat_row, -2)
     att_back = swapped(att_far)
-    dq_own, dq_far, dq_squares, near_dk, near_dv = own_gradients(
+    dq_own, dq_far, dq_squares = query_gradients(
         plan, own_qd, far_qd, kv, arrived, key_row, near_col, memory_bias, level, delta
     )
     next_stats, dq_far, att_back = lax.optimization_barrier((next_stats, dq_far, att_back))
     dq_back = swapped(dq_far)
-    dk_own, dv_own, second_send, share = key_gradient_next(
-        plan, next_own_qd, next_far_qd, own_kv, far_kv, next_row, near_col, next_stats,
-        near_dk, near_dv, dq_squares, devices,
+    dk_own, dv_own, second_send, share = key_gradients(
+        plan, (own_qd, far_qd, next_own_qd, next_far_qd), own_kv, far_kv, query_row, near_col,
+        stat_row, next_stats, dq_squares, devices,
     )
     second_send, dq_back = lax.optimization_barrier((second_send, dq_back))
     second_back = swapped(second_send)

time: 91.8 us -> 91.7 us (level)
    ppermute x5, waiting for transfers between devices: 9.77 us -> 7.22 us  [swapped(): return lax.ppermute(value, 'ctx', [(i, i ^ 1) for i in range(count)])]
    ppermute x5, waiting for transfers between devices: 2.17 us -> 3.6 us  [shifted(): return lax.ppermute(value, 'ctx', pairs)]
    ppermute x5 -> x6, waiting for transfers between devices: 4.07 us -> 4.74 us  [on_device(): lax.ppermute(token, 'head', [(i, i ^ 1) for i in range(lax.axis_size('hea...]
    unnamed x13 -> x17, local copies, waits for them, and re-layouts: 2.32 us -> 2.61 us
  transfers between devices with their start and end apart: 17 -> 18, of which waited for: 8 -> 10; matrix products, arithmetic and copies ran while one was open for 4% -> 5% of each run, Pallas kernels for 25% -> 26%
where the time goes in v6:
time: 91.7 us; the launch traced here: 91.1 us
  starting transfers between devices  36.6 us (40%)
  Pallas kernels  26.8 us (29%)
  waiting for transfers between devices  20.7 us (23%)
  other arithmetic  3.16 us (3%)
  local copies, waits for them, and re-layouts  3.01 us (3%)
    ppermute x5, starting transfers between devices, shifted(): return lax.ppermute(value, 'ctx', pairs)  15.3 us
    all_to_all x1, starting transfers between devices, on_device(): lax.all_to_all(share, ('ctx', 'head'), split_axis=0, concat_axis=0, tiled...  9.22 us
    ppermute x5, starting transfers between devices, swapped(): return lax.ppermute(value, 'ctx', [(i, i ^ 1) for i in range(count)])  7.41 us
    ppermute x5, waiting for transfers between devices, swapped(): return lax.ppermute(value, 'ctx', [(i, i ^ 1) for i in range(count)])  7.22 us
    pallas_call x1, Pallas kernels, query_gradients(): pl.pallas_call(body, grid=(plan.steps,), out_shape=(pltpu.HBM((rows, plan...  5.67 us
    pallas_call x1, Pallas kernels, key_gradients(): pl.pallas_call(body, grid=(plan.steps,), out_shape=(jax.ShapeDtypeStruct(...  5.32 us
    all_to_all x1, waiting for transfers between devices, on_device(): lax.all_to_all(share, ('ctx', 'head'), split_axis=0, concat_axis=0, tiled...  5.11 us
    ppermute x6, waiting for transfers between devices, on_device(): lax.ppermute(token, 'head', [(i, i ^ 1) for i in range(lax.axis_size('hea...  4.74 us
  transfers between devices with their start and end apart: 18, of which 10 were waited for; matrix products, arithmetic and copies ran while one was open for 5% of the time, Pallas kernels for 26%

profile of v6, /device:TPU:0, one launch (start us, length us, event | category | flops | bytes accessed | tf_op | source)
XLA Modules:
  0.0 91.1 jit_solution(2168947427846452855)
XLA Ops:
  0.6 2.2 %halves.3 = (bf16[128,2048]{1,0:T(8,128)(2,1)}, bf16[128,2048]{1,0:T(8,128)(2,1)}) custom-call(s32[1]{0:T(128)} %bitcast.where, bf16[128,2048]{1,0:T(8,128)(2,1)} %one.3, bf16[128,2048]{1,0:T(8,128)(2,1)} %two.3), custom_call_target="tpu_custom_call" | custom-call | bytes 2097152 | tf_op jit(solution)/shard_map/halves/pallas_call | solution.py:63
  2.8 3.0 %collective-permute-start = (bf16[128,2048]{1,0:T(8,128)(2,1)}, bf16[128,2048]{1,0:T(8,128)(2,1)S(1)}, u32[]{:S(2)}, u32[]{:S(2)}) collective-permute-start(bf16[128,2048]{1,0:T(8,128)(2,1)} %get-tuple-element.43), channel_id=1, source_target_pairs={{0,4},{4,0},{8,12},{12,8},{16,20},{20,16},{24,28},{28,24},{1,5},{5... | collective-permute-start | bytes 1572872 | tf_op jit(solution)/shard_map/ppermute | solution.py:36
  5.9 3.5 %collective-permute-start.2 = (bf16[128,2048]{1,0:T(8,128)(2,1)}, bf16[128,2048]{1,0:T(8,128)(2,1)S(1)}, u32[]{:S(2)}, u32[]{:S(2)}) collective-permute-start(bf16[128,2048]{1,0:T(8,128)(2,1)} %get-tuple-element.47.k0.v0), channel_id=1, source_target_pairs={{0,8},{4,12},{8,16},{12,20},{16,24},{20,28},{1,9},{5,13},{9,17},{1... | collective-permute-start | bytes 1572872 | tf_op jit(solution)/shard_map/ppermute | solution.py:31
  9.4 3.0 %pack_memory.1 = bf16[8,2,2,8,2048]{4,3,2,1,0:T(8,128)(2,1)} custom-call(s32[1]{0:T(128)} %bitcast.where, s32[96]{0:T(128)} %bitcast.39, bf16[12,8,2048]{2,1,0:T(8,128)(2,1)} %bitcast.36, bf16[12,8,2048]{2,1,0:T(8,128)(2,1)} %bitcast.37), custom_call_target="tpu_custom_call" | custom-call | bytes 1572864 | tf_op jit(solution)/shard_map/pack_memory/pallas_call | solution.py:111
  12.4 3.8 %all-to-all-start = ((bf16[8,32,2048]{2,1,0:T(8,128)(2,1)}), bf16[8,32,2048]{2,1,0:T(8,128)(2,1)S(1)}, u32[]{:S(2)}, u32[]{:S(2)}) async-start(bf16[8,32,2048]{2,1,0:T(8,128)(2,1)} %bitcast.35), calls=%async_computation | async-start | bytes 2097152 | tf_op jit(solution)/shard_map/all_to_all | solution.py:500
  16.2 2.3 %halves.2 = (bf16[128,2048]{1,0:T(8,128)(2,1)}, bf16[128,2048]{1,0:T(8,128)(2,1)}) custom-call(s32[1]{0:T(128)} %bitcast.where, bf16[128,2048]{1,0:T(8,128)(2,1)} %one.2, bf16[128,2048]{1,0:T(8,128)(2,1)} %two.2), custom_call_target="tpu_custom_call" | custom-call | bytes 2097152 | tf_op jit(solution)/shard_map/halves/pallas_call | solution.py:63
  18.5 1.3 %collective-permute-start.12 = (bf16[128,2048]{1,0:T(8,128)(2,1)}, bf16[128,2048]{1,0:T(8,128)(2,1)}, u32[]{:S(2)}, u32[]{:S(2)}) collective-permute-start(bf16[128,2048]{1,0:T(8,128)(2,1)} %get-tuple-element.42.qo.do_o.q0.do0), channel_id=1, source_target_pairs={{8,0},{12,4},{16,8},{20,12},{24,16},{28,20},{9,1},{13,5},{17,9},{2... | collective-permute-start | bytes 1572872 | tf_op jit(solution)/shard_map/ppermute | solution.py:31
  19.9 0.0 copy-start.7
  19.9 0.6 broadcast.61
  20.4 0.1 copy-done.7
  20.5 0.6 reduce.3
  21.2 0.1 eq.21
  21.2 0.1 pad_add_fusion
  21.3 0.2 convert_reduce_fusion
  21.5 0.0 copy-start.6
  21.5 0.0 collective-permute-done.k1.v1
  21.6 0.5 collective-permute-done.2.k0.v0.k2.v2
  22.0 0.0 collective-permute-start.3
  22.0 0.2 copy-done.6
  22.2 0.1 fusion.5
  22.3 0.9 collective-permute-done.3
  23.2 0.2 collective-permute-start.4
  23.4 1.0 %collective-permute-done.4 = bf16[8,128]{1,0:T(8,128)(2,1)S(1)} collective-permute-done((bf16[8,128]{1,0:T(8,128)(2,1)S(1)}, bf16[8,128]{1,0:T(8,128)(2,1)S(1)}, u32[]{:S(2)}, u32[]{:S(2)}) %collective-permute-start.4) | collective-permute-done | bytes 2080 | tf_op jit(solution)/shard_map/ppermute | solution.py:494
  24.3 0.2 collective-permute-start.5
  24.5 1.0 %collective-permute-done.5 = bf16[8,128]{1,0:T(8,128)(2,1)S(1)} collective-permute-done((bf16[8,128]{1,0:T(8,128)(2,1)S(1)}, bf16[8,128]{1,0:T(8,128)(2,1)S(1)}, u32[]{:S(2)}, u32[]{:S(2)}) %collective-permute-start.5) | collective-permute-done | bytes 2080 | tf_op jit(solution)/shard_map/ppermute | solution.py:494
  25.5 0.2 collective-permute-start.6
  25.7 1.0 %collective-permute-done.6 = bf16[8,128]{1,0:T(8,128)(2,1)S(1)} collective-permute-done((bf16[8,128]{1,0:T(8,128)(2,1)S(1)}, bf16[8,128]{1,0:T(8,128)(2,1)S(1)}, u32[]{:S(2)}, u32[]{:S(2)}) %collective-permute-start.6) | collective-permute-done | bytes 2080 | tf_op jit(solution)/shard_map/ppermute | solution.py:494
  26.6 0.2 collective-permute-start.7
  26.8 2.0 %collective-permute-start.1 = (bf16[128,2048]{1,0:T(8,128)(2,1)}, bf16[128,2048]{1,0:T(8,128)(2,1)S(1)}, u32[]{:S(2)}, u32[]{:S(2)}) collective-permute-start(bf16[128,2048]{1,0:T(8,128)(2,1)} %get-tuple-element.45), channel_id=1, source_target_pairs={{0,4},{4,0},{8,12},{12,8},{16,20},{20,16},{24,28},{28,24},{1,5},{5... | collective-permute-start | bytes 1572872 | tf_op jit(solution)/shard_map/ppermute | solution.py:36
  28.8 0.0 collective-permute-done.7
  28.8 0.1 collective-permute-start.8
  28.9 0.1 copy.24
  29.0 0.9 %collective-permute-done.8._ = bf16[8,128]{1,0:T(8,128)(2,1)S(1)} collective-permute-done((bf16[8,128]{1,0:T(8,128)(2,1)S(1)}, bf16[8,128]{1,0:T(8,128)(2,1)S(1)}, u32[]{:S(2)}, u32[]{:S(2)}) %collective-permute-start.8) | collective-permute-done | bytes 2080 | tf_op jit(solution)/shard_map/ppermute | solution.py:494
  30.0 8.0 %collective-permute-start.9 = (bf16[128,2048]{1,0:T(8,128)(2,1)S(1)}, bf16[128,2048]{1,0:T(8,128)(2,1)}, u32[]{:S(2)}, u32[]{:S(2)}) collective-permute-start(bf16[128,2048]{1,0:T(8,128)(2,1)S(1)} %collective-permute-done.k1.v1), channel_id=1, source_target_pairs={{0,8},{4,12},{8,16},{12,20},{16,24},{20,28},{1,9},{5,13},{9,17},{1... | collective-permute-start | bytes 1572872 | tf_op jit(solution)/shard_map/ppermute | solution.py:31
  38.0 0.1 fusion
  38.0 0.1 broadcast_in_dim.38
  38.1 0.1 reshape.77.mbias
  38.3 6.2 %collective-permute-done.1.qf.do_f.q1.do1 = bf16[128,2048]{1,0:T(8,128)(2,1)S(1)} collective-permute-done((bf16[128,2048]{1,0:T(8,128)(2,1)}, bf16[128,2048]{1,0:T(8,128)(2,1)S(1)}, u32[]{:S(2)}, u32[]{:S(2)}) %collective-permute-start.1) | collective-permute-done | bytes 524320 | tf_op jit(solution)/shard_map/ppermute | solution.py:36
  44.5 1.3 %collective-permute-start.13 = (bf16[128,2048]{1,0:T(8,128)(2,1)S(1)}, bf16[128,2048]{1,0:T(8,128)(2,1)}, u32[]{:S(2)}, u32[]{:S(2)}) collective-permute-start(bf16[128,2048]{1,0:T(8,128)(2,1)S(1)} %collective-permute-done.1.qf.do_f.q1.do1), channel_id=1, source_target_pairs={{8,0},{12,4},{16,8},{20,12},{24,16},{28,20},{9,1},{13,5},{17,9},{2... | collective-permute-start | bytes 1572872 | tf_op jit(solution)/shard_map/ppermute | solution.py:31
  45.8 0.0 all-to-all-done
  45.8 0.0 copy-done.1
  45.8 0.0 copy-start
  45.8 1.0 %copy-done = bf16[128,2048]{1,0:T(8,128)(2,1)S(1)} copy-done((bf16[128,2048]{1,0:T(8,128)(2,1)S(1)}, bf16[128,2048]{1,0:T(8,128)(2,1)}, u32[]{:S(2)}) %copy-start) | copy-done | bytes 524312
  46.8 3.3 %attend_near.1 = (f32[256,1024]{1,0:T(8,128)S(1)}, f32[256,1024]{1,0:T(8,128)S(1)}, f32[256,1024]{1,0:T(8,128)S(1)}) custom-call(bf16[128,2048]{1,0:T(8,128)(2,1)S(1)} %copy-done, bf16[128,2048]{1,0:T(8,128)(2,1)S(1)} %collective-permute-done.1.qf.do_f.q1.do1, bf16[128,2048]{1,0:T(8,128)(2,1)S(1)} %copy-done.1, ...), custom_call_target="tpu_custom_call" | custom-call | flops 402653184 | bytes 3145728 | tf_op jit(solution)/shard_map/attend_near/pallas_call | solution.py:220
  50.2 0.0 collective-permute-done.9.k1.v1.k3.v3
  50.2 3.7 %attend_prev.1 = (bf16[128,1024]{1,0:T(8,128)(2,1)S(1)}, bf16[128,1024]{1,0:T(8,128)(2,1)S(1)}, f32[256,1024]{1,0:T(8,128)S(1)}, f32[256,1024]{1,0:T(8,128)S(1)}, f32[2,8,256]{2,1,0:T(8,128)S(1)}) custom-call(bf16[128,2048]{1,0:T(8,128)(2,1)S(1)} %copy-done, bf16[128,2048]{1,0:T(8,128)(2,1)S(1)} %collective-permute-done.1.qf.do_f.q1.do1, ...), custom_call_target="tpu_custom_call" | custom-call | flops 268435456 | bytes 4194304 | tf_op jit(solution)/shard_map/attend_prev/pallas_call | solution.py:272
  53.9 0.2 collective-permute-start.11
  54.1 1.3 %collective-permute-start.10 = (f32[2,8,256]{2,1,0:T(8,128)S(1)}, f32[2,8,256]{2,1,0:T(8,128)S(1)}, u32[]{:S(2)}, u32[]{:S(2)}) collective-permute-start(f32[2,8,256]{2,1,0:T(8,128)S(1)} %get-tuple-element.59.stat0), channel_id=1, source_target_pairs={{8,0},{12,4},{16,8},{20,12},{24,16},{28,20},{9,1},{13,5},{17,9},{2... | collective-permute-start | bytes 49160 | tf_op jit(solution)/shard_map/ppermute | solution.py:31
  55.4 5.7 %query_gradients.1 = (f32[128,1024]{1,0:T(8,128)}, bf16[128,1024]{1,0:T(8,128)(2,1)S(1)}, f32[8,128]{1,0:T(8,128)S(1)}) custom-call(bf16[128,2048]{1,0:T(8,128)(2,1)S(1)} %copy-done, bf16[128,2048]{1,0:T(8,128)(2,1)S(1)} %collective-permute-done.1.qf.do_f.q1.do1, bf16[128,2048]{1,0:T(8,128)(2,1)S(1)} %copy-done, ...), custom_call_target="tpu_custom_call" | custom-call | flops 1006632960 | bytes 3670016 | tf_op jit(solution)/shard_map/query_gradients/pallas_call | solution.py:345
  61.1 3.1 %collective-permute-done.10.stat1 = f32[2,8,256]{2,1,0:T(8,128)S(1)} collective-permute-done((f32[2,8,256]{2,1,0:T(8,128)S(1)}, f32[2,8,256]{2,1,0:T(8,128)S(1)}, u32[]{:S(2)}, u32[]{:S(2)}) %collective-permute-start.10) | collective-permute-done | bytes 16416 | tf_op jit(solution)/shard_map/ppermute | solution.py:31
  64.2 0.0 collective-permute-done.11
  64.2 1.5 %collective-permute-start.14 = (bf16[128,1024]{1,0:T(8,128)(2,1)S(1)}, bf16[128,1024]{1,0:T(8,128)(2,1)S(1)}, u32[]{:S(2)}, u32[]{:S(2)}) collective-permute-start(bf16[128,1024]{1,0:T(8,128)(2,1)S(1)} %get-tuple-element.72), channel_id=1, source_target_pairs={{0,4},{4,0},{8,12},{12,8},{16,20},{20,16},{24,28},{28,24},{1,5},{5... | collective-permute-start | bytes 786440 | tf_op jit(solution)/shard_map/ppermute | solution.py:36
  65.7 0.0 collective-permute-done.12.q2.do2
  65.7 0.0 collective-permute-done.13.q3.do3
  65.7 5.3 %key_gradients.1 = (f32[128,1024]{1,0:T(8,128)S(1)}, f32[128,1024]{1,0:T(8,128)S(1)}, bf16[2,128,1024]{2,1,0:T(8,128)(2,1)}, f32[32,128]{1,0:T(8,128)}) custom-call(bf16[128,2048]{1,0:T(8,128)(2,1)S(1)} %copy-done, bf16[128,2048]{1,0:T(8,128)(2,1)S(1)} %collective-permute-done.1.qf.do_f.q1.do1, bf16[128,2048]{1,0:T(8,128)(2,1)} %collective-permute-done.12.q2.do2, ...), custom_call_target="tpu_custom_call" | custom-call | flops 1073741824 | bytes 6291456 | tf_op jit(solution)/shard_map/key_gradients/pallas_call | solution.py:419
  71.0 1.0 %collective-permute-done.14.dq_other = bf16[128,1024]{1,0:T(8,128)(2,1)S(1)} collective-permute-done((bf16[128,1024]{1,0:T(8,128)(2,1)S(1)}, bf16[128,1024]{1,0:T(8,128)(2,1)S(1)}, u32[]{:S(2)}, u32[]{:S(2)}) %collective-permute-start.14) | collective-permute-done | bytes 262176 | tf_op jit(solution)/shard_map/ppermute | solution.py:36
  72.0 0.7 copy-done.3
  72.7 0.7 collective-permute-start.15
  73.4 9.2 %all-to-all-start.1 = ((f32[32,1,128]{2,1,0:T(1,128)}), f32[32,1,128]{2,1,0:T(1,128)S(1)}, u32[]{:S(2)}, u32[]{:S(2)}) async-start(f32[32,1,128]{2,1,0:T(1,128)} %bitcast.38), calls=%async_computation.1 | async-start | bytes 32768 | tf_op jit(solution)/shard_map/all_to_all | solution.py:544
  82.6 0.0 copy-start.2
  82.6 2.0 %maximum_select_fusion = bf16[128,2048]{1,0:T(8,128)(2,1)} fusion(bf16[128,1024]{1,0:T(8,128)(2,1)} %copy-done.5, bf16[128,1024]{1,0:T(8,128)(2,1)S(1)} %get-tuple-element.58, pred[]{:T(512)S(6)} %eq.20), kind=kLoop, calls=%fused_computation | loop fusion | flops 2359296 | bytes 1048577 | tf_op jit(solution)/shard_map/jit(_where)/select_n | solution.py:549
  84.7 5.1 %all-to-all-done.1 = f32[32,1,128]{2,1,0:T(1,128)S(1)} async-done(((f32[32,1,128]{2,1,0:T(1,128)}), f32[32,1,128]{2,1,0:T(1,128)S(1)}, u32[]{:S(2)}, u32[]{:S(2)}) %all-to-all-start.1) | async-done | bytes 16416 | tf_op jit(solution)/shard_map/all_to_all | solution.py:544
  89.8 0.0 collective-permute-done.15.other
  89.8 1.4 %scaled.1 = (bf16[128,2048]{1,0:T(8,128)(2,1)}, bf16[128,2048]{1,0:T(8,128)(2,1)}, bf16[128,2048]{1,0:T(8,128)(2,1)}) custom-call(s32[1]{0:T(128)} %bitcast.14.side_ref, f32[32,128]{1,0:T(8,128)S(1)} %bitcast.34, f32[128,1024]{1,0:T(8,128)S(1)} %copy-done.2, bf16[128,1024]{1,0:T(8,128)(2,1)S(1)} %copy-done.4, f32[128,1024]{1,0:T(8,128)S(1)} %get-tuple-element.74.dk, ...), custom_call_target="tpu_custom_call" | custom-call | flops 786432 | bytes 2621440 | tf_op jit(solution)/shard_map/scaled/pallas_call | solution.py:463
  (15 shorter events, 0.1 us)
Async XLA Ops:
  2.8 18.7 %collective-permute-start = (bf16[128,2048]{1,0:T(8,128)(2,1)}, bf16[128,2048]{1,0:T(8,128)(2,1)S(1)}, u32[]{:S(2)}, u32[]{:S(2)}) collective-permute-start(bf16[128,2048]{1,0:T(8,128)(2,1)} %get-tuple-element.43), channel_id=1, source_target_pairs={{0,4},{4,0},{8,12},{12,8},{16,20},{20,16},{24,28},{28,24},{1,5},{5... | collective-permute-start | bytes 1572872 | tf_op jit(solution)/shard_map/ppermute | solution.py:36
  5.9 16.1 %collective-permute-start.2 = (bf16[128,2048]{1,0:T(8,128)(2,1)}, bf16[128,2048]{1,0:T(8,128)(2,1)S(1)}, u32[]{:S(2)}, u32[]{:S(2)}) collective-permute-start(bf16[128,2048]{1,0:T(8,128)(2,1)} %get-tuple-element.47.k0.v0), channel_id=1, source_target_pairs={{0,8},{4,12},{8,16},{12,20},{16,24},{20,28},{1,9},{5,13},{9,17},{1... | collective-permute-start | bytes 1572872 | tf_op jit(solution)/shard_map/ppermute | solution.py:31
  12.4 33.4 %all-to-all-start = ((bf16[8,32,2048]{2,1,0:T(8,128)(2,1)}), bf16[8,32,2048]{2,1,0:T(8,128)(2,1)S(1)}, u32[]{:S(2)}, u32[]{:S(2)}) async-start(bf16[8,32,2048]{2,1,0:T(8,128)(2,1)} %bitcast.35), calls=%async_computation | async-start | bytes 2097152 | tf_op jit(solution)/shard_map/all_to_all | solution.py:500
  16.2 29.5 %copy-start.1 = (bf16[128,2048]{1,0:T(8,128)(2,1)S(1)}, bf16[128,2048]{1,0:T(8,128)(2,1)}, u32[]{:S(2)}) copy-start(bf16[128,2048]{1,0:T(8,128)(2,1)} %get-tuple-element.47.k0.v0) | copy-start | bytes 1572868
  18.5 47.1 %collective-permute-start.12 = (bf16[128,2048]{1,0:T(8,128)(2,1)}, bf16[128,2048]{1,0:T(8,128)(2,1)}, u32[]{:S(2)}, u32[]{:S(2)}) collective-permute-start(bf16[128,2048]{1,0:T(8,128)(2,1)} %get-tuple-element.42.qo.do_o.q0.do0), channel_id=1, source_target_pairs={{8,0},{12,4},{16,8},{20,12},{24,16},{28,20},{9,1},{13,5},{17,9},{2... | collective-permute-start | bytes 1572872 | tf_op jit(solution)/shard_map/ppermute | solution.py:31
  19.9 0.7 copy-start.7
  21.5 0.7 copy-start.6
  22.0 1.2 %collective-permute-start.3 = (bf16[8,128]{1,0:T(8,128)(2,1)S(1)}, bf16[8,128]{1,0:T(8,128)(2,1)S(1)}, u32[]{:S(2)}, u32[]{:S(2)}) collective-permute-start(bf16[8,128]{1,0:T(8,128)(2,1)S(1)} %slice_add_fusion), channel_id=1, source_target_pairs={{0,1},{1,0},{2,3},{3,2},{4,5},{5,4},{6,7},{7,6},{8,9},{9,8},{10,11... | collective-permute-start | bytes 6152 | tf_op jit(solution)/shard_map/ppermute | solution.py:494
  23.2 1.2 %collective-permute-start.4 = (bf16[8,128]{1,0:T(8,128)(2,1)S(1)}, bf16[8,128]{1,0:T(8,128)(2,1)S(1)}, u32[]{:S(2)}, u32[]{:S(2)}) collective-permute-start(bf16[8,128]{1,0:T(8,128)(2,1)S(1)} %collective-permute-done.3), channel_id=1, source_target_pairs={{0,1},{1,0},{2,3},{3,2},{4,5},{5,4},{6,7},{7,6},{8,9},{9,8},{10,11... | collective-permute-start | bytes 6152 | tf_op jit(solution)/shard_map/ppermute | solution.py:494
  24.3 1.2 %collective-permute-start.5 = (bf16[8,128]{1,0:T(8,128)(2,1)S(1)}, bf16[8,128]{1,0:T(8,128)(2,1)S(1)}, u32[]{:S(2)}, u32[]{:S(2)}) collective-permute-start(bf16[8,128]{1,0:T(8,128)(2,1)S(1)} %collective-permute-done.4), channel_id=1, source_target_pairs={{0,1},{1,0},{2,3},{3,2},{4,5},{5,4},{6,7},{7,6},{8,9},{9,8},{10,11... | collective-permute-start | bytes 6152 | tf_op jit(solution)/shard_map/ppermute | solution.py:494
  25.5 1.2 %collective-permute-start.6 = (bf16[8,128]{1,0:T(8,128)(2,1)S(1)}, bf16[8,128]{1,0:T(8,128)(2,1)S(1)}, u32[]{:S(2)}, u32[]{:S(2)}) collective-permute-start(bf16[8,128]{1,0:T(8,128)(2,1)S(1)} %collective-permute-done.5), channel_id=1, source_target_pairs={{0,1},{1,0},{2,3},{3,2},{4,5},{5,4},{6,7},{7,6},{8,9},{9,8},{10,11... | collective-permute-start | bytes 6152 | tf_op jit(solution)/shard_map/ppermute | solution.py:494
  26.6 2.2 %collective-permute-start.7 = (bf16[8,128]{1,0:T(8,128)(2,1)S(1)}, bf16[8,128]{1,0:T(8,128)(2,1)S(1)}, u32[]{:S(2)}, u32[]{:S(2)}) collective-permute-start(bf16[8,128]{1,0:T(8,128)(2,1)S(1)} %collective-permute-done.6), channel_id=1, source_target_pairs={{0,1},{1,0},{2,3},{3,2},{4,5},{5,4},{6,7},{7,6},{8,9},{9,8},{10,11... | collective-permute-start | bytes 6152 | tf_op jit(solution)/shard_map/ppermute | solution.py:494
  26.8 17.6 %collective-permute-start.1 = (bf16[128,2048]{1,0:T(8,128)(2,1)}, bf16[128,2048]{1,0:T(8,128)(2,1)S(1)}, u32[]{:S(2)}, u32[]{:S(2)}) collective-permute-start(bf16[128,2048]{1,0:T(8,128)(2,1)} %get-tuple-element.45), channel_id=1, source_target_pairs={{0,4},{4,0},{8,12},{12,8},{16,20},{20,16},{24,28},{28,24},{1,5},{5... | collective-permute-start | bytes 1572872 | tf_op jit(solution)/shard_map/ppermute | solution.py:36
  28.8 1.2 %collective-permute-start.8 = (bf16[8,128]{1,0:T(8,128)(2,1)S(1)}, bf16[8,128]{1,0:T(8,128)(2,1)S(1)}, u32[]{:S(2)}, u32[]{:S(2)}) collective-permute-start(bf16[8,128]{1,0:T(8,128)(2,1)S(1)} %collective-permute-done.7), channel_id=1, source_target_pairs={{0,1},{1,0},{2,3},{3,2},{4,5},{5,4},{6,7},{7,6},{8,9},{9,8},{10,11... | collective-permute-start | bytes 6152 | tf_op jit(solution)/shard_map/ppermute | solution.py:494
  30.0 20.2 %collective-permute-start.9 = (bf16[128,2048]{1,0:T(8,128)(2,1)S(1)}, bf16[128,2048]{1,0:T(8,128)(2,1)}, u32[]{:S(2)}, u32[]{:S(2)}) collective-permute-start(bf16[128,2048]{1,0:T(8,128)(2,1)S(1)} %collective-permute-done.k1.v1), channel_id=1, source_target_pairs={{0,8},{4,12},{8,16},{12,20},{16,24},{20,28},{1,9},{5,13},{9,17},{1... | collective-permute-start | bytes 1572872 | tf_op jit(solution)/shard_map/ppermute | solution.py:31
  44.5 21.2 %collective-permute-start.13 = (bf16[128,2048]{1,0:T(8,128)(2,1)S(1)}, bf16[128,2048]{1,0:T(8,128)(2,1)}, u32[]{:S(2)}, u32[]{:S(2)}) collective-permute-start(bf16[128,2048]{1,0:T(8,128)(2,1)S(1)} %collective-permute-done.1.qf.do_f.q1.do1), channel_id=1, source_target_pairs={{8,0},{12,4},{16,8},{20,12},{24,16},{28,20},{9,1},{13,5},{17,9},{2... | collective-permute-start | bytes 1572872 | tf_op jit(solution)/shard_map/ppermute | solution.py:31
  45.8 1.0 %copy-start = (bf16[128,2048]{1,0:T(8,128)(2,1)S(1)}, bf16[128,2048]{1,0:T(8,128)(2,1)}, u32[]{:S(2)}) copy-start(bf16[128,2048]{1,0:T(8,128)(2,1)} %get-tuple-element.42.qo.do_o.q0.do0) | copy-start | bytes 1572868
  53.9 10.3 %collective-permute-start.11 = (bf16[128,1024]{1,0:T(8,128)(2,1)S(1)}, bf16[128,1024]{1,0:T(8,128)(2,1)S(1)}, u32[]{:S(2)}, u32[]{:S(2)}) collective-permute-start(bf16[128,1024]{1,0:T(8,128)(2,1)S(1)} %get-tuple-element.64), channel_id=1, source_target_pairs={{0,4},{4,0},{8,12},{12,8},{16,20},{20,16},{24,28},{28,24},{1,5},{5... | collective-permute-start | bytes 786440 | tf_op jit(solution)/shard_map/ppermute | solution.py:36
  54.1 10.1 %collective-permute-start.10 = (f32[2,8,256]{2,1,0:T(8,128)S(1)}, f32[2,8,256]{2,1,0:T(8,128)S(1)}, u32[]{:S(2)}, u32[]{:S(2)}) collective-permute-start(f32[2,8,256]{2,1,0:T(8,128)S(1)} %get-tuple-element.59.stat0), channel_id=1, source_target_pairs={{8,0},{12,4},{16,8},{20,12},{24,16},{28,20},{9,1},{13,5},{17,9},{2... | collective-permute-start | bytes 49160 | tf_op jit(solution)/shard_map/ppermute | solution.py:31
  64.2 6.8 %copy-start.5 = (bf16[128,1024]{1,0:T(8,128)(2,1)}, bf16[128,1024]{1,0:T(8,128)(2,1)S(1)}, u32[]{:S(2)}) copy-start(bf16[128,1024]{1,0:T(8,128)(2,1)S(1)} %collective-permute-done.11) | copy-start | bytes 786436
  64.2 7.8 %collective-permute-start.14 = (bf16[128,1024]{1,0:T(8,128)(2,1)S(1)}, bf16[128,1024]{1,0:T(8,128)(2,1)S(1)}, u32[]{:S(2)}, u32[]{:S(2)}) collective-permute-start(bf16[128,1024]{1,0:T(8,128)(2,1)S(1)} %get-tuple-element.72), channel_id=1, source_target_pairs={{0,4},{4,0},{8,12},{12,8},{16,20},{20,16},{24,28},{28,24},{1,5},{5... | collective-permute-start | bytes 786440 | tf_op jit(solution)/shard_map/ppermute | solution.py:36
  72.0 0.7 copy-start.3
  72.7 17.1 %collective-permute-start.15 = (bf16[2,128,1024]{2,1,0:T(8,128)(2,1)}, bf16[2,128,1024]{2,1,0:T(8,128)(2,1)S(1)}, u32[]{:S(2)}, u32[]{:S(2)}) collective-permute-start(bf16[2,128,1024]{2,1,0:T(8,128)(2,1)} %get-tuple-element.76), channel_id=1, source_target_pairs={{0,4},{4,0},{8,12},{12,8},{16,20},{20,16},{24,28},{28,24},{1,5},{5... | collective-permute-start | bytes 1572872 | tf_op jit(solution)/shard_map/ppermute | solution.py:36
  73.4 16.4 %all-to-all-start.1 = ((f32[32,1,128]{2,1,0:T(1,128)}), f32[32,1,128]{2,1,0:T(1,128)S(1)}, u32[]{:S(2)}, u32[]{:S(2)}) async-start(f32[32,1,128]{2,1,0:T(1,128)} %bitcast.38), calls=%async_computation.1 | async-start | bytes 32768 | tf_op jit(solution)/shard_map/all_to_all | solution.py:544
  82.6 7.2 %copy-start.2 = (f32[128,1024]{1,0:T(8,128)S(1)}, f32[128,1024]{1,0:T(8,128)}, u32[]{:S(2)}) copy-start(f32[128,1024]{1,0:T(8,128)} %get-tuple-element.70.dq) | copy-start | bytes 1572868
  82.6 7.1 %copy-start.4 = (bf16[128,1024]{1,0:T(8,128)(2,1)S(1)}, bf16[128,1024]{1,0:T(8,128)(2,1)}, u32[]{:S(2)}) copy-start(bf16[128,1024]{1,0:T(8,128)(2,1)} %copy-done.3) | copy-start | bytes 786436
